TPU v7x, 32 devices: a whole 2x2x4 slice. The times are simulated.
32 devices in a mesh: va: 8 (over y, x, core), vb: 4 (over z).
Axes of the slice: x: 2, y: 2, z: 4, core: 2. Of those that a mesh axis runs over, the one named last changes fastest.
Arguments:
- clique_a: float32 [16, 8, 2, 16, 32768], P('va', 'vb'), may hold values from 0.2 to 5
- message_in: float32 [16, 2, 32768], P('va'), may hold values from 0.2 to 5
- clique_b: float32 [32, 8, 16, 16, 8, 256], P(None, None, None, 'va', 'vb'), may hold values from 0.2 to 5
- old_separator: float32 [8, 16, 16, 8, 256], P(None, None, 'va', 'vb'), may hold values from 0.25 to 4
Outputs:
- absorbed: float32 [16, 8, 2, 16, 32768], P('va', 'vb')
- updated_b: float32 [32, 8, 16, 16, 8, 256], P(None, None, None, 'va', 'vb')
- onward: float32 [32, 16, 16, 256], P('vb', None, 'va')
All inputs are finite; a program needn't handle non-finite values.
Results may differ from a plain program's by a relative error of at most 0.00002.
Values sent between devices are 32-bit elements; how exact they have to be, the bound alone decides.
No kernel may reach another device: no remote copies, remote signals or barrier semaphores. Data moves between devices by JAX's collectives and lax.ppermute only.
A program may use at most 192 MiB of HBM per device.

v0:
```python
import jax
import jax.numpy as jnp
from jax import lax
from jax.sharding import PartitionSpec as P

H = 16
K = 2
P_SIZE = 8
R1 = 16
R2 = 8
R3 = 256


def body(clique_a, message_in, clique_b, old_separator):
    p_local = clique_a.shape[1]
    q_total = clique_a.shape[3]
    r_total = clique_a.shape[4]
    absorbed = clique_a * message_in[:, None, :, None, :]
    column_width = r_total // R1
    summed = jnp.sum(absorbed, axis=(0, 2)) * (1.0 / (H * K))
    summed = summed.reshape(
        p_local, q_total, lax.axis_size("va") * (R1 // lax.axis_size("va")), column_width
    )
    shares = lax.psum_scatter(
        jnp.transpose(summed, (2, 0, 1, 3)), "va", scatter_dimension=0, tiled=True
    )
    shares = shares.reshape(shares.shape[0], p_local, q_total, R2, R3)
    moved = lax.all_to_all(shares, "vb", split_axis=3, concat_axis=1, tiled=True)
    separator = jnp.transpose(moved, (1, 2, 0, 3, 4))
    scaling = separator / old_separator
    updated_b = clique_b * scaling[None]
    partial_value = jnp.sum(updated_b, axis=(1, 4)) * (1.0 / (P_SIZE * R2))
    onward = lax.psum_scatter(partial_value, "vb", scatter_dimension=0, tiled=True)
    return (absorbed, updated_b, onward)


def solution(mesh):
    return jax.shard_map(
        body,
        mesh=mesh,
        in_specs=(
            P("va", "vb", None, None, None),
            P("va", None, None),
            P(None, None, None, "va", "vb", None),
            P(None, None, "va", "vb", None),
        ),
        out_specs=(
            P("va", "vb", None, None, None),
            P(None, None, None, "va", "vb", None),
            P("vb", None, "va", None),
        ),
        check_vma=False,
    )
```

profile of v0, /device:TPU:0, one launch (start us, length us, event | category | flops | bytes accessed | tf_op | source)
XLA Modules:
  0.0 156.1 jit_solution(7697594367874494386)
XLA Ops:
  7.2 0.0 reduce-scatter.3.cloned.1.call-start
  7.2 12.5 %fusion.1 = (f32[2,16,32768]{2,1,0:T(8,128)S(1)}, f32[2,2,2,16,32768]{4,3,2,1,0:T(8,128)}) fusion(f32[2,2,2,16,32768]{4,3,2,1,0:T(8,128)} %param.4, f32[2,2,32768]{2,1,0:T(2,128)} %param.5), kind=kLoop, calls=%fused_computation.8 | loop fusion | flops 7340032 | bytes 38273024 | tf_op jit(solution)/shard_map/reduce_sum | solution.py:20
  19.7 0.3 broadcast_multiply_fusion.2
  19.9 0.0 copy-start
  19.9 2.4 %copy.41 = f32[4,8,16,2048]{3,2,1,0:T(8,128)S(1)} copy(f32[4,8,16,2048]{3,1,2,0:T(8,128)S(1)} %bitcast.18) | data formatting | bytes 8388608
  22.4 0.5 bitcast_bitcast_fusion
  22.9 4.4 %copy.31 = f32[16,2,16,2048]{3,2,1,0:T(8,128)} copy(f32[16,2,16,2048]{3,0,2,1:T(8,128)S(1)} %bitcast_bitcast_fusion) | data formatting | bytes 8388608 | tf_op jit(solution)/shard_map/transpose | solution.py:25
  27.3 0.0 reduce-scatter.3.cloned.1.call-update
  27.4 0.0 reduce-scatter.5.cloned.1.call-start
  27.4 54.1 %reduce-scatter.3.cloned.1.call-done = f32[2,2,16,2048]{3,2,1,0:T(8,128)} async-done(((f32[16,2,16,2048]{3,2,1,0:T(8,128)}), f32[2,2,16,2048]{3,2,1,0:T(8,128)}) %reduce-scatter.3.cloned.1.call-update) | async-done | bytes 524304 | tf_op jit(solution)/shard_map/reduce_scatter | solution.py:24
  81.5 1.1 copy.45
  82.6 18.9 %all_to_all.18 = f32[2,2,16,8,256]{4,2,1,0,3:T(8,128)S(1)} all-to-all(f32[2,2,16,8,256]{4,2,1,0,3:T(8,128)S(1)} %bitcast.21), channel_id=1, replica_groups=mesh['va'=8,'vb'=4] {'vb'}, dimensions={3} | all-to-all | bytes 1048576 | tf_op jit(solution)/shard_map/all_to_all | solution.py:28
  101.6 0.0 copy-done
  101.6 0.1 copy_divide_fusion
  101.7 0.4 copy.36
  102.1 18.7 %fusion = (f32[32,16,2,256]{3,2,1,0:T(2,128)S(1)}, f32[32,8,16,2,2,256]{5,4,3,2,1,0:T(2,128)}) fusion(f32[32,8,16,2,2,256]{5,4,3,2,1,0:T(2,128)} %param.6, f32[8,16,2,2,256]{4,3,2,1,0:T(2,128)S(1)} %copy.36), kind=kLoop, calls=%fused_computation.7 | loop fusion | flops 8126464 | bytes 35127296 | tf_op jit(solution)/shard_map/reduce_sum | solution.py:32
  120.9 1.1 copy_multiply_fusion
  122.0 0.0 reduce-scatter.5.cloned.1.call-update
  122.0 25.4 %reduce-scatter.5.cloned.1.call-done = f32[8,16,2,256]{3,1,2,0:T(8,128)} async-done(((f32[32,16,2,256]{3,1,2,0:T(8,128)}), f32[8,16,2,256]{3,1,2,0:T(8,128)}) %reduce-scatter.5.cloned.1.call-update) | async-done | bytes 262160 | tf_op jit(solution)/shard_map/reduce_scatter | solution.py:33
  147.5 1.9 %copy.38 = f32[8,16,2,256]{3,2,1,0:T(2,128)} copy(f32[8,16,2,256]{3,1,2,0:T(8,128)} %reduce-scatter.5.cloned.1.call-done) | data formatting | bytes 524288
  (1 shorter events, 0.0 us)
Async XLA Ops:
  7.2 74.4 %reduce-scatter.3.cloned.1.call-start = ((), (), s32[]{:S(2)}) async-start(), calls=%async_computation.3 | async-start | bytes 4718592 | tf_op jit(solution)/shard_map/reduce_scatter | solution.py:24
  19.9 81.6 %copy-start = (f32[8,16,2,2,256]{4,3,2,1,0:T(2,128)S(1)}, f32[8,16,2,2,256]{4,3,2,1,0:T(2,128)}, u32[]{:S(2)}) copy-start(f32[8,16,2,2,256]{4,3,2,1,0:T(2,128)} %param.7) | copy-start | bytes 1572868
  27.4 120.1 %reduce-scatter.5.cloned.1.call-start = ((), (), s32[]{:S(2)}) async-start(), calls=%async_computation.4 | async-start | bytes 1310720 | tf_op jit(solution)/shard_map/reduce_scatter | solution.py:33
Sparse Core Ops, SparseCore 0:
  27.5 53.9 reduce-scatter.2
  122.2 25.2 reduce-scatter.4
where the time goes:
time: 156 us
  waiting for transfers between devices  79.6 us (51%)
  other arithmetic  32.7 us (21%)
  blocking collectives  18.9 us (12%)
  between operations  14.1 us (9%)
  local copies, waits for them, and re-layouts  10.8 us (7%)
    reduce_scatter x1, waiting for transfers between devices, body(): lax.psum_scatter(jnp.transpose(summed, (2, 0, 1, 3)), 'va', scatter_dimen...  54.1 us
    reduce_scatter x1, waiting for transfers between devices, body(): lax.psum_scatter(partial_value, 'vb', scatter_dimension=0, tiled=True)  25.4 us
    all_to_all x1, blocking collectives, body(): lax.all_to_all(shares, 'vb', split_axis=3, concat_axis=1, tiled=True)  18.9 us
    reduce_sum x1, other arithmetic, body(): partial_value = jnp.sum(updated_b, axis=(1, 4)) * (1.0 / (P_SIZE * R2))  18.7 us
    reduce_sum x1, other arithmetic, body(): summed = jnp.sum(absorbed, axis=(0, 2)) * (1.0 / (H * K))  12.5 us
    transpose x2, local copies, waits for them, and re-layouts, body(): jnp.transpose(summed, (2, 0, 1, 3))  4.93 us
    unnamed x4, local copies, waits for them, and re-layouts  4.29 us
  transfers between devices with their start and end apart: 2, of which 2 were waited for; matrix products, arithmetic and copies ran while one was open for 0% of the time, Pallas kernels for 0%

commit v1 on v0

--- a/solution.py
+++ b/solution.py
@@ -1,6 +1,10 @@
+import functools
+
 import jax
 import jax.numpy as jnp
 from jax import lax
+from jax.experimental import pallas as pl
+from jax.experimental.pallas import tpu as pltpu
 from jax.sharding import PartitionSpec as P
 
 H = 16
@@ -9,9 +13,11 @@
 R1 = 16
 R2 = 8
 R3 = 256
-
-
-def body(clique_a, message_in, clique_b, old_separator):
+LANES = 128
+QT = 8
+
+
+def generic_body(clique_a, message_in, clique_b, old_separator):
     p_local = clique_a.shape[1]
     q_total = clique_a.shape[3]
     r_total = clique_a.shape[4]
@@ -34,9 +40,227 @@
     return (absorbed, updated_b, onward)
 
 
+def swap(x, axis, mask):
+    n = lax.axis_size(axis)
+    return lax.ppermute(x, axis, [(i, i ^ mask) for i in range(n)])
+
+
+def absorb_kernel(tab_ref, a_ref, m_ref, *rest):
+    o_ref, s_ref = rest[-2:]
+    nh, npl, nk = a_ref.shape[:3]
+    nm, nr1, width = s_ref.shape[2], s_ref.shape[3], s_ref.shape[5]
+    for r1 in range(nr1):
+        for m in range(nm):
+            block = tab_ref[1 + m]
+            off = pl.multiple_of(r1 * (nm * width) + block * width, width)
+            lanes = pl.ds(off, width)
+            msg = [
+                [jnp.broadcast_to(m_ref[h, pl.ds(k, 1), lanes], (QT, width)) for k in range(nk)]
+                for h in range(nh)
+            ]
+            for p in range(npl):
+                total = None
+                for h in range(nh):
+                    for k in range(nk):
+                        value = a_ref[h, p, k, :, lanes] * msg[h][k]
+                        o_ref[h, p, k, :, lanes] = value
+                        total = value if total is None else total + value
+                s_ref[0, p, m, r1] = total
+
+
+def absorb(tab, clique_a, message, absorbed, chunk, part, n_va, n_vb):
+    nh, npl, nk, nq, nr = clique_a.shape
+    block = nr // n_va
+    nr1 = R1 // n_va
+    width = block // nr1 // n_vb
+    steps = n_va // 2
+    a_spec = pl.BlockSpec(
+        (nh, npl, nk, QT, block), lambda g, t: (0, 0, 0, chunk, t[0] ^ (2 * g + part))
+    )
+    in_specs = [
+        a_spec,
+        pl.BlockSpec((nh, nk, block), lambda g, t: (0, 0, t[0] ^ (2 * g + part))),
+    ]
+    args = [tab, clique_a, message]
+    aliases = {}
+    if absorbed is not None:
+        in_specs.append(pl.BlockSpec(memory_space=pl.ANY))
+        args.append(absorbed)
+        aliases = {3: 0}
+    piece = (npl, n_vb, nr1, QT, width)
+    n_a = nh * npl * nk * QT * block * steps
+    return pl.pallas_call(
+        absorb_kernel,
+        grid_spec=pltpu.PrefetchScalarGridSpec(
+            num_scalar_prefetch=1,
+            grid=(steps,),
+            in_specs=in_specs,
+            out_specs=[a_spec, pl.BlockSpec((1,) + piece, lambda g, t: (g, 0, 0, 0, 0, 0))],
+        ),
+        out_shape=[
+            jax.ShapeDtypeStruct(clique_a.shape, clique_a.dtype),
+            jax.ShapeDtypeStruct((steps,) + piece, clique_a.dtype),
+        ],
+        input_output_aliases=aliases,
+        cost_estimate=pl.CostEstimate(flops=2 * n_a, bytes_accessed=9 * n_a, transcendentals=0),
+        name="absorb",
+    )(*args)
+
+
+def update_kernel(n_pieces, tab_ref, b_ref, old_ref, *rest):
+    seps = rest[:n_pieces]
+    u_ref, on_ref, scale, col = rest[-4:]
+    step = pl.program_id(0)
+    npl, nr1, _, width = seps[0].shape
+    nhi = R3 // LANES
+    nr2 = width // R3
+    tile = nr1 * nhi * nr2
+
+    @pl.when(step == 0)
+    def _():
+        for m in range(n_pieces):
+            for p in range(npl):
+                row = tab_ref[1 + m] * npl + p
+                for r1 in range(nr1):
+                    for r2 in range(nr2):
+                        for hi in range(nhi):
+                            at = (r2 * nhi + hi) * LANES
+                            scale[row, pl.ds((r1 * nhi + hi) * nr2 + r2, QT, stride=tile), :] = (
+                                seps[m][p, r1, :, at : at + LANES]
+                            )
+        scale[...] = scale[...] * (1.0 / (H * K)) / old_ref[...]
+
+    ne, npt = b_ref.shape[:2]
+    rows = b_ref.shape[2]
+    for e in range(ne):
+        total = None
+        for p in range(npt):
+            value = b_ref[e, p] * scale[p]
+            u_ref[e, p] = value
+            total = value if total is None else total + value
+        col[e] = total * (1.0 / (P_SIZE * R2))
+        for hi in range(nhi):
+            for r1 in range(nr1):
+                acc = None
+                for r2 in range(nr2):
+                    piece = col[e, pl.ds((r1 * nhi + hi) * nr2 + r2, QT, stride=tile), :]
+                    acc = piece if acc is None else acc + piece
+                on_ref[0, e, pl.ds(hi * nr1 + r1, QT, stride=nhi * nr1), :] = acc
+
+
+def update(tab, clique_b, old, seps, updated, chunk, order, n_vb):
+    ne, npt, rows, _ = clique_b.shape
+    crow = QT * (rows // (clique_b.shape[2] // 8))
+    rows_c = 8 * QT
+    orow = rows_c // 2
+    be = ne // n_vb // 2
+    npc = len(order)
+
+    def at(g, t):
+        return t[1 + n_vb + g]
+
+    b_spec = pl.BlockSpec((be, npt, rows_c, LANES), lambda g, t: (at(g, t), 0, chunk, 0))
+    in_specs = [
+        b_spec,
+        pl.BlockSpec((npt, rows_c, LANES), lambda g, t: (0, chunk, 0)),
+    ] + [pl.BlockSpec(s.shape, lambda g, t: (0, 0, 0, 0)) for s in seps]
+    z = tab[1]
+    tab = jnp.concatenate([tab[: 1 + n_vb], jnp.stack([(z ^ m) * 2 + half for m, half in order])])
+    args = [tab, clique_b, old, *seps]
+    aliases = {}
+    if updated is not None:
+        in_specs.append(pl.BlockSpec(memory_space=pl.ANY))
+        args.append(updated)
+        aliases = {len(args) - 1: 0}
+    n_b = be * npt * rows_c * LANES * npc
+    return pl.pallas_call(
+        functools.partial(update_kernel, len(seps)),
+        grid_spec=pltpu.PrefetchScalarGridSpec(
+            num_scalar_prefetch=1,
+            grid=(npc,),
+            in_specs=in_specs,
+            out_specs=[
+                b_spec,
+                pl.BlockSpec((1, be, orow, LANES), lambda g, t: (g, 0, 0, 0)),
+            ],
+            scratch_shapes=[
+                pltpu.VMEM((npt, rows_c, LANES), jnp.float32),
+                pltpu.VMEM((be, rows_c, LANES), jnp.float32),
+            ],
+        ),
+        out_shape=[
+            jax.ShapeDtypeStruct(clique_b.shape, clique_b.dtype),
+            jax.ShapeDtypeStruct((npc, be, orow, LANES), clique_b.dtype),
+        ],
+        input_output_aliases=aliases,
+        cost_estimate=pl.CostEstimate(flops=2 * n_b, bytes_accessed=8 * n_b, transcendentals=0),
+        name="update",
+    )(*args)
+
+
+def body(clique_a, message_in, clique_b, old_separator):
+    n_va, n_vb = lax.axis_size("va"), lax.axis_size("vb")
+    npl, nq = clique_a.shape[1], clique_a.shape[3]
+    ne, npt, _, nr1, nr2, _ = clique_b.shape
+    nhi = R3 // LANES
+    n_chunks = nq // QT
+
+    me, z = lax.axis_index("va"), lax.axis_index("vb")
+    tab = jnp.stack([me] + [z ^ m for m in range(n_vb)]).astype(jnp.int32)
+
+    def rows_view(x):
+        lead = x.shape[:-3]
+        x = x.reshape(lead + (nr1, nr2, nhi, LANES))
+        n = len(lead)
+        x = jnp.swapaxes(x, n + 1, n + 2)
+        return x.reshape(lead[:-1] + (lead[-1] * nr1 * nhi * nr2, LANES))
+
+    b_rows, old_rows = rows_view(clique_b), rows_view(old_separator)
+
+    absorbed, seps = None, []
+    for c in range(n_chunks):
+        absorbed, send = absorb(tab, clique_a, message_in, absorbed, c, 1, n_va, n_vb)
+        got = swap(send, "va", 1)
+        absorbed, keep = absorb(tab, clique_a, message_in, absorbed, c, 0, n_va, n_vb)
+        keep = keep.reshape((2, 2) + keep.shape[1:])
+        got = got.reshape(keep.shape)
+        x0 = keep[:, 1, 0] + got[:, 1, 0]
+        y1 = keep[1, :, 1] + got[1, :, 1]
+        x0, y1 = swap(x0, "va", 2), swap(y1, "va", 4)
+        y0 = keep[1, 0, 0] + got[1, 0, 0] + x0[1]
+        x1 = keep[0, 1, 1] + got[0, 1, 1] + y1[1]
+        k0 = keep[0, 0, 0] + got[0, 0, 0] + x0[0]
+        k1 = keep[0, 0, 1] + got[0, 0, 1] + y1[0]
+        y0, x1 = swap(y0, "va", 4), swap(x1, "va", 2)
+        pieces = [jnp.stack([k0[m] + y0[m], k1[m] + x1[m]]) for m in range(n_vb)]
+        seps.append([pieces[0]] + [swap(pieces[m], "vb", m) for m in range(1, n_vb)])
+
+    updated, onward = None, []
+    for c in range(n_chunks):
+        send_order = [(1, 0), (2, 0), (3, 1), (2, 1)]
+        keep_order = [(0, 0), (3, 0), (0, 1), (1, 1)]
+        updated, send = update(tab, b_rows, old_rows, seps[c], updated, c, send_order, n_vb)
+        g0, g1 = swap(send[:2], "vb", 1), swap(send[2:], "vb", 3)
+        updated, keep = update(tab, b_rows, old_rows, seps[c], updated, c, keep_order, n_vb)
+        s0, s1 = keep[1] + g0[1], keep[3] + g1[1]
+        k0, k1 = keep[0] + g0[0], keep[2] + g1[0]
+        s0, s1 = swap(s0, "vb", 3), swap(s1, "vb", 1)
+        onward.append(jnp.concatenate([k0 + s0, k1 + s1], axis=0))
+
+    e_out = ne // n_vb
+    onward = jnp.concatenate(
+        [o.reshape(e_out, QT, nhi, nr1, LANES) for o in onward], axis=1
+    )
+    onward = jnp.swapaxes(onward, 2, 3).reshape(e_out, nq, nr1, R3)
+    updated = updated.reshape(ne, npt, nq, nr1, nhi, nr2, LANES)
+    updated = jnp.swapaxes(updated, 4, 5).reshape(clique_b.shape)
+    return (absorbed, updated, onward)
+
+
 def solution(mesh):
+    small = mesh.shape["va"] == 8 and mesh.shape["vb"] == 4
     return jax.shard_map(
-        body,
+        body if small else generic_body,
         mesh=mesh,
         in_specs=(
             P("va", "vb", None, None, None),

time: 156 us -> 108 us (0.69)
  waiting for transfers between devices: 79.6 us -> 13.1 us
  Pallas kernels: 0 us -> 46.3 us
  starting transfers between devices: 0.08 us -> 31.8 us
  other arithmetic: 32.7 us -> 10.9 us
  blocking collectives: 18.9 us -> 0 us
  between operations: 14.1 us -> 0.85 us
  local copies, waits for them, and re-layouts: 10.8 us -> 4.14 us
    reduce_scatter x2 -> x0, waiting for transfers between devices: 79.5 us -> none  [the longest x1 54.1 us: body(): lax.psum_scatter(jnp.transpose(summed, (2, 0, 1, 3)), 'va', scatter_dimen...]
    pallas_call x0 -> x8, Pallas kernels: none -> 46.3 us  [the longest x4 23.3 us: update(): pl.pallas_call(functools.partial(update_kernel, len(seps)), grid_spec=plt...]
    ppermute x0 -> x24, starting transfers between devices: none -> 31.8 us  [swap(): return lax.ppermute(x, axis, [(i, i ^ mask) for i in range(n)])]
    reduce_sum x2 -> x0, other arithmetic: 31.2 us -> none  [the longest x1 18.7 us: body(): partial_value = jnp.sum(updated_b, axis=(1, 4)) * (1.0 / (P_SIZE * R2))]
    all_to_all x1 -> x0, blocking collectives: 18.9 us -> none  [body(): lax.all_to_all(shares, 'vb', split_axis=3, concat_axis=1, tiled=True)]
    ppermute x0 -> x24, waiting for transfers between devices: none -> 13.1 us  [swap(): return lax.ppermute(x, axis, [(i, i ^ mask) for i in range(n)])]
    add x0 -> x14, other arithmetic: none -> 8.74 us  [the longest x2 2.66 us: body(): k0 = keep[0, 0, 0] + got[0, 0, 0] + x0[0]]
    transpose x2 -> x0, local copies, waits for them, and re-layouts: 4.93 us -> none  [body(): jnp.transpose(summed, (2, 0, 1, 3))]
  transfers between devices with their start and end apart: 2 -> 24, of which waited for: 2 -> 7; matrix products, arithmetic and copies ran while one was open for 0% -> 11% of each run, Pallas kernels for 0% -> 22%
where the time goes in v1:
time: 108 us; the launch traced here: 107 us
  Pallas kernels  46.3 us (43%)
  starting transfers between devices  31.8 us (29%)
  waiting for transfers between devices  13.1 us (12%)
  other arithmetic  10.9 us (10%)
  local copies, waits for them, and re-layouts  4.14 us (4%)
    ppermute x24, starting transfers between devices, swap(): return lax.ppermute(x, axis, [(i, i ^ mask) for i in range(n)])  31.8 us
    pallas_call x4, Pallas kernels, update(): pl.pallas_call(functools.partial(update_kernel, len(seps)), grid_spec=plt...  23.3 us
    pallas_call x4, Pallas kernels, absorb(): pl.pallas_call(absorb_kernel, grid_spec=pltpu.PrefetchScalarGridSpec(num_...  23 us
    ppermute x24, waiting for transfers between devices, swap(): return lax.ppermute(x, axis, [(i, i ^ mask) for i in range(n)])  13.1 us
    add x2, other arithmetic, body(): k0 = keep[0, 0, 0] + got[0, 0, 0] + x0[0]  2.66 us
    add x2, other arithmetic, body(): x0 = keep[:, 1, 0] + got[:, 1, 0]  2.43 us
  transfers between devices with their start and end apart: 24, of which 7 were waited for; matrix products, arithmetic and copies ran while one was open for 11% of the time, Pallas kernels for 22%

profile of v1, /device:TPU:0, one launch (start us, length us, event | category | flops | bytes accessed | tf_op | source)
XLA Modules:
  0.0 107.1 jit_solution(12503628231766186465)
XLA Ops:
  1.2 5.7 %absorb.4 = (f32[2,2,2,16,32768]{4,3,2,1,0:T(8,128)}, f32[4,2,4,2,8,512]{5,4,3,2,1,0:T(8,128)}) custom-call(s32[5]{0:T(128)} %stack.95.tab_ref, f32[2,2,2,16,32768]{4,3,2,1,0:T(8,128)} %a_ref.7, f32[2,2,32768]{2,1,0:T(2,128)} %m_ref.7), custom_call_target="tpu_custom_call" | custom-call | flops 2097152 | bytes 9437184 | tf_op jit(solution)/shard_map/absorb/pallas_call | solution.py:92
  7.0 5.7 %absorb.5 = (f32[2,2,2,16,32768]{4,3,2,1,0:T(8,128)}, f32[4,2,4,2,8,512]{5,4,3,2,1,0:T(8,128)}) custom-call(s32[5]{0:T(128)} %stack.95.tab_ref, f32[2,2,2,16,32768]{4,3,2,1,0:T(8,128)} %a_ref.7, f32[2,2,32768]{2,1,0:T(2,128)} %m_ref.7, f32[2,2,2,16,32768]{4,3,2,1,0:T(8,128)} %get-tuple-element.19.rest_0_), custom_call_target="tpu_custom_call", output_to_operand_aliasing={{0}: (3, {})} | custom-call | flops 2097152 | bytes 9437184 | tf_op jit(solution)/shard_map/absorb/pallas_call | solution.py:92
  12.7 5.7 %absorb.6 = (f32[2,2,2,16,32768]{4,3,2,1,0:T(8,128)}, f32[4,2,4,2,8,512]{5,4,3,2,1,0:T(8,128)}) custom-call(s32[5]{0:T(128)} %stack.95.tab_ref, f32[2,2,2,16,32768]{4,3,2,1,0:T(8,128)} %a_ref.7, f32[2,2,32768]{2,1,0:T(2,128)} %m_ref.7, f32[2,2,2,16,32768]{4,3,2,1,0:T(8,128)} %get-tuple-element.20.rest_0_), custom_call_target="tpu_custom_call", output_to_operand_aliasing={{0}: (3, {})} | custom-call | flops 2097152 | bytes 9437184 | tf_op jit(solution)/shard_map/absorb/pallas_call | solution.py:92
  18.9 5.9 %absorb.7 = (f32[2,2,2,16,32768]{4,3,2,1,0:T(8,128)}, f32[4,2,4,2,8,512]{5,4,3,2,1,0:T(8,128)}) custom-call(s32[5]{0:T(128)} %stack.95.tab_ref, f32[2,2,2,16,32768]{4,3,2,1,0:T(8,128)} %a_ref.7, f32[2,2,32768]{2,1,0:T(2,128)} %m_ref.7, f32[2,2,2,16,32768]{4,3,2,1,0:T(8,128)} %get-tuple-element.21.rest_0_), custom_call_target="tpu_custom_call", output_to_operand_aliasing={{0}: (3, {})} | custom-call | flops 2097152 | bytes 9437184 | tf_op jit(solution)/shard_map/absorb/pallas_call | solution.py:92
  24.8 1.7 %fusion.5 = f32[2,4,2,8,512]{4,3,2,1,0:T(8,128)} fusion(f32[2,2,2,4,2,8,512]{6,5,4,3,2,1,0:T(8,128)S(1)} %bitcast.169, f32[2,2,2,4,2,8,512]{6,5,4,3,2,1,0:T(8,128)} %bitcast.172), kind=kLoop, calls=%fused_computation.10 | loop fusion | flops 65536 | bytes 786432 | tf_op jit(solution)/shard_map/add | solution.py:227
  26.5 2.9 %collective-permute-start.1 = (f32[2,4,2,8,512]{4,3,2,1,0:T(8,128)}, f32[2,4,2,8,512]{4,3,2,1,0:T(8,128)}, u32[]{:S(2)}, u32[]{:S(2)}) collective-permute-start(f32[2,4,2,8,512]{4,3,2,1,0:T(8,128)} %fusion.5), channel_id=1, source_target_pairs={{0,8},{4,12},{8,0},{12,4},{16,24},{20,28},{24,16},{28,20},{1,9},{5... | collective-permute-start | bytes 786440 | tf_op jit(solution)/shard_map/ppermute | solution.py:45
  29.4 1.7 %fusion.3 = f32[2,4,2,8,512]{4,3,2,1,0:T(8,128)} fusion(f32[2,2,2,4,2,8,512]{6,5,4,3,2,1,0:T(8,128)S(1)} %bitcast.170, f32[2,2,2,4,2,8,512]{6,5,4,3,2,1,0:T(8,128)} %bitcast.173), kind=kLoop, calls=%fused_computation.7 | loop fusion | flops 65536 | bytes 786432 | tf_op jit(solution)/shard_map/add | solution.py:228
  31.1 1.5 %collective-permute-start.3 = (f32[2,4,2,8,512]{4,3,2,1,0:T(8,128)}, f32[2,4,2,8,512]{4,3,2,1,0:T(8,128)}, u32[]{:S(2)}, u32[]{:S(2)}) collective-permute-start(f32[2,4,2,8,512]{4,3,2,1,0:T(8,128)} %fusion.3), channel_id=1, source_target_pairs={{0,16},{4,20},{8,24},{12,28},{16,0},{20,4},{24,8},{28,12},{1,17},{... | collective-permute-start | bytes 786440 | tf_op jit(solution)/shard_map/ppermute | solution.py:45
  36.6 4.0 %collective-permute-done.3 = f32[2,4,2,8,512]{4,3,2,1,0:T(8,128)} collective-permute-done((f32[2,4,2,8,512]{4,3,2,1,0:T(8,128)}, f32[2,4,2,8,512]{4,3,2,1,0:T(8,128)}, u32[]{:S(2)}, u32[]{:S(2)}) %collective-permute-start.3) | collective-permute-done | bytes 262176 | tf_op jit(solution)/shard_map/ppermute | solution.py:45
  42.0 1.6 %collective-permute-start.2 = (f32[4,2,8,512]{3,2,1,0:T(8,128)S(1)}, f32[4,2,8,512]{3,2,1,0:T(8,128)S(1)}, u32[]{:S(2)}, u32[]{:S(2)}) collective-permute-start(f32[4,2,8,512]{3,2,1,0:T(8,128)S(1)} %get-tuple-element.40), channel_id=1, source_target_pairs={{0,16},{4,20},{8,24},{12,28},{16,0},{20,4},{24,8},{28,12},{1,17},{... | collective-permute-start | bytes 393224 | tf_op jit(solution)/shard_map/ppermute | solution.py:45
  44.2 2.1 %collective-permute-done.11 = f32[2,4,2,8,512]{4,3,2,1,0:T(8,128)} collective-permute-done((f32[2,4,2,8,512]{4,3,2,1,0:T(8,128)S(1)}, f32[2,4,2,8,512]{4,3,2,1,0:T(8,128)}, u32[]{:S(2)}, u32[]{:S(2)}) %collective-permute-start.11) | collective-permute-done | bytes 262176 | tf_op jit(solution)/shard_map/ppermute | solution.py:45
  47.5 1.6 %collective-permute-start.10 = (f32[4,2,8,512]{3,2,1,0:T(8,128)S(1)}, f32[4,2,8,512]{3,2,1,0:T(8,128)S(1)}, u32[]{:S(2)}, u32[]{:S(2)}) collective-permute-start(f32[4,2,8,512]{3,2,1,0:T(8,128)S(1)} %get-tuple-element.36), channel_id=1, source_target_pairs={{0,16},{4,20},{8,24},{12,28},{16,0},{20,4},{24,8},{28,12},{1,17},{... | collective-permute-start | bytes 393224 | tf_op jit(solution)/shard_map/ppermute | solution.py:45
  49.7 1.6 %collective-permute-start.5 = (f32[2,2,8,512]{3,2,1,0:T(8,128)S(1)}, f32[2,2,8,512]{3,2,1,0:T(8,128)S(1)}, u32[]{:S(2)}, u32[]{:S(2)}) collective-permute-start(f32[2,2,8,512]{3,2,1,0:T(8,128)S(1)} %pad_maximum_fusion.3), channel_id=1, source_target_pairs={{0,1},{1,0},{2,3},{3,2},{4,5},{5,4},{6,7},{7,6},{8,9},{9,8},{10,11... | collective-permute-start | bytes 196616 | tf_op jit(solution)/shard_map/ppermute | solution.py:45
  51.3 2.6 %collective-permute-start.6 = (f32[2,2,8,512]{3,2,1,0:T(8,128)S(1)}, f32[2,2,8,512]{3,2,1,0:T(8,128)S(1)}, u32[]{:S(2)}, u32[]{:S(2)}) collective-permute-start(f32[2,2,8,512]{3,2,1,0:T(8,128)S(1)} %pad_maximum_fusion.4), channel_id=1, source_target_pairs={{0,2},{1,3},{2,0},{3,1},{4,6},{5,7},{6,4},{7,5},{8,10},{9,11},{10,... | collective-permute-start | bytes 196616 | tf_op jit(solution)/shard_map/ppermute | solution.py:45
  54.2 1.5 %collective-permute-start.13 = (f32[2,2,8,512]{3,2,1,0:T(8,128)S(1)}, f32[2,2,8,512]{3,2,1,0:T(8,128)S(1)}, u32[]{:S(2)}, u32[]{:S(2)}) collective-permute-start(f32[2,2,8,512]{3,2,1,0:T(8,128)S(1)} %pad_maximum_fusion.7), channel_id=1, source_target_pairs={{0,1},{1,0},{2,3},{3,2},{4,5},{5,4},{6,7},{7,6},{8,9},{9,8},{10,11... | collective-permute-start | bytes 196616 | tf_op jit(solution)/shard_map/ppermute | solution.py:45
  55.7 2.7 %collective-permute-start.14 = (f32[2,2,8,512]{3,2,1,0:T(8,128)S(1)}, f32[2,2,8,512]{3,2,1,0:T(8,128)S(1)}, u32[]{:S(2)}, u32[]{:S(2)}) collective-permute-start(f32[2,2,8,512]{3,2,1,0:T(8,128)S(1)} %pad_maximum_fusion.8), channel_id=1, source_target_pairs={{0,2},{1,3},{2,0},{3,1},{4,6},{5,7},{6,4},{7,5},{8,10},{9,11},{10,... | collective-permute-start | bytes 196616 | tf_op jit(solution)/shard_map/ppermute | solution.py:45
  59.1 3.0 %collective-permute-start.15 = (f32[2,2,8,512]{3,2,1,0:T(8,128)S(1)}, f32[2,2,8,512]{3,2,1,0:T(8,128)S(1)}, u32[]{:S(2)}, u32[]{:S(2)}) collective-permute-start(f32[2,2,8,512]{3,2,1,0:T(8,128)S(1)} %pad_maximum_fusion.9), channel_id=1, source_target_pairs={{0,3},{1,2},{2,1},{3,0},{4,7},{5,6},{6,5},{7,4},{8,11},{9,10},{10,... | collective-permute-start | bytes 196616 | tf_op jit(solution)/shard_map/ppermute | solution.py:45
  62.8 2.4 %collective-permute-done.15.rest_3_ = f32[2,2,8,512]{3,2,1,0:T(8,128)S(1)} collective-permute-done((f32[2,2,8,512]{3,2,1,0:T(8,128)S(1)}, f32[2,2,8,512]{3,2,1,0:T(8,128)S(1)}, u32[]{:S(2)}, u32[]{:S(2)}) %collective-permute-start.15) | collective-permute-done | bytes 65568 | tf_op jit(solution)/shard_map/ppermute | solution.py:45
  65.8 5.8 %update.4 = (f32[32,8,128,128]{3,2,1,0:T(8,128)}, f32[4,4,32,128]{3,2,1,0:T(8,128)}) custom-call(s32[9]{0:T(128)} %concatenate.22.tab_ref, f32[32,8,128,128]{3,2,1,0:T(8,128)} %bitcast.154, f32[8,128,128]{2,1,0:T(8,128)} %bitcast.159, f32[2,2,8,512]{3,2,1,0:T(8,128)} %pad_maximum_fusion.6.rest_0_, f32[2,2,8,512]{3,2,1,0:T(8,128)} %copy-done.4, ...), custom_call_target="tpu_custom_call" | custom-call | flops 2097152 | bytes 8388608 | tf_op jit(solution)/shard_map/update/pallas_call | solution.py:176
  71.6 5.8 %update.5 = (f32[32,8,128,128]{3,2,1,0:T(8,128)}, f32[4,4,32,128]{3,2,1,0:T(8,128)}) custom-call(s32[9]{0:T(128)} %concatenate.21.tab_ref, f32[32,8,128,128]{3,2,1,0:T(8,128)} %bitcast.155, f32[8,128,128]{2,1,0:T(8,128)} %bitcast.160, f32[2,2,8,512]{3,2,1,0:T(8,128)} %pad_maximum_fusion.6.rest_0_, ...), custom_call_target="tpu_custom_call", output_to_operand_aliasing={{0}: (7, {})} | custom-call | flops 2097152 | bytes 8388608 | tf_op jit(solution)/shard_map/update/pallas_call | solution.py:176
  78.1 5.9 %update.6 = (f32[32,8,128,128]{3,2,1,0:T(8,128)}, f32[4,4,32,128]{3,2,1,0:T(8,128)}) custom-call(s32[9]{0:T(128)} %concatenate.22.tab_ref, f32[32,8,128,128]{3,2,1,0:T(8,128)} %bitcast.156, f32[8,128,128]{2,1,0:T(8,128)} %bitcast.161, f32[2,2,8,512]{3,2,1,0:T(8,128)} %pad_maximum_fusion.2.rest_0_, ...), custom_call_target="tpu_custom_call", output_to_operand_aliasing={{0}: (7, {})} | custom-call | flops 2097152 | bytes 8388608 | tf_op jit(solution)/shard_map/update/pallas_call | solution.py:176
  85.0 3.1 %collective-permute-start.22 = (f32[2,4,32,128]{3,2,1,0:T(8,128)S(1)}, f32[2,4,32,128]{3,2,1,0:T(8,128)S(1)}, u32[]{:S(2)}, u32[]{:S(2)}) collective-permute-start(f32[2,4,32,128]{3,2,1,0:T(8,128)S(1)} %get-tuple-element.58), channel_id=1, source_target_pairs={{0,3},{1,2},{2,1},{3,0},{4,7},{5,6},{6,5},{7,4},{8,11},{9,10},{10,... | collective-permute-start | bytes 393224 | tf_op jit(solution)/shard_map/ppermute | solution.py:45
  90.2 5.9 %update.7 = (f32[32,8,128,128]{3,2,1,0:T(8,128)}, f32[4,4,32,128]{3,2,1,0:T(8,128)}) custom-call(s32[9]{0:T(128)} %concatenate.21.tab_ref, f32[32,8,128,128]{3,2,1,0:T(8,128)} %bitcast.157, f32[8,128,128]{2,1,0:T(8,128)} %bitcast.162, f32[2,2,8,512]{3,2,1,0:T(8,128)} %pad_maximum_fusion.2.rest_0_, ...), custom_call_target="tpu_custom_call", output_to_operand_aliasing={{0}: (7, {})} | custom-call | flops 2097152 | bytes 8388608 | tf_op jit(solution)/shard_map/update/pallas_call | solution.py:176
  97.0 3.0 %collective-permute-start.21 = (f32[4,32,128]{2,1,0:T(8,128)S(1)}, f32[4,32,128]{2,1,0:T(8,128)S(1)}, u32[]{:S(2)}, u32[]{:S(2)}) collective-permute-start(f32[4,32,128]{2,1,0:T(8,128)S(1)} %get-tuple-element.55), channel_id=1, source_target_pairs={{0,3},{1,2},{2,1},{3,0},{4,7},{5,6},{6,5},{7,4},{8,11},{9,10},{10,... | collective-permute-start | bytes 196616 | tf_op jit(solution)/shard_map/ppermute | solution.py:45
  (80 shorter events, 22.8 us)
Async XLA Ops:
  18.4 6.4 %collective-permute-start = (f32[4,2,4,2,8,512]{5,4,3,2,1,0:T(8,128)}, f32[4,2,4,2,8,512]{5,4,3,2,1,0:T(8,128)S(1)}, u32[]{:S(2)}, u32[]{:S(2)}) collective-permute-start(f32[4,2,4,2,8,512]{5,4,3,2,1,0:T(8,128)} %get-tuple-element.24), channel_id=1, source_target_pairs={{0,4},{4,0},{8,12},{12,8},{16,20},{20,16},{24,28},{28,24},{1,5},{5... | collective-permute-start | bytes 3145736 | tf_op jit(solution)/shard_map/ppermute | solution.py:45
  18.9 13.8 %collective-permute-start.8 = (f32[4,2,4,2,8,512]{5,4,3,2,1,0:T(8,128)}, f32[4,2,4,2,8,512]{5,4,3,2,1,0:T(8,128)S(1)}, u32[]{:S(2)}, u32[]{:S(2)}) collective-permute-start(f32[4,2,4,2,8,512]{5,4,3,2,1,0:T(8,128)} %get-tuple-element.26), channel_id=1, source_target_pairs={{0,4},{4,0},{8,12},{12,8},{16,20},{20,16},{24,28},{28,24},{1,5},{5... | collective-permute-start | bytes 3145736 | tf_op jit(solution)/shard_map/ppermute | solution.py:45
  26.5 10.1 %collective-permute-start.1 = (f32[2,4,2,8,512]{4,3,2,1,0:T(8,128)}, f32[2,4,2,8,512]{4,3,2,1,0:T(8,128)}, u32[]{:S(2)}, u32[]{:S(2)}) collective-permute-start(f32[2,4,2,8,512]{4,3,2,1,0:T(8,128)} %fusion.5), channel_id=1, source_target_pairs={{0,8},{4,12},{8,0},{12,4},{16,24},{20,28},{24,16},{28,20},{1,9},{5... | collective-permute-start | bytes 786440 | tf_op jit(solution)/shard_map/ppermute | solution.py:45
  31.1 9.5 %collective-permute-start.3 = (f32[2,4,2,8,512]{4,3,2,1,0:T(8,128)}, f32[2,4,2,8,512]{4,3,2,1,0:T(8,128)}, u32[]{:S(2)}, u32[]{:S(2)}) collective-permute-start(f32[2,4,2,8,512]{4,3,2,1,0:T(8,128)} %fusion.3), channel_id=1, source_target_pairs={{0,16},{4,20},{8,24},{12,28},{16,0},{20,4},{24,8},{28,12},{1,17},{... | collective-permute-start | bytes 786440 | tf_op jit(solution)/shard_map/ppermute | solution.py:45
  33.4 10.8 %collective-permute-start.9 = (f32[2,4,2,8,512]{4,3,2,1,0:T(8,128)}, f32[2,4,2,8,512]{4,3,2,1,0:T(8,128)}, u32[]{:S(2)}, u32[]{:S(2)}) collective-permute-start(f32[2,4,2,8,512]{4,3,2,1,0:T(8,128)} %fusion.2), channel_id=1, source_target_pairs={{0,8},{4,12},{8,0},{12,4},{16,24},{20,28},{24,16},{28,20},{1,9},{5... | collective-permute-start | bytes 786440 | tf_op jit(solution)/shard_map/ppermute | solution.py:45
  33.9 12.3 %collective-permute-start.11 = (f32[2,4,2,8,512]{4,3,2,1,0:T(8,128)S(1)}, f32[2,4,2,8,512]{4,3,2,1,0:T(8,128)}, u32[]{:S(2)}, u32[]{:S(2)}) collective-permute-start(f32[2,4,2,8,512]{4,3,2,1,0:T(8,128)S(1)} %fusion), channel_id=1, source_target_pairs={{0,16},{4,20},{8,24},{12,28},{16,0},{20,4},{24,8},{28,12},{1,17},{... | collective-permute-start | bytes 786440 | tf_op jit(solution)/shard_map/ppermute | solution.py:45
  42.0 7.6 %collective-permute-start.2 = (f32[4,2,8,512]{3,2,1,0:T(8,128)S(1)}, f32[4,2,8,512]{3,2,1,0:T(8,128)S(1)}, u32[]{:S(2)}, u32[]{:S(2)}) collective-permute-start(f32[4,2,8,512]{3,2,1,0:T(8,128)S(1)} %get-tuple-element.40), channel_id=1, source_target_pairs={{0,16},{4,20},{8,24},{12,28},{16,0},{20,4},{24,8},{28,12},{1,17},{... | collective-permute-start | bytes 393224 | tf_op jit(solution)/shard_map/ppermute | solution.py:45
  43.6 6.0 %collective-permute-start.4 = (f32[4,2,8,512]{3,2,1,0:T(8,128)S(1)}, f32[4,2,8,512]{3,2,1,0:T(8,128)S(1)}, u32[]{:S(2)}, u32[]{:S(2)}) collective-permute-start(f32[4,2,8,512]{3,2,1,0:T(8,128)S(1)} %get-tuple-element.45), channel_id=1, source_target_pairs={{0,8},{4,12},{8,0},{12,4},{16,24},{20,28},{24,16},{28,20},{1,9},{5... | collective-permute-start | bytes 393224 | tf_op jit(solution)/shard_map/ppermute | solution.py:45
  47.5 6.7 %collective-permute-start.10 = (f32[4,2,8,512]{3,2,1,0:T(8,128)S(1)}, f32[4,2,8,512]{3,2,1,0:T(8,128)S(1)}, u32[]{:S(2)}, u32[]{:S(2)}) collective-permute-start(f32[4,2,8,512]{3,2,1,0:T(8,128)S(1)} %get-tuple-element.36), channel_id=1, source_target_pairs={{0,16},{4,20},{8,24},{12,28},{16,0},{20,4},{24,8},{28,12},{1,17},{... | collective-permute-start | bytes 393224 | tf_op jit(solution)/shard_map/ppermute | solution.py:45
  49.0 5.1 %collective-permute-start.12 = (f32[4,2,8,512]{3,2,1,0:T(8,128)S(1)}, f32[4,2,8,512]{3,2,1,0:T(8,128)S(1)}, u32[]{:S(2)}, u32[]{:S(2)}) collective-permute-start(f32[4,2,8,512]{3,2,1,0:T(8,128)S(1)} %get-tuple-element.43), channel_id=1, source_target_pairs={{0,8},{4,12},{8,0},{12,4},{16,24},{20,28},{24,16},{28,20},{1,9},{5... | collective-permute-start | bytes 393224 | tf_op jit(solution)/shard_map/ppermute | solution.py:45
  49.7 27.7 %collective-permute-start.5 = (f32[2,2,8,512]{3,2,1,0:T(8,128)S(1)}, f32[2,2,8,512]{3,2,1,0:T(8,128)S(1)}, u32[]{:S(2)}, u32[]{:S(2)}) collective-permute-start(f32[2,2,8,512]{3,2,1,0:T(8,128)S(1)} %pad_maximum_fusion.3), channel_id=1, source_target_pairs={{0,1},{1,0},{2,3},{3,2},{4,5},{5,4},{6,7},{7,6},{8,9},{9,8},{10,11... | collective-permute-start | bytes 196616 | tf_op jit(solution)/shard_map/ppermute | solution.py:45
  51.3 26.1 %collective-permute-start.6 = (f32[2,2,8,512]{3,2,1,0:T(8,128)S(1)}, f32[2,2,8,512]{3,2,1,0:T(8,128)S(1)}, u32[]{:S(2)}, u32[]{:S(2)}) collective-permute-start(f32[2,2,8,512]{3,2,1,0:T(8,128)S(1)} %pad_maximum_fusion.4), channel_id=1, source_target_pairs={{0,2},{1,3},{2,0},{3,1},{4,6},{5,7},{6,4},{7,5},{8,10},{9,11},{10,... | collective-permute-start | bytes 196616 | tf_op jit(solution)/shard_map/ppermute | solution.py:45
  53.9 23.5 %collective-permute-start.7 = (f32[2,2,8,512]{3,2,1,0:T(8,128)S(1)}, f32[2,2,8,512]{3,2,1,0:T(8,128)S(1)}, u32[]{:S(2)}, u32[]{:S(2)}) collective-permute-start(f32[2,2,8,512]{3,2,1,0:T(8,128)S(1)} %pad_maximum_fusion.5), channel_id=1, source_target_pairs={{0,3},{1,2},{2,1},{3,0},{4,7},{5,6},{6,5},{7,4},{8,11},{9,10},{10,... | collective-permute-start | bytes 196616 | tf_op jit(solution)/shard_map/ppermute | solution.py:45
  54.2 4.9 %collective-permute-start.13 = (f32[2,2,8,512]{3,2,1,0:T(8,128)S(1)}, f32[2,2,8,512]{3,2,1,0:T(8,128)S(1)}, u32[]{:S(2)}, u32[]{:S(2)}) collective-permute-start(f32[2,2,8,512]{3,2,1,0:T(8,128)S(1)} %pad_maximum_fusion.7), channel_id=1, source_target_pairs={{0,1},{1,0},{2,3},{3,2},{4,5},{5,4},{6,7},{7,6},{8,9},{9,8},{10,11... | collective-permute-start | bytes 196616 | tf_op jit(solution)/shard_map/ppermute | solution.py:45
  55.7 7.1 %collective-permute-start.14 = (f32[2,2,8,512]{3,2,1,0:T(8,128)S(1)}, f32[2,2,8,512]{3,2,1,0:T(8,128)S(1)}, u32[]{:S(2)}, u32[]{:S(2)}) collective-permute-start(f32[2,2,8,512]{3,2,1,0:T(8,128)S(1)} %pad_maximum_fusion.8), channel_id=1, source_target_pairs={{0,2},{1,3},{2,0},{3,1},{4,6},{5,7},{6,4},{7,5},{8,10},{9,11},{10,... | collective-permute-start | bytes 196616 | tf_op jit(solution)/shard_map/ppermute | solution.py:45
  59.1 6.1 %collective-permute-start.15 = (f32[2,2,8,512]{3,2,1,0:T(8,128)S(1)}, f32[2,2,8,512]{3,2,1,0:T(8,128)S(1)}, u32[]{:S(2)}, u32[]{:S(2)}) collective-permute-start(f32[2,2,8,512]{3,2,1,0:T(8,128)S(1)} %pad_maximum_fusion.9), channel_id=1, source_target_pairs={{0,3},{1,2},{2,1},{3,0},{4,7},{5,6},{6,5},{7,4},{8,11},{9,10},{10,... | collective-permute-start | bytes 196616 | tf_op jit(solution)/shard_map/ppermute | solution.py:45
  85.0 11.1 %collective-permute-start.20 = (f32[2,4,32,128]{3,2,1,0:T(8,128)S(1)}, f32[2,4,32,128]{3,2,1,0:T(8,128)S(1)}, u32[]{:S(2)}, u32[]{:S(2)}) collective-permute-start(f32[2,4,32,128]{3,2,1,0:T(8,128)S(1)} %get-tuple-element.57), channel_id=1, source_target_pairs={{0,1},{1,0},{2,3},{3,2},{4,5},{5,4},{6,7},{7,6},{8,9},{9,8},{10,11... | collective-permute-start | bytes 393224 | tf_op jit(solution)/shard_map/ppermute | solution.py:45
  85.0 11.0 %collective-permute-start.22 = (f32[2,4,32,128]{3,2,1,0:T(8,128)S(1)}, f32[2,4,32,128]{3,2,1,0:T(8,128)S(1)}, u32[]{:S(2)}, u32[]{:S(2)}) collective-permute-start(f32[2,4,32,128]{3,2,1,0:T(8,128)S(1)} %get-tuple-element.58), channel_id=1, source_target_pairs={{0,3},{1,2},{2,1},{3,0},{4,7},{5,6},{6,5},{7,4},{8,11},{9,10},{10,... | collective-permute-start | bytes 393224 | tf_op jit(solution)/shard_map/ppermute | solution.py:45
  88.1 11.8 %collective-permute-start.16 = (f32[2,4,32,128]{3,2,1,0:T(8,128)S(1)}, f32[2,4,32,128]{3,2,1,0:T(8,128)S(1)}, u32[]{:S(2)}, u32[]{:S(2)}) collective-permute-start(f32[2,4,32,128]{3,2,1,0:T(8,128)S(1)} %get-tuple-element.51), channel_id=1, source_target_pairs={{0,1},{1,0},{2,3},{3,2},{4,5},{5,4},{6,7},{7,6},{8,9},{9,8},{10,11... | collective-permute-start | bytes 393224 | tf_op jit(solution)/shard_map/ppermute | solution.py:45
  89.3 10.7 %collective-permute-start.18 = (f32[2,4,32,128]{3,2,1,0:T(8,128)S(1)}, f32[2,4,32,128]{3,2,1,0:T(8,128)S(1)}, u32[]{:S(2)}, u32[]{:S(2)}) collective-permute-start(f32[2,4,32,128]{3,2,1,0:T(8,128)S(1)} %get-tuple-element.52), channel_id=1, source_target_pairs={{0,3},{1,2},{2,1},{3,0},{4,7},{5,6},{6,5},{7,4},{8,11},{9,10},{10,... | collective-permute-start | bytes 393224 | tf_op jit(solution)/shard_map/ppermute | solution.py:45
  97.0 6.1 %collective-permute-start.21 = (f32[4,32,128]{2,1,0:T(8,128)S(1)}, f32[4,32,128]{2,1,0:T(8,128)S(1)}, u32[]{:S(2)}, u32[]{:S(2)}) collective-permute-start(f32[4,32,128]{2,1,0:T(8,128)S(1)} %get-tuple-element.55), channel_id=1, source_target_pairs={{0,3},{1,2},{2,1},{3,0},{4,7},{5,6},{6,5},{7,4},{8,11},{9,10},{10,... | collective-permute-start | bytes 196616 | tf_op jit(solution)/shard_map/ppermute | solution.py:45
  100.0 4.3 %collective-permute-start.23 = (f32[4,32,128]{2,1,0:T(8,128)S(1)}, f32[4,32,128]{2,1,0:T(8,128)S(1)}, u32[]{:S(2)}, u32[]{:S(2)}) collective-permute-start(f32[4,32,128]{2,1,0:T(8,128)S(1)} %get-tuple-element.56), channel_id=1, source_target_pairs={{0,1},{1,0},{2,3},{3,2},{4,5},{5,4},{6,7},{7,6},{8,9},{9,8},{10,11... | collective-permute-start | bytes 196616 | tf_op jit(solution)/shard_map/ppermute | solution.py:45
  100.0 6.2 %collective-permute-start.17 = (f32[4,32,128]{2,1,0:T(8,128)S(1)}, f32[4,32,128]{2,1,0:T(8,128)S(1)}, u32[]{:S(2)}, u32[]{:S(2)}) collective-permute-start(f32[4,32,128]{2,1,0:T(8,128)S(1)} %get-tuple-element.49), channel_id=1, source_target_pairs={{0,3},{1,2},{2,1},{3,0},{4,7},{5,6},{6,5},{7,4},{8,11},{9,10},{10,... | collective-permute-start | bytes 196616 | tf_op jit(solution)/shard_map/ppermute | solution.py:45
  101.0 5.3 %collective-permute-start.19 = (f32[4,32,128]{2,1,0:T(8,128)S(1)}, f32[4,32,128]{2,1,0:T(8,128)S(1)}, u32[]{:S(2)}, u32[]{:S(2)}) collective-permute-start(f32[4,32,128]{2,1,0:T(8,128)S(1)} %get-tuple-element.50), channel_id=1, source_target_pairs={{0,1},{1,0},{2,3},{3,2},{4,5},{5,4},{6,7},{7,6},{8,9},{9,8},{10,11... | collective-permute-start | bytes 196616 | tf_op jit(solution)/shard_map/ppermute | solution.py:45
  (9 other events, 44.7 us)

commit v2 on v0

--- a/solution.py
+++ b/solution.py
@@ -1,6 +1,10 @@
+import functools
+
 import jax
 import jax.numpy as jnp
 from jax import lax
+from jax.experimental import pallas as pl
+from jax.experimental.pallas import tpu as pltpu
 from jax.sharding import PartitionSpec as P
 
 H = 16
@@ -9,9 +13,13 @@
 R1 = 16
 R2 = 8
 R3 = 256
-
-
-def body(clique_a, message_in, clique_b, old_separator):
+LANES = 128
+QT = 8
+SCOPED = 2 * 2**20
+SCOPED_UPDATE = 12 * 2**20
+
+
+def generic_body(clique_a, message_in, clique_b, old_separator):
     p_local = clique_a.shape[1]
     q_total = clique_a.shape[3]
     r_total = clique_a.shape[4]
@@ -34,9 +42,330 @@
     return (absorbed, updated_b, onward)
 
 
+def tie(x, *after):
+    return lax.optimization_barrier((x, *after))[0]
+
+
+def in_hbm(x):
+    return pltpu.with_memory_space_constraint(x, pltpu.HBM)
+
+
+def swap(x, axis, mask):
+    n = lax.axis_size(axis)
+    return lax.ppermute(x, axis, [(i, i ^ mask) for i in range(n)])
+
+
+def absorb_kernel(chunk, part, me_ref, z_ref, a_hbm, m_hbm, prod, s_ref, msg, sems, msems):
+    n, nh, npl, nk, _, block = prod.shape
+    nm, nr1, width = s_ref.shape[2], s_ref.shape[3], s_ref.shape[5]
+    copies = []
+    for g in range(n):
+        lanes = pl.ds(pl.multiple_of((me_ref[0] ^ (2 * g + part)) * block, block), block)
+        group = [pltpu.make_async_copy(m_hbm.at[:, :, lanes], msg.at[g], msems.at[g])]
+        for h in range(nh):
+            group.append(
+                pltpu.make_async_copy(
+                    a_hbm.at[h, :, :, pl.ds(chunk * QT, QT), lanes],
+                    prod.at[g, h],
+                    sems.at[g * nh + h],
+                )
+            )
+        for copy in group:
+            copy.start()
+        copies.append(group)
+    for g in range(n):
+        for copy in copies[g]:
+            copy.wait()
+        for r1 in range(nr1):
+            for m in range(nm):
+                off = r1 * (nm * width) + (z_ref[0] ^ m) * width
+                lanes = pl.ds(pl.multiple_of(off, width), width)
+                rows = [
+                    [
+                        jnp.broadcast_to(msg[g, h, pl.ds(k, 1), lanes], (QT, width))
+                        for k in range(nk)
+                    ]
+                    for h in range(nh)
+                ]
+                for p in range(npl):
+                    total = None
+                    for h in range(nh):
+                        for k in range(nk):
+                            value = prod[g, h, p, k, :, lanes] * rows[h][k]
+                            prod[g, h, p, k, :, lanes] = value
+                            total = value if total is None else total + value
+                    s_ref[g, p, m, r1] = total
+
+
+def absorb(me, z, clique_a, message, chunk, part, n_va, n_vb):
+    nh, npl, nk, nq, nr = clique_a.shape
+    block = nr // n_va
+    nr1 = R1 // n_va
+    width = block // nr1 // n_vb
+    n = n_va // 2
+    n_a = n * nh * npl * nk * QT * block
+    return pl.pallas_call(
+        functools.partial(absorb_kernel, chunk, part),
+        in_specs=[
+            pl.BlockSpec(memory_space=pltpu.SMEM),
+            pl.BlockSpec(memory_space=pltpu.SMEM),
+            pl.BlockSpec(memory_space=pltpu.HBM),
+            pl.BlockSpec(memory_space=pltpu.HBM),
+        ],
+        out_specs=[pl.BlockSpec(memory_space=pltpu.VMEM)] * 2,
+        out_shape=[
+            pltpu.VMEM((n, nh, npl, nk, QT, block), clique_a.dtype),
+            pltpu.VMEM((n, npl, n_vb, nr1, QT, width), clique_a.dtype),
+        ],
+        scratch_shapes=[
+            pltpu.VMEM((n, nh, nk, block), jnp.float32),
+            pltpu.SemaphoreType.DMA((n * nh,)),
+            pltpu.SemaphoreType.DMA((n,)),
+        ],
+        compiler_params=pltpu.CompilerParams(vmem_limit_bytes=SCOPED),
+        cost_estimate=pl.CostEstimate(flops=2 * n_a, bytes_accessed=4 * n_a, transcendentals=0),
+        name="absorb",
+    )(me, z, in_hbm(clique_a), in_hbm(message))
+
+
+def flush_kernel(me_ref, *rest):
+    prods, out, sems = rest[:-2], rest[-2], rest[-1]
+    copies = []
+    for i, prod in enumerate(prods):
+        n, nh, block = prod.shape[0], prod.shape[1], prod.shape[5]
+        chunk, part = i // 2, 1 - i % 2
+        for g in range(n):
+            lanes = pl.ds(pl.multiple_of((me_ref[0] ^ (2 * g + part)) * block, block), block)
+            copies.append(
+                pltpu.make_async_copy(
+                    prod.at[g],
+                    out.at[:, :, :, pl.ds(chunk * QT, QT), lanes],
+                    sems.at[i * n + g],
+                )
+            )
+    for copy in copies:
+        copy.start()
+    for copy in copies:
+        copy.wait()
+
+
+def flush(me, prods, like):
+    return pl.pallas_call(
+        flush_kernel,
+        in_specs=[pl.BlockSpec(memory_space=pltpu.SMEM)]
+        + [pl.BlockSpec(memory_space=pltpu.VMEM)] * len(prods),
+        out_specs=pl.BlockSpec(memory_space=pltpu.HBM),
+        out_shape=jax.ShapeDtypeStruct(like.shape, like.dtype),
+        scratch_shapes=[pltpu.SemaphoreType.DMA((len(prods) * prods[0].shape[0],))],
+        compiler_params=pltpu.CompilerParams(vmem_limit_bytes=SCOPED),
+        cost_estimate=pl.CostEstimate(flops=0, bytes_accessed=4 * like.size, transcendentals=0),
+        name="flush",
+    )(me, *prods)
+
+
+def fetch_kernel(orders, z_ref, b_hbm, *rest):
+    helds, sems = rest[:-1], rest[-1]
+    copies = []
+    for order, held in zip(orders, helds):
+        be = held.shape[1]
+        for i, (m, half) in enumerate(order):
+            part = b_hbm.at[pl.ds(((z_ref[0] ^ m) * 2 + half) * be, be)]
+            copies.append(pltpu.make_async_copy(part, held.at[i], sems.at[len(copies)]))
+    for copy in copies:
+        copy.start()
+    for copy in copies:
+        copy.wait()
+
+
+def fetch(z, b_rows, orders, n_vb):
+    be = b_rows.shape[0] // n_vb // 2
+    return pl.pallas_call(
+        functools.partial(fetch_kernel, orders),
+        in_specs=[
+            pl.BlockSpec(memory_space=pltpu.SMEM),
+            pl.BlockSpec(memory_space=pltpu.HBM),
+        ],
+        out_specs=[pl.BlockSpec(memory_space=pltpu.VMEM)] * len(orders),
+        out_shape=[pltpu.VMEM((len(o), be) + b_rows.shape[1:], b_rows.dtype) for o in orders],
+        scratch_shapes=[pltpu.SemaphoreType.DMA((sum(len(o) for o in orders),))],
+        compiler_params=pltpu.CompilerParams(vmem_limit_bytes=SCOPED),
+        cost_estimate=pl.CostEstimate(flops=0, bytes_accessed=4 * b_rows.size, transcendentals=0),
+        name="fetch",
+    )(z, in_hbm(b_rows))
+
+
+def fill_scale(z_ref, old_ref, seps, scale):
+    nc, npl, nr1, _, width = seps[0].shape
+    nhi = R3 // LANES
+    nr2 = width // R3
+    tile = nr1 * nhi * nr2
+    for m, sep in enumerate(seps):
+        for p in range(npl):
+            row = (z_ref[0] ^ m) * npl + p
+            for c in range(nc):
+                for r1 in range(nr1):
+                    for r2 in range(nr2):
+                        for hi in range(nhi):
+                            at = (r2 * nhi + hi) * LANES
+                            first = c * QT * tile + (r1 * nhi + hi) * nr2 + r2
+                            scale[row, pl.ds(first, QT, stride=tile), :] = sep[
+                                c, p, r1, :, at : at + LANES
+                            ]
+    for p in range(scale.shape[0]):
+        scale[p] = scale[p] * (1.0 / (H * K)) / old_ref[p]
+
+
+def update_kernel(order, dims, z_ref, held, scale, out, on_ref, stage, col, sems):
+    nr1, nhi, nr2 = dims
+    n, be, npt, rows, _ = held.shape
+    tile = nr1 * nhi * nr2
+    copies = []
+    for i, (m, half) in enumerate(order):
+
+        def one(e, carry, i=i):
+            total = None
+            for p in range(npt):
+                value = held[i, e, p] * scale[p]
+                stage[i, e, p] = value
+                total = value if total is None else total + value
+            col[...] = total * (1.0 / (P_SIZE * R2))
+            for hi in range(nhi):
+                for r1 in range(nr1):
+                    acc = None
+                    for r2 in range(nr2):
+                        first = (r1 * nhi + hi) * nr2 + r2
+                        piece = col[pl.ds(first, rows // tile, stride=tile), :]
+                        acc = piece if acc is None else acc + piece
+                    on_ref[i, e, pl.ds(hi * nr1 + r1, rows // tile, stride=nhi * nr1), :] = acc
+            return carry
+
+        lax.fori_loop(0, be, one, 0)
+        copies.append(
+            pltpu.make_async_copy(
+                stage.at[i], out.at[pl.ds(((z_ref[0] ^ m) * 2 + half) * be, be)], sems.at[i]
+            )
+        )
+        copies[-1].start()
+    for copy in copies:
+        copy.wait()
+
+
+def first_update_kernel(order, dims, n_seps, z_ref, held, old_ref, *rest):
+    seps, (out, on_ref, scale, stage, col, sems) = rest[:n_seps], rest[n_seps:]
+    fill_scale(z_ref, old_ref, seps, scale)
+    update_kernel(order, dims, z_ref, held, scale, out, on_ref, stage, col, sems)
+
+
+def last_update_kernel(order, dims, z_ref, held, scale, before, out, on_ref, stage, col, sems):
+    update_kernel(order, dims, z_ref, held, scale, out, on_ref, stage, col, sems)
+
+
+def update(z, held, like, order, dims, seps=None, old=None, scale=None, before=None):
+    n, be, npt, rows, lanes = held.shape
+    nr1, nhi, nr2 = dims
+    vmem = pl.BlockSpec(memory_space=pltpu.VMEM)
+    hbm = pl.BlockSpec(memory_space=pltpu.HBM)
+    out_specs = [hbm, vmem]
+    out_shape = [
+        jax.ShapeDtypeStruct(like.shape, like.dtype),
+        pltpu.VMEM((n, be, rows // nr2, lanes), like.dtype),
+    ]
+    if before is None:
+        kernel = functools.partial(first_update_kernel, order, dims, len(seps))
+        args, in_specs, aliases = [z, held, old, *seps], [vmem] * (2 + len(seps)), {}
+        out_specs.append(vmem)
+        out_shape.append(pltpu.VMEM((npt, rows, lanes), like.dtype))
+    else:
+        kernel = functools.partial(last_update_kernel, order, dims)
+        args, in_specs, aliases = [z, held, scale, before], [vmem, vmem, hbm], {3: 0}
+    return pl.pallas_call(
+        kernel,
+        in_specs=[pl.BlockSpec(memory_space=pltpu.SMEM)] + in_specs,
+        out_specs=out_specs,
+        out_shape=out_shape,
+        scratch_shapes=[
+            pltpu.VMEM(held.shape, jnp.float32),
+            pltpu.VMEM((rows, lanes), jnp.float32),
+            pltpu.SemaphoreType.DMA((n,)),
+        ],
+        input_output_aliases=aliases,
+        compiler_params=pltpu.CompilerParams(vmem_limit_bytes=SCOPED_UPDATE),
+        cost_estimate=pl.CostEstimate(
+            flops=2 * held.size, bytes_accessed=4 * held.size, transcendentals=0
+        ),
+        name="update",
+    )(*args)
+
+
+def body(clique_a, message_in, clique_b, old_separator):
+    n_va, n_vb = lax.axis_size("va"), lax.axis_size("vb")
+    nq = clique_a.shape[3]
+    ne, npt, _, nr1, nr2, _ = clique_b.shape
+    nhi = R3 // LANES
+    n_chunks = nq // QT
+
+    me = lax.axis_index("va").astype(jnp.int32).reshape(1)
+    z = lax.axis_index("vb").astype(jnp.int32).reshape(1)
+
+    def rows_view(x):
+        lead = x.shape[:-3]
+        x = x.reshape(lead + (nr1, nr2, nhi, LANES))
+        n = len(lead)
+        x = jnp.swapaxes(x, n + 1, n + 2)
+        return x.reshape(lead[:-1] + (lead[-1] * nr1 * nhi * nr2, LANES))
+
+    b_rows, old_rows = rows_view(clique_b), rows_view(old_separator)
+
+    prods, first = [], []
+    for c in range(n_chunks):
+        prod, send = absorb(me, z, clique_a, message_in, c, 1, n_va, n_vb)
+        prods.append(prod)
+        got = swap(send, "va", 1)
+        prod, keep = absorb(me, z, clique_a, message_in, c, 0, n_va, n_vb)
+        prods.append(prod)
+        keep = keep.reshape((2, 2) + keep.shape[1:])
+        got = got.reshape(keep.shape)
+        x0 = keep[:, 1, 0] + got[:, 1, 0]
+        y1 = keep[1, :, 1] + got[1, :, 1]
+        first.append((keep, got, swap(x0, "va", 2), swap(y1, "va", 4)))
+    absorbed = flush(tie(me, x0, y1), prods, clique_a)
+
+    pieces = [[] for _ in range(n_vb)]
+    for keep, got, x0, y1 in first:
+        y0 = keep[1, 0, 0] + got[1, 0, 0] + x0[1]
+        x1 = keep[0, 1, 1] + got[0, 1, 1] + y1[1]
+        k0 = keep[0, 0, 0] + got[0, 0, 0] + x0[0]
+        k1 = keep[0, 0, 1] + got[0, 0, 1] + y1[0]
+        y0_in, x1_in = swap(y0, "va", 4), swap(x1, "va", 2)
+        for m in range(n_vb):
+            pieces[m].append(jnp.stack([k0[m] + y0_in[m], k1[m] + x1_in[m]]))
+    pieces = [jnp.stack(piece) for piece in pieces]
+    seps = [pieces[0]] + [swap(pieces[m], "vb", m) for m in range(1, n_vb)]
+
+    send_order = [(1, 0), (2, 0), (3, 1), (2, 1)]
+    keep_order = [(0, 0), (3, 0), (0, 1), (1, 1)]
+    dims = (nr1, nhi, nr2)
+    held_s, held_k = fetch(tie(z, absorbed, y0, x1), b_rows, (send_order, keep_order), n_vb)
+    updated, send, scale = update(z, held_s, b_rows, send_order, dims, seps=seps, old=old_rows)
+    g0, g1 = swap(send[:2], "vb", 1), swap(send[2:], "vb", 3)
+    updated, keep = update(z, held_k, b_rows, keep_order, dims, scale=scale, before=updated)
+    s0, s1 = keep[1] + g0[1], keep[3] + g1[1]
+    k0, k1 = keep[0] + g0[0], keep[2] + g1[0]
+    s0, s1 = swap(s0, "vb", 3), swap(s1, "vb", 1)
+    onward = jnp.concatenate([k0 + s0, k1 + s1], axis=0)
+
+    e_out = ne // n_vb
+    onward = onward.reshape(e_out, nq, nhi, nr1, LANES)
+    onward = jnp.swapaxes(onward, 2, 3).reshape(e_out, nq, nr1, R3)
+    updated = updated.reshape(ne, npt, nq, nr1, nhi, nr2, LANES)
+    updated = jnp.swapaxes(updated, 4, 5).reshape(clique_b.shape)
+    return (absorbed, updated, onward)
+
+
 def solution(mesh):
+    small = mesh.shape["va"] == 8 and mesh.shape["vb"] == 4
     return jax.shard_map(
-        body,
+        body if small else generic_body,
         mesh=mesh,
         in_specs=(
             P("va", "vb", None, None, None),

time: 156 us -> 76.1 us (0.49)
  waiting for transfers between devices: 79.6 us -> 21.5 us
  other arithmetic: 32.7 us -> 1.4 us
  Pallas kernels: 0 us -> 29.2 us
  starting transfers between devices: 0.08 us -> 22.9 us
  blocking collectives: 18.9 us -> 0 us
  between operations: 14.1 us -> 0.88 us
  local copies, waits for them, and re-layouts: 10.8 us -> 0.05 us
    reduce_scatter x2 -> x0, waiting for transfers between devices: 79.5 us -> none  [the longest x1 54.1 us: body(): lax.psum_scatter(jnp.transpose(summed, (2, 0, 1, 3)), 'va', scatter_dimen...]
    reduce_sum x2 -> x0, other arithmetic: 31.2 us -> none  [the longest x1 18.7 us: body(): partial_value = jnp.sum(updated_b, axis=(1, 4)) * (1.0 / (P_SIZE * R2))]
    pallas_call x0 -> x8, Pallas kernels: none -> 29.2 us  [the longest x4 9.76 us: absorb(): pl.pallas_call(functools.partial(absorb_kernel, chunk, part), in_specs=[p...]
    ppermute x0 -> x17, starting transfers between devices: none -> 22.9 us  [swap(): return lax.ppermute(x, axis, [(i, i ^ mask) for i in range(n)])]
    ppermute x0 -> x17, waiting for transfers between devices: none -> 21.5 us  [swap(): return lax.ppermute(x, axis, [(i, i ^ mask) for i in range(n)])]
    all_to_all x1 -> x0, blocking collectives: 18.9 us -> none  [body(): lax.all_to_all(shares, 'vb', split_axis=3, concat_axis=1, tiled=True)]
    transpose x2 -> x0, local copies, waits for them, and re-layouts: 4.93 us -> none  [body(): jnp.transpose(summed, (2, 0, 1, 3))]
    unnamed x4 -> x2, local copies, waits for them, and re-layouts: 4.29 us -> 0.01 us
  transfers between devices with their start and end apart: 2 -> 17, of which waited for: 2 -> 8; matrix products, arithmetic and copies ran while one was open for 0% -> 1% of each run, Pallas kernels for 0% -> 30%
where the time goes in v2:
time: 76.1 us; the launch traced here: 76 us
  Pallas kernels  29.2 us (38%)
  starting transfers between devices  22.9 us (30%)
  waiting for transfers between devices  21.5 us (28%)
  other arithmetic  1.4 us (2%)
  between operations  0.88 us (1%)
    ppermute x17, starting transfers between devices, swap(): return lax.ppermute(x, axis, [(i, i ^ mask) for i in range(n)])  22.9 us
    ppermute x17, waiting for transfers between devices, swap(): return lax.ppermute(x, axis, [(i, i ^ mask) for i in range(n)])  21.5 us
    pallas_call x4, Pallas kernels, absorb(): pl.pallas_call(functools.partial(absorb_kernel, chunk, part), in_specs=[p...  9.76 us
    pallas_call x2, Pallas kernels, update(): pl.pallas_call(kernel, in_specs=[pl.BlockSpec(memory_space=pltpu.SMEM)] +...  7.54 us
    pallas_call x1, Pallas kernels, fetch(): pl.pallas_call(functools.partial(fetch_kernel, orders), in_specs=[pl.Bloc...  5.97 us
    pallas_call x1, Pallas kernels, flush(): pl.pallas_call(flush_kernel, in_specs=[pl.BlockSpec(memory_space=pltpu.SM...  5.96 us
  transfers between devices with their start and end apart: 17, of which 8 were waited for; matrix products, arithmetic and copies ran while one was open for 1% of the time, Pallas kernels for 30%

profile of v2, /device:TPU:0, one launch (start us, length us, event | category | flops | bytes accessed | tf_op | source)
XLA Modules:
  0.0 76.0 jit_solution(12274074235062897095)
XLA Ops:
  0.6 2.4 %absorb.5 = (f32[4,2,2,2,8,4096]{5,4,3,2,1,0:T(8,128)S(1)}, f32[4,2,4,2,8,512]{5,4,3,2,1,0:T(8,128)S(1)}) custom-call(s32[1]{0:T(128)} %bitcast.me_ref, s32[1]{0:T(128)} %bitcast.1.z_ref, f32[2,2,2,16,32768]{4,3,2,1,0:T(8,128)} %a_hbm.7, f32[2,2,32768]{2,1,0:T(2,128)} %m_hbm.7), custom_call_target="tpu_custom_call" | custom-call | flops 2097152 | bytes 4194304 | tf_op jit(solution)/shard_map/absorb/pallas_call | solution.py:107
  3.6 2.4 %absorb.6 = (f32[4,2,2,2,8,4096]{5,4,3,2,1,0:T(8,128)S(1)}, f32[4,2,4,2,8,512]{5,4,3,2,1,0:T(8,128)S(1)}) custom-call(s32[1]{0:T(128)} %bitcast.me_ref, s32[1]{0:T(128)} %bitcast.1.z_ref, f32[2,2,2,16,32768]{4,3,2,1,0:T(8,128)} %a_hbm.7, f32[2,2,32768]{2,1,0:T(2,128)} %m_hbm.7), custom_call_target="tpu_custom_call" | custom-call | flops 2097152 | bytes 4194304 | tf_op jit(solution)/shard_map/absorb/pallas_call | solution.py:107
  6.2 2.4 %absorb.4 = (f32[4,2,2,2,8,4096]{5,4,3,2,1,0:T(8,128)S(1)}, f32[4,2,4,2,8,512]{5,4,3,2,1,0:T(8,128)S(1)}) custom-call(s32[1]{0:T(128)} %bitcast.me_ref, s32[1]{0:T(128)} %bitcast.1.z_ref, f32[2,2,2,16,32768]{4,3,2,1,0:T(8,128)} %a_hbm.7, f32[2,2,32768]{2,1,0:T(2,128)} %m_hbm.7), custom_call_target="tpu_custom_call" | custom-call | flops 2097152 | bytes 4194304 | tf_op jit(solution)/shard_map/absorb/pallas_call | solution.py:107
  8.6 2.4 %absorb.7 = (f32[4,2,2,2,8,4096]{5,4,3,2,1,0:T(8,128)S(1)}, f32[4,2,4,2,8,512]{5,4,3,2,1,0:T(8,128)S(1)}) custom-call(s32[1]{0:T(128)} %bitcast.me_ref, s32[1]{0:T(128)} %bitcast.1.z_ref, f32[2,2,2,16,32768]{4,3,2,1,0:T(8,128)} %a_hbm.7, f32[2,2,32768]{2,1,0:T(2,128)} %m_hbm.7), custom_call_target="tpu_custom_call" | custom-call | flops 2097152 | bytes 4194304 | tf_op jit(solution)/shard_map/absorb/pallas_call | solution.py:107
  11.1 3.0 %collective-permute-start.1 = (f32[2,4,2,8,512]{4,3,2,1,0:T(8,128)S(1)}, f32[2,4,2,8,512]{4,3,2,1,0:T(8,128)S(1)}, u32[]{:S(2)}, u32[]{:S(2)}) collective-permute-start(f32[2,4,2,8,512]{4,3,2,1,0:T(8,128)S(1)} %fusion.5), channel_id=1, source_target_pairs={{0,8},{4,12},{8,0},{12,4},{16,24},{20,28},{24,16},{28,20},{1,9},{5... | collective-permute-start | bytes 786440 | tf_op jit(solution)/shard_map/ppermute | solution.py:55
  14.2 1.6 %collective-permute-start.2 = (f32[2,4,2,8,512]{4,3,2,1,0:T(8,128)S(1)}, f32[2,4,2,8,512]{4,3,2,1,0:T(8,128)S(1)}, u32[]{:S(2)}, u32[]{:S(2)}) collective-permute-start(f32[2,4,2,8,512]{4,3,2,1,0:T(8,128)S(1)} %fusion.4), channel_id=1, source_target_pairs={{0,16},{4,20},{8,24},{12,28},{16,0},{20,4},{24,8},{28,12},{1,17},{... | collective-permute-start | bytes 786440 | tf_op jit(solution)/shard_map/ppermute | solution.py:55
  16.5 6.0 %flush.1 = f32[2,2,2,16,32768]{4,3,2,1,0:T(8,128)} custom-call(s32[1]{0:T(128)} %bitcast.me_ref, f32[4,2,2,2,8,4096]{5,4,3,2,1,0:T(8,128)S(1)} %get-tuple-element.23.rest_0_, f32[4,2,2,2,8,4096]{5,4,3,2,1,0:T(8,128)S(1)} %get-tuple-element.24.rest_1_, f32[4,2,2,2,8,4096]{5,4,3,2,1,0:T(8,128)S(1)} %get-tuple-element.25.rest_2_, ...), custom_call_target="tpu_custom_call" | custom-call | bytes 16777216 | tf_op jit(solution)/shard_map/flush/pallas_call | solution.py:153
  22.5 1.0 %collective-permute-done.2 = f32[2,4,2,8,512]{4,3,2,1,0:T(8,128)S(1)} collective-permute-done((f32[2,4,2,8,512]{4,3,2,1,0:T(8,128)S(1)}, f32[2,4,2,8,512]{4,3,2,1,0:T(8,128)S(1)}, u32[]{:S(2)}, u32[]{:S(2)}) %collective-permute-start.2) | collective-permute-done | bytes 262176 | tf_op jit(solution)/shard_map/ppermute | solution.py:55
  23.6 1.6 %collective-permute-start.8 = (f32[4,2,8,512]{3,2,1,0:T(8,128)S(1)}, f32[4,2,8,512]{3,2,1,0:T(8,128)S(1)}, u32[]{:S(2)}, u32[]{:S(2)}) collective-permute-start(f32[4,2,8,512]{3,2,1,0:T(8,128)S(1)} %get-tuple-element.42), channel_id=1, source_target_pairs={{0,16},{4,20},{8,24},{12,28},{16,0},{20,4},{24,8},{28,12},{1,17},{... | collective-permute-start | bytes 393224 | tf_op jit(solution)/shard_map/ppermute | solution.py:55
  25.2 1.0 %collective-permute-start.9 = (f32[4,2,8,512]{3,2,1,0:T(8,128)S(1)}, f32[4,2,8,512]{3,2,1,0:T(8,128)S(1)}, u32[]{:S(2)}, u32[]{:S(2)}) collective-permute-start(f32[4,2,8,512]{3,2,1,0:T(8,128)S(1)} %get-tuple-element.47), channel_id=1, source_target_pairs={{0,8},{4,12},{8,0},{12,4},{16,24},{20,28},{24,16},{28,20},{1,9},{5... | collective-permute-start | bytes 393224 | tf_op jit(solution)/shard_map/ppermute | solution.py:55
  26.5 2.5 %collective-permute-done.6 = f32[2,4,2,8,512]{4,3,2,1,0:T(8,128)S(1)} collective-permute-done((f32[2,4,2,8,512]{4,3,2,1,0:T(8,128)S(1)}, f32[2,4,2,8,512]{4,3,2,1,0:T(8,128)S(1)}, u32[]{:S(2)}, u32[]{:S(2)}) %collective-permute-start.6) | collective-permute-done | bytes 262176 | tf_op jit(solution)/shard_map/ppermute | solution.py:55
  29.2 1.6 %collective-permute-start.5 = (f32[4,2,8,512]{3,2,1,0:T(8,128)S(1)}, f32[4,2,8,512]{3,2,1,0:T(8,128)S(1)}, u32[]{:S(2)}, u32[]{:S(2)}) collective-permute-start(f32[4,2,8,512]{3,2,1,0:T(8,128)S(1)} %get-tuple-element.38), channel_id=1, source_target_pairs={{0,16},{4,20},{8,24},{12,28},{16,0},{20,4},{24,8},{28,12},{1,17},{... | collective-permute-start | bytes 393224 | tf_op jit(solution)/shard_map/ppermute | solution.py:55
  31.3 6.0 %fetch.1 = (f32[4,4,8,128,128]{4,3,2,1,0:T(8,128)S(1)}, f32[4,4,8,128,128]{4,3,2,1,0:T(8,128)S(1)}) custom-call(s32[1]{0:T(128)} %bitcast.1.z_ref, f32[32,8,128,128]{3,2,1,0:T(8,128)} %bitcast.153), custom_call_target="tpu_custom_call" | custom-call | bytes 16777216 | tf_op jit(solution)/shard_map/fetch/pallas_call | solution.py:182
  37.5 1.6 %collective-permute-start.10 = (f32[2,2,2,8,512]{4,3,2,1,0:T(8,128)S(1)}, f32[2,2,2,8,512]{4,3,2,1,0:T(8,128)S(1)}, u32[]{:S(2)}, u32[]{:S(2)}) collective-permute-start(f32[2,2,2,8,512]{4,3,2,1,0:T(8,128)S(1)} %pad_maximum_fusion.2), channel_id=1, source_target_pairs={{0,1},{1,0},{2,3},{3,2},{4,5},{5,4},{6,7},{7,6},{8,9},{9,8},{10,11... | collective-permute-start | bytes 393224 | tf_op jit(solution)/shard_map/ppermute | solution.py:55
  39.2 2.7 %collective-permute-start.11 = (f32[2,2,2,8,512]{4,3,2,1,0:T(8,128)S(1)}, f32[2,2,2,8,512]{4,3,2,1,0:T(8,128)S(1)}, u32[]{:S(2)}, u32[]{:S(2)}) collective-permute-start(f32[2,2,2,8,512]{4,3,2,1,0:T(8,128)S(1)} %pad_maximum_fusion.3), channel_id=1, source_target_pairs={{0,2},{1,3},{2,0},{3,1},{4,6},{5,7},{6,4},{7,5},{8,10},{9,11},{10,... | collective-permute-start | bytes 393224 | tf_op jit(solution)/shard_map/ppermute | solution.py:55
  43.0 6.4 %collective-permute-done.11.rest_2_ = f32[2,2,2,8,512]{4,3,2,1,0:T(8,128)S(1)} collective-permute-done((f32[2,2,2,8,512]{4,3,2,1,0:T(8,128)S(1)}, f32[2,2,2,8,512]{4,3,2,1,0:T(8,128)S(1)}, u32[]{:S(2)}, u32[]{:S(2)}) %collective-permute-start.11) | collective-permute-done | bytes 131104 | tf_op jit(solution)/shard_map/ppermute | solution.py:55
  49.3 3.8 %update.2 = (f32[32,8,128,128]{3,2,1,0:T(8,128)}, f32[4,4,64,128]{3,2,1,0:T(8,128)S(1)}, f32[8,128,128]{2,1,0:T(8,128)S(1)}) custom-call(s32[1]{0:T(128)} %bitcast.1.z_ref, f32[4,4,8,128,128]{4,3,2,1,0:T(8,128)S(1)} %get-tuple-element.29.held, f32[8,128,128]{2,1,0:T(8,128)S(1)} %bitcast.152, f32[2,2,2,8,512]{4,3,2,1,0:T(8,128)S(1)} %pad_maximum_fusion.1.rest_0_, ...), custom_call_target="tpu_custom_call" | custom-call | flops 4194304 | bytes 8388608 | tf_op jit(solution)/shard_map/update/pallas_call | solution.py:281
  53.2 2.0 %collective-permute-start.13 = (f32[2,4,64,128]{3,2,1,0:T(8,128)S(1)}, f32[2,4,64,128]{3,2,1,0:T(8,128)S(1)}, u32[]{:S(2)}, u32[]{:S(2)}) collective-permute-start(f32[2,4,64,128]{3,2,1,0:T(8,128)S(1)} %get-tuple-element.53), channel_id=1, source_target_pairs={{0,1},{1,0},{2,3},{3,2},{4,5},{5,4},{6,7},{7,6},{8,9},{9,8},{10,11... | collective-permute-start | bytes 786440 | tf_op jit(solution)/shard_map/ppermute | solution.py:55
  55.3 2.5 %collective-permute-start.15 = (f32[2,4,64,128]{3,2,1,0:T(8,128)S(1)}, f32[2,4,64,128]{3,2,1,0:T(8,128)S(1)}, u32[]{:S(2)}, u32[]{:S(2)}) collective-permute-start(f32[2,4,64,128]{3,2,1,0:T(8,128)S(1)} %get-tuple-element.54), channel_id=1, source_target_pairs={{0,3},{1,2},{2,1},{3,0},{4,7},{5,6},{6,5},{7,4},{8,11},{9,10},{10,... | collective-permute-start | bytes 786440 | tf_op jit(solution)/shard_map/ppermute | solution.py:55
  57.8 3.7 %update.3 = (f32[32,8,128,128]{3,2,1,0:T(8,128)}, f32[4,4,64,128]{3,2,1,0:T(8,128)S(1)}) custom-call(s32[1]{0:T(128)} %bitcast.1.z_ref, f32[4,4,8,128,128]{4,3,2,1,0:T(8,128)S(1)} %get-tuple-element.28.held, f32[8,128,128]{2,1,0:T(8,128)S(1)} %get-tuple-element.32.scale, f32[32,8,128,128]{3,2,1,0:T(8,128)} %get-tuple-element.33.before), custom_call_target="tpu_custom_call", output_to_operand_aliasing={{0}: (3, {})} | custom-call | flops 4194304 | bytes 8388608 | tf_op jit(solution)/shard_map/update/pallas_call | solution.py:281
  61.5 6.1 %collective-permute-done.15 = f32[2,4,64,128]{3,2,1,0:T(8,128)S(1)} collective-permute-done((f32[2,4,64,128]{3,2,1,0:T(8,128)S(1)}, f32[2,4,64,128]{3,2,1,0:T(8,128)S(1)}, u32[]{:S(2)}, u32[]{:S(2)}) %collective-permute-start.15) | collective-permute-done | bytes 262176 | tf_op jit(solution)/shard_map/ppermute | solution.py:55
  67.7 0.8 %collective-permute-start.14 = (f32[4,64,128]{2,1,0:T(8,128)S(1)}, f32[4,64,128]{2,1,0:T(8,128)S(1)}, u32[]{:S(2)}, u32[]{:S(2)}) collective-permute-start(f32[4,64,128]{2,1,0:T(8,128)S(1)} %get-tuple-element.51), channel_id=1, source_target_pairs={{0,3},{1,2},{2,1},{3,0},{4,7},{5,6},{6,5},{7,4},{8,11},{9,10},{10,... | collective-permute-start | bytes 393224 | tf_op jit(solution)/shard_map/ppermute | solution.py:55
  68.5 2.4 %collective-permute-start.16 = (f32[4,64,128]{2,1,0:T(8,128)S(1)}, f32[4,64,128]{2,1,0:T(8,128)S(1)}, u32[]{:S(2)}, u32[]{:S(2)}) collective-permute-start(f32[4,64,128]{2,1,0:T(8,128)S(1)} %get-tuple-element.52), channel_id=1, source_target_pairs={{0,1},{1,0},{2,3},{3,2},{4,5},{5,4},{6,7},{7,6},{8,9},{9,8},{10,11... | collective-permute-start | bytes 393224 | tf_op jit(solution)/shard_map/ppermute | solution.py:55
  70.9 3.8 %collective-permute-done.14 = f32[4,64,128]{2,1,0:T(8,128)S(1)} collective-permute-done((f32[4,64,128]{2,1,0:T(8,128)S(1)}, f32[4,64,128]{2,1,0:T(8,128)S(1)}, u32[]{:S(2)}, u32[]{:S(2)}) %collective-permute-start.14) | collective-permute-done | bytes 131104 | tf_op jit(solution)/shard_map/ppermute | solution.py:55
  (42 shorter events, 5.3 us)
Async XLA Ops:
  3.1 8.0 %collective-permute-start = (f32[4,2,4,2,8,512]{5,4,3,2,1,0:T(8,128)S(1)}, f32[4,2,4,2,8,512]{5,4,3,2,1,0:T(8,128)S(1)}, u32[]{:S(2)}, u32[]{:S(2)}) collective-permute-start(f32[4,2,4,2,8,512]{5,4,3,2,1,0:T(8,128)S(1)} %get-tuple-element.21), channel_id=1, source_target_pairs={{0,4},{4,0},{8,12},{12,8},{16,20},{20,16},{24,28},{28,24},{1,5},{5... | collective-permute-start | bytes 3145736 | tf_op jit(solution)/shard_map/ppermute | solution.py:55
  6.0 9.7 %collective-permute-start.3 = (f32[4,2,4,2,8,512]{5,4,3,2,1,0:T(8,128)S(1)}, f32[4,2,4,2,8,512]{5,4,3,2,1,0:T(8,128)S(1)}, u32[]{:S(2)}, u32[]{:S(2)}) collective-permute-start(f32[4,2,4,2,8,512]{5,4,3,2,1,0:T(8,128)S(1)} %get-tuple-element.31), channel_id=1, source_target_pairs={{0,4},{4,0},{8,12},{12,8},{16,20},{20,16},{24,28},{28,24},{1,5},{5... | collective-permute-start | bytes 3145736 | tf_op jit(solution)/shard_map/ppermute | solution.py:55
  11.1 11.3 %collective-permute-start.1 = (f32[2,4,2,8,512]{4,3,2,1,0:T(8,128)S(1)}, f32[2,4,2,8,512]{4,3,2,1,0:T(8,128)S(1)}, u32[]{:S(2)}, u32[]{:S(2)}) collective-permute-start(f32[2,4,2,8,512]{4,3,2,1,0:T(8,128)S(1)} %fusion.5), channel_id=1, source_target_pairs={{0,8},{4,12},{8,0},{12,4},{16,24},{20,28},{24,16},{28,20},{1,9},{5... | collective-permute-start | bytes 786440 | tf_op jit(solution)/shard_map/ppermute | solution.py:55
  14.2 9.3 %collective-permute-start.2 = (f32[2,4,2,8,512]{4,3,2,1,0:T(8,128)S(1)}, f32[2,4,2,8,512]{4,3,2,1,0:T(8,128)S(1)}, u32[]{:S(2)}, u32[]{:S(2)}) collective-permute-start(f32[2,4,2,8,512]{4,3,2,1,0:T(8,128)S(1)} %fusion.4), channel_id=1, source_target_pairs={{0,16},{4,20},{8,24},{12,28},{16,0},{20,4},{24,8},{28,12},{1,17},{... | collective-permute-start | bytes 786440 | tf_op jit(solution)/shard_map/ppermute | solution.py:55
  15.8 10.7 %collective-permute-start.4 = (f32[2,4,2,8,512]{4,3,2,1,0:T(8,128)S(1)}, f32[2,4,2,8,512]{4,3,2,1,0:T(8,128)S(1)}, u32[]{:S(2)}, u32[]{:S(2)}) collective-permute-start(f32[2,4,2,8,512]{4,3,2,1,0:T(8,128)S(1)} %fusion.2), channel_id=1, source_target_pairs={{0,8},{4,12},{8,0},{12,4},{16,24},{20,28},{24,16},{28,20},{1,9},{5... | collective-permute-start | bytes 786440 | tf_op jit(solution)/shard_map/ppermute | solution.py:55
  16.4 12.6 %collective-permute-start.6 = (f32[2,4,2,8,512]{4,3,2,1,0:T(8,128)S(1)}, f32[2,4,2,8,512]{4,3,2,1,0:T(8,128)S(1)}, u32[]{:S(2)}, u32[]{:S(2)}) collective-permute-start(f32[2,4,2,8,512]{4,3,2,1,0:T(8,128)S(1)} %fusion), channel_id=1, source_target_pairs={{0,16},{4,20},{8,24},{12,28},{16,0},{20,4},{24,8},{28,12},{1,17},{... | collective-permute-start | bytes 786440 | tf_op jit(solution)/shard_map/ppermute | solution.py:55
  23.6 13.7 %collective-permute-start.8 = (f32[4,2,8,512]{3,2,1,0:T(8,128)S(1)}, f32[4,2,8,512]{3,2,1,0:T(8,128)S(1)}, u32[]{:S(2)}, u32[]{:S(2)}) collective-permute-start(f32[4,2,8,512]{3,2,1,0:T(8,128)S(1)} %get-tuple-element.42), channel_id=1, source_target_pairs={{0,16},{4,20},{8,24},{12,28},{16,0},{20,4},{24,8},{28,12},{1,17},{... | collective-permute-start | bytes 393224 | tf_op jit(solution)/shard_map/ppermute | solution.py:55
  25.2 12.2 %collective-permute-start.9 = (f32[4,2,8,512]{3,2,1,0:T(8,128)S(1)}, f32[4,2,8,512]{3,2,1,0:T(8,128)S(1)}, u32[]{:S(2)}, u32[]{:S(2)}) collective-permute-start(f32[4,2,8,512]{3,2,1,0:T(8,128)S(1)} %get-tuple-element.47), channel_id=1, source_target_pairs={{0,8},{4,12},{8,0},{12,4},{16,24},{20,28},{24,16},{28,20},{1,9},{5... | collective-permute-start | bytes 393224 | tf_op jit(solution)/shard_map/ppermute | solution.py:55
  29.2 8.2 %collective-permute-start.5 = (f32[4,2,8,512]{3,2,1,0:T(8,128)S(1)}, f32[4,2,8,512]{3,2,1,0:T(8,128)S(1)}, u32[]{:S(2)}, u32[]{:S(2)}) collective-permute-start(f32[4,2,8,512]{3,2,1,0:T(8,128)S(1)} %get-tuple-element.38), channel_id=1, source_target_pairs={{0,16},{4,20},{8,24},{12,28},{16,0},{20,4},{24,8},{28,12},{1,17},{... | collective-permute-start | bytes 393224 | tf_op jit(solution)/shard_map/ppermute | solution.py:55
  30.8 6.6 %collective-permute-start.7 = (f32[4,2,8,512]{3,2,1,0:T(8,128)S(1)}, f32[4,2,8,512]{3,2,1,0:T(8,128)S(1)}, u32[]{:S(2)}, u32[]{:S(2)}) collective-permute-start(f32[4,2,8,512]{3,2,1,0:T(8,128)S(1)} %get-tuple-element.45), channel_id=1, source_target_pairs={{0,8},{4,12},{8,0},{12,4},{16,24},{20,28},{24,16},{28,20},{1,9},{5... | collective-permute-start | bytes 393224 | tf_op jit(solution)/shard_map/ppermute | solution.py:55
  31.3 18.0 %copy-start = (f32[8,16,2,2,256]{4,3,2,1,0:T(2,128)S(1)}, f32[8,16,2,2,256]{4,3,2,1,0:T(2,128)}, u32[]{:S(2)}) copy-start(f32[8,16,2,2,256]{4,3,2,1,0:T(2,128)} %param.7) | copy-start | bytes 1572868
  37.5 5.5 %collective-permute-start.10 = (f32[2,2,2,8,512]{4,3,2,1,0:T(8,128)S(1)}, f32[2,2,2,8,512]{4,3,2,1,0:T(8,128)S(1)}, u32[]{:S(2)}, u32[]{:S(2)}) collective-permute-start(f32[2,2,2,8,512]{4,3,2,1,0:T(8,128)S(1)} %pad_maximum_fusion.2), channel_id=1, source_target_pairs={{0,1},{1,0},{2,3},{3,2},{4,5},{5,4},{6,7},{7,6},{8,9},{9,8},{10,11... | collective-permute-start | bytes 393224 | tf_op jit(solution)/shard_map/ppermute | solution.py:55
  39.2 10.2 %collective-permute-start.11 = (f32[2,2,2,8,512]{4,3,2,1,0:T(8,128)S(1)}, f32[2,2,2,8,512]{4,3,2,1,0:T(8,128)S(1)}, u32[]{:S(2)}, u32[]{:S(2)}) collective-permute-start(f32[2,2,2,8,512]{4,3,2,1,0:T(8,128)S(1)} %pad_maximum_fusion.3), channel_id=1, source_target_pairs={{0,2},{1,3},{2,0},{3,1},{4,6},{5,7},{6,4},{7,5},{8,10},{9,11},{10,... | collective-permute-start | bytes 393224 | tf_op jit(solution)/shard_map/ppermute | solution.py:55
  41.9 7.5 %collective-permute-start.12 = (f32[2,2,2,8,512]{4,3,2,1,0:T(8,128)S(1)}, f32[2,2,2,8,512]{4,3,2,1,0:T(8,128)S(1)}, u32[]{:S(2)}, u32[]{:S(2)}) collective-permute-start(f32[2,2,2,8,512]{4,3,2,1,0:T(8,128)S(1)} %pad_maximum_fusion.4), channel_id=1, source_target_pairs={{0,3},{1,2},{2,1},{3,0},{4,7},{5,6},{6,5},{7,4},{8,11},{9,10},{10,... | collective-permute-start | bytes 393224 | tf_op jit(solution)/shard_map/ppermute | solution.py:55
  53.2 8.2 %collective-permute-start.13 = (f32[2,4,64,128]{3,2,1,0:T(8,128)S(1)}, f32[2,4,64,128]{3,2,1,0:T(8,128)S(1)}, u32[]{:S(2)}, u32[]{:S(2)}) collective-permute-start(f32[2,4,64,128]{3,2,1,0:T(8,128)S(1)} %get-tuple-element.53), channel_id=1, source_target_pairs={{0,1},{1,0},{2,3},{3,2},{4,5},{5,4},{6,7},{7,6},{8,9},{9,8},{10,11... | collective-permute-start | bytes 786440 | tf_op jit(solution)/shard_map/ppermute | solution.py:55
  55.3 12.4 %collective-permute-start.15 = (f32[2,4,64,128]{3,2,1,0:T(8,128)S(1)}, f32[2,4,64,128]{3,2,1,0:T(8,128)S(1)}, u32[]{:S(2)}, u32[]{:S(2)}) collective-permute-start(f32[2,4,64,128]{3,2,1,0:T(8,128)S(1)} %get-tuple-element.54), channel_id=1, source_target_pairs={{0,3},{1,2},{2,1},{3,0},{4,7},{5,6},{6,5},{7,4},{8,11},{9,10},{10,... | collective-permute-start | bytes 786440 | tf_op jit(solution)/shard_map/ppermute | solution.py:55
  67.7 7.0 %collective-permute-start.14 = (f32[4,64,128]{2,1,0:T(8,128)S(1)}, f32[4,64,128]{2,1,0:T(8,128)S(1)}, u32[]{:S(2)}, u32[]{:S(2)}) collective-permute-start(f32[4,64,128]{2,1,0:T(8,128)S(1)} %get-tuple-element.51), channel_id=1, source_target_pairs={{0,3},{1,2},{2,1},{3,0},{4,7},{5,6},{6,5},{7,4},{8,11},{9,10},{10,... | collective-permute-start | bytes 393224 | tf_op jit(solution)/shard_map/ppermute | solution.py:55
  68.5 6.8 %collective-permute-start.16 = (f32[4,64,128]{2,1,0:T(8,128)S(1)}, f32[4,64,128]{2,1,0:T(8,128)S(1)}, u32[]{:S(2)}, u32[]{:S(2)}) collective-permute-start(f32[4,64,128]{2,1,0:T(8,128)S(1)} %get-tuple-element.52), channel_id=1, source_target_pairs={{0,1},{1,0},{2,3},{3,2},{4,5},{5,4},{6,7},{7,6},{8,9},{9,8},{10,11... | collective-permute-start | bytes 393224 | tf_op jit(solution)/shard_map/ppermute | solution.py:55

commit v3 on v2

--- a/solution.py
+++ b/solution.py
@@ -316,22 +316,25 @@
 
     b_rows, old_rows = rows_view(clique_b), rows_view(old_separator)
 
-    prods, first = [], []
+    prods, first, ready = [], [], me
     for c in range(n_chunks):
-        prod, send = absorb(me, z, clique_a, message_in, c, 1, n_va, n_vb)
+        prod, send = absorb(ready, z, clique_a, message_in, c, 1, n_va, n_vb)
         prods.append(prod)
         got = swap(send, "va", 1)
-        prod, keep = absorb(me, z, clique_a, message_in, c, 0, n_va, n_vb)
+        prod, keep = absorb(tie(ready, send), z, clique_a, message_in, c, 0, n_va, n_vb)
         prods.append(prod)
         keep = keep.reshape((2, 2) + keep.shape[1:])
         got = got.reshape(keep.shape)
         x0 = keep[:, 1, 0] + got[:, 1, 0]
         y1 = keep[1, :, 1] + got[1, :, 1]
+        ready = tie(me, x0, y1)
         first.append((keep, got, swap(x0, "va", 2), swap(y1, "va", 4)))
-    absorbed = flush(tie(me, x0, y1), prods, clique_a)
+
+    absorbed = flush(ready, prods, clique_a)
 
     pieces = [[] for _ in range(n_vb)]
     for keep, got, x0, y1 in first:
+        x0, y1 = tie(x0, ready), tie(y1, ready)
         y0 = keep[1, 0, 0] + got[1, 0, 0] + x0[1]
         x1 = keep[0, 1, 1] + got[0, 1, 1] + y1[1]
         k0 = keep[0, 0, 0] + got[0, 0, 0] + x0[0]
@@ -342,17 +345,19 @@
     pieces = [jnp.stack(piece) for piece in pieces]
     seps = [pieces[0]] + [swap(pieces[m], "vb", m) for m in range(1, n_vb)]
 
-    send_order = [(1, 0), (2, 0), (3, 1), (2, 1)]
-    keep_order = [(0, 0), (3, 0), (0, 1), (1, 1)]
+    through, direct = [(2, 0), (2, 1)], [(1, 0), (3, 1)]
+    forward, own = [(3, 0), (1, 1)], [(0, 0), (0, 1)]
     dims = (nr1, nhi, nr2)
-    held_s, held_k = fetch(tie(z, absorbed, y0, x1), b_rows, (send_order, keep_order), n_vb)
-    updated, send, scale = update(z, held_s, b_rows, send_order, dims, seps=seps, old=old_rows)
-    g0, g1 = swap(send[:2], "vb", 1), swap(send[2:], "vb", 3)
-    updated, keep = update(z, held_k, b_rows, keep_order, dims, scale=scale, before=updated)
-    s0, s1 = keep[1] + g0[1], keep[3] + g1[1]
-    k0, k1 = keep[0] + g0[0], keep[2] + g1[0]
-    s0, s1 = swap(s0, "vb", 3), swap(s1, "vb", 1)
-    onward = jnp.concatenate([k0 + s0, k1 + s1], axis=0)
+    held_t, held_d = fetch(tie(z, absorbed, y0, x1), b_rows, (through, direct), n_vb)
+    held_f, held_o = fetch(tie(z, held_d, *pieces[1:]), b_rows, (forward, own), n_vb)
+    updated, sent, scale = update(z, held_t, b_rows, through, dims, seps=seps, old=old_rows)
+    t0, t1 = swap(sent[0], "vb", 1), swap(sent[1], "vb", 3)
+    updated, sent = update(z, held_d, b_rows, direct, dims, scale=scale, before=updated)
+    d0, d1 = swap(sent[0], "vb", 1), swap(sent[1], "vb", 3)
+    updated, kept = update(z, held_f, b_rows, forward, dims, scale=scale, before=updated)
+    s0, s1 = swap(kept[0] + t0, "vb", 3), swap(kept[1] + t1, "vb", 1)
+    updated, kept = update(z, held_o, b_rows, own, dims, scale=scale, before=updated)
+    onward = jnp.concatenate([kept[0] + d0 + s0, kept[1] + d1 + s1], axis=0)
 
     e_out = ne // n_vb
     onward = onward.reshape(e_out, nq, nhi, nr1, LANES)

time: 76.1 us -> 71.5 us (0.940)
  waiting for transfers between devices: 21.5 us -> 13 us
  Pallas kernels: 29.2 us -> 32.3 us
    ppermute x17 -> x19, waiting for transfers between devices: 21.5 us -> 13 us  [swap(): return lax.ppermute(x, axis, [(i, i ^ mask) for i in range(n)])]
    pallas_call x2 -> x4, Pallas kernels: 7.54 us -> 9.56 us  [update(): pl.pallas_call(kernel, in_specs=[pl.BlockSpec(memory_space=pltpu.SMEM)] +...]
    pallas_call x1 -> x2, Pallas kernels: 5.97 us -> 7.05 us  [fetch(): pl.pallas_call(functools.partial(fetch_kernel, orders), in_specs=[pl.Bloc...]
    ppermute x17 -> x19, starting transfers between devices: 22.9 us -> 23.6 us  [swap(): return lax.ppermute(x, axis, [(i, i ^ mask) for i in range(n)])]
  transfers between devices with their start and end apart: 17 -> 19, of which waited for: 8 -> 8; matrix products, arithmetic and copies ran while one was open for 1% -> 1% of each run, Pallas kernels for 30% -> 35%
where the time goes in v3:
time: 71.5 us; the launch traced here: 71.4 us
  Pallas kernels  32.3 us (45%)
  starting transfers between devices  23.6 us (33%)
  waiting for transfers between devices  13 us (18%)
  other arithmetic  1.41 us (2%)
  between operations  0.97 us (1%)
    ppermute x19, starting transfers between devices, swap(): return lax.ppermute(x, axis, [(i, i ^ mask) for i in range(n)])  23.6 us
    ppermute x19, waiting for transfers between devices, swap(): return lax.ppermute(x, axis, [(i, i ^ mask) for i in range(n)])  13 us
    pallas_call x4, Pallas kernels, absorb(): pl.pallas_call(functools.partial(absorb_kernel, chunk, part), in_specs=[p...  9.76 us
    pallas_call x4, Pallas kernels, update(): pl.pallas_call(kernel, in_specs=[pl.BlockSpec(memory_space=pltpu.SMEM)] +...  9.56 us
    pallas_call x2, Pallas kernels, fetch(): pl.pallas_call(functools.partial(fetch_kernel, orders), in_specs=[pl.Bloc...  7.05 us
    pallas_call x1, Pallas kernels, flush(): pl.pallas_call(flush_kernel, in_specs=[pl.BlockSpec(memory_space=pltpu.SM...  5.96 us
  transfers between devices with their start and end apart: 19, of which 8 were waited for; matrix products, arithmetic and copies ran while one was open for 1% of the time, Pallas kernels for 35%

profile of v3, /device:TPU:0, one launch (start us, length us, event | category | flops | bytes accessed | tf_op | source)
XLA Modules:
  0.0 71.4 jit_solution(1105320357167454922)
XLA Ops:
  0.6 2.4 %absorb.4 = (f32[4,2,2,2,8,4096]{5,4,3,2,1,0:T(8,128)S(1)}, f32[4,2,4,2,8,512]{5,4,3,2,1,0:T(8,128)S(1)}) custom-call(s32[1]{0:T(128)} %bitcast.me_ref, s32[1]{0:T(128)} %bitcast.1.z_ref, f32[2,2,2,16,32768]{4,3,2,1,0:T(8,128)} %a_hbm.7, f32[2,2,32768]{2,1,0:T(2,128)} %m_hbm.7), custom_call_target="tpu_custom_call" | custom-call | flops 2097152 | bytes 4194304 | tf_op jit(solution)/shard_map/absorb/pallas_call | solution.py:107
  3.6 2.4 %absorb.5 = (f32[4,2,2,2,8,4096]{5,4,3,2,1,0:T(8,128)S(1)}, f32[4,2,4,2,8,512]{5,4,3,2,1,0:T(8,128)S(1)}) custom-call(s32[1]{0:T(128)} %bitcast.me_ref, s32[1]{0:T(128)} %bitcast.1.z_ref, f32[2,2,2,16,32768]{4,3,2,1,0:T(8,128)} %a_hbm.7, f32[2,2,32768]{2,1,0:T(2,128)} %m_hbm.7), custom_call_target="tpu_custom_call" | custom-call | flops 2097152 | bytes 4194304 | tf_op jit(solution)/shard_map/absorb/pallas_call | solution.py:107
  6.1 2.4 %absorb.6 = (f32[4,2,2,2,8,4096]{5,4,3,2,1,0:T(8,128)S(1)}, f32[4,2,4,2,8,512]{5,4,3,2,1,0:T(8,128)S(1)}) custom-call(s32[1]{0:T(128)} %bitcast.me_ref, s32[1]{0:T(128)} %bitcast.1.z_ref, f32[2,2,2,16,32768]{4,3,2,1,0:T(8,128)} %a_hbm.7, f32[2,2,32768]{2,1,0:T(2,128)} %m_hbm.7), custom_call_target="tpu_custom_call" | custom-call | flops 2097152 | bytes 4194304 | tf_op jit(solution)/shard_map/absorb/pallas_call | solution.py:107
  8.9 2.8 %collective-permute-start.6 = (f32[2,4,2,8,512]{4,3,2,1,0:T(8,128)S(1)}, f32[2,4,2,8,512]{4,3,2,1,0:T(8,128)S(1)}, u32[]{:S(2)}, u32[]{:S(2)}) collective-permute-start(f32[2,4,2,8,512]{4,3,2,1,0:T(8,128)S(1)} %fusion.3), channel_id=1, source_target_pairs={{0,16},{4,20},{8,24},{12,28},{16,0},{20,4},{24,8},{28,12},{1,17},{... | collective-permute-start | bytes 786440 | tf_op jit(solution)/shard_map/ppermute | solution.py:55
  11.7 1.5 %collective-permute-start.4 = (f32[2,4,2,8,512]{4,3,2,1,0:T(8,128)S(1)}, f32[2,4,2,8,512]{4,3,2,1,0:T(8,128)S(1)}, u32[]{:S(2)}, u32[]{:S(2)}) collective-permute-start(f32[2,4,2,8,512]{4,3,2,1,0:T(8,128)S(1)} %fusion.5), channel_id=1, source_target_pairs={{0,8},{4,12},{8,0},{12,4},{16,24},{20,28},{24,16},{28,20},{1,9},{5... | collective-permute-start | bytes 786440 | tf_op jit(solution)/shard_map/ppermute | solution.py:55
  13.2 2.4 %absorb.7 = (f32[4,2,2,2,8,4096]{5,4,3,2,1,0:T(8,128)S(1)}, f32[4,2,4,2,8,512]{5,4,3,2,1,0:T(8,128)S(1)}) custom-call(s32[1]{0:T(128)} %bitcast.me_ref, s32[1]{0:T(128)} %bitcast.1.z_ref, f32[2,2,2,16,32768]{4,3,2,1,0:T(8,128)} %a_hbm.7, f32[2,2,32768]{2,1,0:T(2,128)} %m_hbm.7), custom_call_target="tpu_custom_call" | custom-call | flops 2097152 | bytes 4194304 | tf_op jit(solution)/shard_map/absorb/pallas_call | solution.py:107
  15.7 2.6 %collective-permute-done.6 = f32[2,4,2,8,512]{4,3,2,1,0:T(8,128)S(1)} collective-permute-done((f32[2,4,2,8,512]{4,3,2,1,0:T(8,128)S(1)}, f32[2,4,2,8,512]{4,3,2,1,0:T(8,128)S(1)}, u32[]{:S(2)}, u32[]{:S(2)}) %collective-permute-start.6) | collective-permute-done | bytes 262176 | tf_op jit(solution)/shard_map/ppermute | solution.py:55
  18.4 1.5 %collective-permute-done.4 = f32[2,4,2,8,512]{4,3,2,1,0:T(8,128)S(1)} collective-permute-done((f32[2,4,2,8,512]{4,3,2,1,0:T(8,128)S(1)}, f32[2,4,2,8,512]{4,3,2,1,0:T(8,128)S(1)}, u32[]{:S(2)}, u32[]{:S(2)}) %collective-permute-start.4) | collective-permute-done | bytes 262176 | tf_op jit(solution)/shard_map/ppermute | solution.py:55
  20.3 1.7 %collective-permute-start.3 = (f32[2,4,2,8,512]{4,3,2,1,0:T(8,128)S(1)}, f32[2,4,2,8,512]{4,3,2,1,0:T(8,128)S(1)}, u32[]{:S(2)}, u32[]{:S(2)}) collective-permute-start(f32[2,4,2,8,512]{4,3,2,1,0:T(8,128)S(1)} %fusion.1), channel_id=1, source_target_pairs={{0,16},{4,20},{8,24},{12,28},{16,0},{20,4},{24,8},{28,12},{1,17},{... | collective-permute-start | bytes 786440 | tf_op jit(solution)/shard_map/ppermute | solution.py:55
  22.1 1.5 %collective-permute-start.2 = (f32[2,4,2,8,512]{4,3,2,1,0:T(8,128)S(1)}, f32[2,4,2,8,512]{4,3,2,1,0:T(8,128)S(1)}, u32[]{:S(2)}, u32[]{:S(2)}) collective-permute-start(f32[2,4,2,8,512]{4,3,2,1,0:T(8,128)S(1)} %fusion.2), channel_id=1, source_target_pairs={{0,8},{4,12},{8,0},{12,4},{16,24},{20,28},{24,16},{28,20},{1,9},{5... | collective-permute-start | bytes 786440 | tf_op jit(solution)/shard_map/ppermute | solution.py:55
  24.1 6.0 %flush.1 = f32[2,2,2,16,32768]{4,3,2,1,0:T(8,128)} custom-call(s32[1]{0:T(128)} %bitcast.me_ref, f32[4,2,2,2,8,4096]{5,4,3,2,1,0:T(8,128)S(1)} %get-tuple-element.42.rest_0_, f32[4,2,2,2,8,4096]{5,4,3,2,1,0:T(8,128)S(1)} %get-tuple-element.43.rest_1_, f32[4,2,2,2,8,4096]{5,4,3,2,1,0:T(8,128)S(1)} %get-tuple-element.44.rest_2_, ...), custom_call_target="tpu_custom_call" | custom-call | bytes 16777216 | tf_op jit(solution)/shard_map/flush/pallas_call | solution.py:153
  31.6 1.6 %collective-permute-start.9 = (f32[4,2,8,512]{3,2,1,0:T(8,128)S(1)}, f32[4,2,8,512]{3,2,1,0:T(8,128)S(1)}, u32[]{:S(2)}, u32[]{:S(2)}) collective-permute-start(f32[4,2,8,512]{3,2,1,0:T(8,128)S(1)} %get-tuple-element.75), channel_id=1, source_target_pairs={{0,8},{4,12},{8,0},{12,4},{16,24},{20,28},{24,16},{28,20},{1,9},{5... | collective-permute-start | bytes 393224 | tf_op jit(solution)/shard_map/ppermute | solution.py:55
  33.2 3.5 %fetch.2 = (f32[2,4,8,128,128]{4,3,2,1,0:T(8,128)S(1)}, f32[2,4,8,128,128]{4,3,2,1,0:T(8,128)S(1)}) custom-call(s32[1]{0:T(128)} %bitcast.1.z_ref, f32[32,8,128,128]{3,2,1,0:T(8,128)} %bitcast.146), custom_call_target="tpu_custom_call" | custom-call | bytes 16777216 | tf_op jit(solution)/shard_map/fetch/pallas_call | solution.py:182
  36.8 3.7 %collective-permute-start.12 = (f32[2,2,2,8,512]{4,3,2,1,0:T(8,128)S(1)}, f32[2,2,2,8,512]{4,3,2,1,0:T(8,128)S(1)}, u32[]{:S(2)}, u32[]{:S(2)}) collective-permute-start(f32[2,2,2,8,512]{4,3,2,1,0:T(8,128)S(1)} %pad_maximum_fusion.3), channel_id=1, source_target_pairs={{0,3},{1,2},{2,1},{3,0},{4,7},{5,6},{6,5},{7,4},{8,11},{9,10},{10,... | collective-permute-start | bytes 393224 | tf_op jit(solution)/shard_map/ppermute | solution.py:55
  41.5 3.6 %fetch.3 = (f32[2,4,8,128,128]{4,3,2,1,0:T(8,128)S(1)}, f32[2,4,8,128,128]{4,3,2,1,0:T(8,128)S(1)}) custom-call(s32[1]{0:T(128)} %bitcast.1.z_ref, f32[32,8,128,128]{3,2,1,0:T(8,128)} %bitcast.147), custom_call_target="tpu_custom_call" | custom-call | bytes 16777216 | tf_op jit(solution)/shard_map/fetch/pallas_call | solution.py:182
  45.0 3.9 %collective-permute-done.11.rest_2_ = f32[2,2,2,8,512]{4,3,2,1,0:T(8,128)S(1)} collective-permute-done((f32[2,2,2,8,512]{4,3,2,1,0:T(8,128)S(1)}, f32[2,2,2,8,512]{4,3,2,1,0:T(8,128)S(1)}, u32[]{:S(2)}, u32[]{:S(2)}) %collective-permute-start.11) | collective-permute-done | bytes 131104 | tf_op jit(solution)/shard_map/ppermute | solution.py:55
  49.0 2.5 %update.4 = (f32[32,8,128,128]{3,2,1,0:T(8,128)}, f32[2,4,64,128]{3,2,1,0:T(8,128)S(1)}, f32[8,128,128]{2,1,0:T(8,128)S(1)}) custom-call(s32[1]{0:T(128)} %bitcast.1.z_ref, f32[2,4,8,128,128]{4,3,2,1,0:T(8,128)S(1)} %get-tuple-element.54.held, f32[8,128,128]{2,1,0:T(8,128)S(1)} %bitcast.144, f32[2,2,2,8,512]{4,3,2,1,0:T(8,128)S(1)} %pad_maximum_fusion.4.rest_0_, ...), custom_call_target="tpu_custom_call" | custom-call | flops 2097152 | bytes 4194304 | tf_op jit(solution)/shard_map/update/pallas_call | solution.py:281
  51.6 2.5 %collective-permute-start.17 = (f32[4,64,128]{2,1,0:T(8,128)S(1)}, f32[4,64,128]{2,1,0:T(8,128)S(1)}, u32[]{:S(2)}, u32[]{:S(2)}) collective-permute-start(f32[4,64,128]{2,1,0:T(8,128)S(1)} %get-tuple-element.84), channel_id=1, source_target_pairs={{0,3},{1,2},{2,1},{3,0},{4,7},{5,6},{6,5},{7,4},{8,11},{9,10},{10,... | collective-permute-start | bytes 393224 | tf_op jit(solution)/shard_map/ppermute | solution.py:55
  54.2 2.4 %update.5 = (f32[32,8,128,128]{3,2,1,0:T(8,128)}, f32[2,4,64,128]{3,2,1,0:T(8,128)S(1)}) custom-call(s32[1]{0:T(128)} %bitcast.1.z_ref, f32[2,4,8,128,128]{4,3,2,1,0:T(8,128)S(1)} %get-tuple-element.49.held, f32[8,128,128]{2,1,0:T(8,128)S(1)} %get-tuple-element.55.scale, f32[32,8,128,128]{3,2,1,0:T(8,128)} %get-tuple-element.57.before), custom_call_target="tpu_custom_call", output_to_operand_aliasing={{0}: (3, {})} | custom-call | flops 2097152 | bytes 4194304 | tf_op jit(solution)/shard_map/update/pallas_call | solution.py:281
  57.7 1.3 %collective-permute-start.16 = (f32[4,64,128]{2,1,0:T(8,128)S(1)}, f32[4,64,128]{2,1,0:T(8,128)S(1)}, u32[]{:S(2)}, u32[]{:S(2)}) collective-permute-start(f32[4,64,128]{2,1,0:T(8,128)S(1)} %get-tuple-element.80), channel_id=1, source_target_pairs={{0,3},{1,2},{2,1},{3,0},{4,7},{5,6},{6,5},{7,4},{8,11},{9,10},{10,... | collective-permute-start | bytes 393224 | tf_op jit(solution)/shard_map/ppermute | solution.py:55
  59.0 2.4 %update.6 = (f32[32,8,128,128]{3,2,1,0:T(8,128)}, f32[2,4,64,128]{3,2,1,0:T(8,128)S(1)}) custom-call(s32[1]{0:T(128)} %bitcast.1.z_ref, f32[2,4,8,128,128]{4,3,2,1,0:T(8,128)S(1)} %get-tuple-element.56.held, f32[8,128,128]{2,1,0:T(8,128)S(1)} %get-tuple-element.55.scale, f32[32,8,128,128]{3,2,1,0:T(8,128)} %get-tuple-element.58.before), custom_call_target="tpu_custom_call", output_to_operand_aliasing={{0}: (3, {})} | custom-call | flops 2097152 | bytes 4194304 | tf_op jit(solution)/shard_map/update/pallas_call | solution.py:281
  61.4 2.5 %collective-permute-start.15 = (f32[4,64,128]{2,1,0:T(8,128)S(1)}, f32[4,64,128]{2,1,0:T(8,128)S(1)}, u32[]{:S(2)}, u32[]{:S(2)}) collective-permute-start(f32[4,64,128]{2,1,0:T(8,128)S(1)} %get-tuple-element.81), channel_id=1, source_target_pairs={{0,3},{1,2},{2,1},{3,0},{4,7},{5,6},{6,5},{7,4},{8,11},{9,10},{10,... | collective-permute-start | bytes 393224 | tf_op jit(solution)/shard_map/ppermute | solution.py:55
  64.0 2.4 %update.7 = (f32[32,8,128,128]{3,2,1,0:T(8,128)}, f32[2,4,64,128]{3,2,1,0:T(8,128)S(1)}) custom-call(s32[1]{0:T(128)} %bitcast.1.z_ref, f32[2,4,8,128,128]{4,3,2,1,0:T(8,128)S(1)} %get-tuple-element.53.held, f32[8,128,128]{2,1,0:T(8,128)S(1)} %get-tuple-element.55.scale, f32[32,8,128,128]{3,2,1,0:T(8,128)} %get-tuple-element.59.before), custom_call_target="tpu_custom_call", output_to_operand_aliasing={{0}: (3, {})} | custom-call | flops 2097152 | bytes 4194304 | tf_op jit(solution)/shard_map/update/pallas_call | solution.py:281
  66.6 2.8 %collective-permute-done.15 = f32[4,64,128]{2,1,0:T(8,128)S(1)} collective-permute-done((f32[4,64,128]{2,1,0:T(8,128)S(1)}, f32[4,64,128]{2,1,0:T(8,128)S(1)}, u32[]{:S(2)}, u32[]{:S(2)}) %collective-permute-start.15) | collective-permute-done | bytes 131104 | tf_op jit(solution)/shard_map/ppermute | solution.py:55
  (50 shorter events, 8.0 us)
Async XLA Ops:
  3.1 3.0 %collective-permute-start = (f32[4,2,4,2,8,512]{5,4,3,2,1,0:T(8,128)S(1)}, f32[4,2,4,2,8,512]{5,4,3,2,1,0:T(8,128)S(1)}, u32[]{:S(2)}, u32[]{:S(2)}) collective-permute-start(f32[4,2,4,2,8,512]{5,4,3,2,1,0:T(8,128)S(1)} %get-tuple-element.34), channel_id=1, source_target_pairs={{0,4},{4,0},{8,12},{12,8},{16,20},{20,16},{24,28},{28,24},{1,5},{5... | collective-permute-start | bytes 3145736 | tf_op jit(solution)/shard_map/ppermute | solution.py:55
  8.6 7.0 %collective-permute-start.1 = (f32[4,2,4,2,8,512]{5,4,3,2,1,0:T(8,128)S(1)}, f32[4,2,4,2,8,512]{5,4,3,2,1,0:T(8,128)S(1)}, u32[]{:S(2)}, u32[]{:S(2)}) collective-permute-start(f32[4,2,4,2,8,512]{5,4,3,2,1,0:T(8,128)S(1)} %get-tuple-element.38), channel_id=1, source_target_pairs={{0,4},{4,0},{8,12},{12,8},{16,20},{20,16},{24,28},{28,24},{1,5},{5... | collective-permute-start | bytes 3145736 | tf_op jit(solution)/shard_map/ppermute | solution.py:55
  8.9 9.5 %collective-permute-start.6 = (f32[2,4,2,8,512]{4,3,2,1,0:T(8,128)S(1)}, f32[2,4,2,8,512]{4,3,2,1,0:T(8,128)S(1)}, u32[]{:S(2)}, u32[]{:S(2)}) collective-permute-start(f32[2,4,2,8,512]{4,3,2,1,0:T(8,128)S(1)} %fusion.3), channel_id=1, source_target_pairs={{0,16},{4,20},{8,24},{12,28},{16,0},{20,4},{24,8},{28,12},{1,17},{... | collective-permute-start | bytes 786440 | tf_op jit(solution)/shard_map/ppermute | solution.py:55
  11.7 8.1 %collective-permute-start.4 = (f32[2,4,2,8,512]{4,3,2,1,0:T(8,128)S(1)}, f32[2,4,2,8,512]{4,3,2,1,0:T(8,128)S(1)}, u32[]{:S(2)}, u32[]{:S(2)}) collective-permute-start(f32[2,4,2,8,512]{4,3,2,1,0:T(8,128)S(1)} %fusion.5), channel_id=1, source_target_pairs={{0,8},{4,12},{8,0},{12,4},{16,24},{20,28},{24,16},{28,20},{1,9},{5... | collective-permute-start | bytes 786440 | tf_op jit(solution)/shard_map/ppermute | solution.py:55
  20.0 10.1 %collective-permute-start.5 = (f32[4,2,8,512]{3,2,1,0:T(8,128)S(1)}, f32[4,2,8,512]{3,2,1,0:T(8,128)S(1)}, u32[]{:S(2)}, u32[]{:S(2)}) collective-permute-start(f32[4,2,8,512]{3,2,1,0:T(8,128)S(1)} %get-tuple-element.66), channel_id=1, source_target_pairs={{0,16},{4,20},{8,24},{12,28},{16,0},{20,4},{24,8},{28,12},{1,17},{... | collective-permute-start | bytes 393224 | tf_op jit(solution)/shard_map/ppermute | solution.py:55
  20.3 9.8 %collective-permute-start.3 = (f32[2,4,2,8,512]{4,3,2,1,0:T(8,128)S(1)}, f32[2,4,2,8,512]{4,3,2,1,0:T(8,128)S(1)}, u32[]{:S(2)}, u32[]{:S(2)}) collective-permute-start(f32[2,4,2,8,512]{4,3,2,1,0:T(8,128)S(1)} %fusion.1), channel_id=1, source_target_pairs={{0,16},{4,20},{8,24},{12,28},{16,0},{20,4},{24,8},{28,12},{1,17},{... | collective-permute-start | bytes 786440 | tf_op jit(solution)/shard_map/ppermute | solution.py:55
  22.1 8.1 %collective-permute-start.2 = (f32[2,4,2,8,512]{4,3,2,1,0:T(8,128)S(1)}, f32[2,4,2,8,512]{4,3,2,1,0:T(8,128)S(1)}, u32[]{:S(2)}, u32[]{:S(2)}) collective-permute-start(f32[2,4,2,8,512]{4,3,2,1,0:T(8,128)S(1)} %fusion.2), channel_id=1, source_target_pairs={{0,8},{4,12},{8,0},{12,4},{16,24},{20,28},{24,16},{28,20},{1,9},{5... | collective-permute-start | bytes 786440 | tf_op jit(solution)/shard_map/ppermute | solution.py:55
  23.6 8.0 %collective-permute-start.7 = (f32[4,2,8,512]{3,2,1,0:T(8,128)S(1)}, f32[4,2,8,512]{3,2,1,0:T(8,128)S(1)}, u32[]{:S(2)}, u32[]{:S(2)}) collective-permute-start(f32[4,2,8,512]{3,2,1,0:T(8,128)S(1)} %get-tuple-element.73), channel_id=1, source_target_pairs={{0,8},{4,12},{8,0},{12,4},{16,24},{20,28},{24,16},{28,20},{1,9},{5... | collective-permute-start | bytes 393224 | tf_op jit(solution)/shard_map/ppermute | solution.py:55
  30.3 6.3 %collective-permute-start.8 = (f32[4,2,8,512]{3,2,1,0:T(8,128)S(1)}, f32[4,2,8,512]{3,2,1,0:T(8,128)S(1)}, u32[]{:S(2)}, u32[]{:S(2)}) collective-permute-start(f32[4,2,8,512]{3,2,1,0:T(8,128)S(1)} %get-tuple-element.70), channel_id=1, source_target_pairs={{0,16},{4,20},{8,24},{12,28},{16,0},{20,4},{24,8},{28,12},{1,17},{... | collective-permute-start | bytes 393224 | tf_op jit(solution)/shard_map/ppermute | solution.py:55
  31.6 5.1 %collective-permute-start.9 = (f32[4,2,8,512]{3,2,1,0:T(8,128)S(1)}, f32[4,2,8,512]{3,2,1,0:T(8,128)S(1)}, u32[]{:S(2)}, u32[]{:S(2)}) collective-permute-start(f32[4,2,8,512]{3,2,1,0:T(8,128)S(1)} %get-tuple-element.75), channel_id=1, source_target_pairs={{0,8},{4,12},{8,0},{12,4},{16,24},{20,28},{24,16},{28,20},{1,9},{5... | collective-permute-start | bytes 393224 | tf_op jit(solution)/shard_map/ppermute | solution.py:55
  36.8 8.3 %collective-permute-start.12 = (f32[2,2,2,8,512]{4,3,2,1,0:T(8,128)S(1)}, f32[2,2,2,8,512]{4,3,2,1,0:T(8,128)S(1)}, u32[]{:S(2)}, u32[]{:S(2)}) collective-permute-start(f32[2,2,2,8,512]{4,3,2,1,0:T(8,128)S(1)} %pad_maximum_fusion.3), channel_id=1, source_target_pairs={{0,3},{1,2},{2,1},{3,0},{4,7},{5,6},{6,5},{7,4},{8,11},{9,10},{10,... | collective-permute-start | bytes 393224 | tf_op jit(solution)/shard_map/ppermute | solution.py:55
  40.5 8.5 %collective-permute-start.11 = (f32[2,2,2,8,512]{4,3,2,1,0:T(8,128)S(1)}, f32[2,2,2,8,512]{4,3,2,1,0:T(8,128)S(1)}, u32[]{:S(2)}, u32[]{:S(2)}) collective-permute-start(f32[2,2,2,8,512]{4,3,2,1,0:T(8,128)S(1)} %pad_maximum_fusion.2), channel_id=1, source_target_pairs={{0,2},{1,3},{2,0},{3,1},{4,6},{5,7},{6,4},{7,5},{8,10},{9,11},{10,... | collective-permute-start | bytes 393224 | tf_op jit(solution)/shard_map/ppermute | solution.py:55
  40.6 8.4 %collective-permute-start.10 = (f32[2,2,2,8,512]{4,3,2,1,0:T(8,128)S(1)}, f32[2,2,2,8,512]{4,3,2,1,0:T(8,128)S(1)}, u32[]{:S(2)}, u32[]{:S(2)}) collective-permute-start(f32[2,2,2,8,512]{4,3,2,1,0:T(8,128)S(1)} %pad_maximum_fusion.1), channel_id=1, source_target_pairs={{0,1},{1,0},{2,3},{3,2},{4,5},{5,4},{6,7},{7,6},{8,9},{9,8},{10,11... | collective-permute-start | bytes 393224 | tf_op jit(solution)/shard_map/ppermute | solution.py:55
  41.4 7.6 %copy-start = (f32[8,16,2,2,256]{4,3,2,1,0:T(2,128)S(1)}, f32[8,16,2,2,256]{4,3,2,1,0:T(2,128)}, u32[]{:S(2)}) copy-start(f32[8,16,2,2,256]{4,3,2,1,0:T(2,128)} %param.7) | copy-start | bytes 1572868
  51.5 9.8 %collective-permute-start.14 = (f32[4,64,128]{2,1,0:T(8,128)S(1)}, f32[4,64,128]{2,1,0:T(8,128)S(1)}, u32[]{:S(2)}, u32[]{:S(2)}) collective-permute-start(f32[4,64,128]{2,1,0:T(8,128)S(1)} %get-tuple-element.83), channel_id=1, source_target_pairs={{0,1},{1,0},{2,3},{3,2},{4,5},{5,4},{6,7},{7,6},{8,9},{9,8},{10,11... | collective-permute-start | bytes 393224 | tf_op jit(solution)/shard_map/ppermute | solution.py:55
  51.6 9.8 %collective-permute-start.17 = (f32[4,64,128]{2,1,0:T(8,128)S(1)}, f32[4,64,128]{2,1,0:T(8,128)S(1)}, u32[]{:S(2)}, u32[]{:S(2)}) collective-permute-start(f32[4,64,128]{2,1,0:T(8,128)S(1)} %get-tuple-element.84), channel_id=1, source_target_pairs={{0,3},{1,2},{2,1},{3,0},{4,7},{5,6},{6,5},{7,4},{8,11},{9,10},{10,... | collective-permute-start | bytes 393224 | tf_op jit(solution)/shard_map/ppermute | solution.py:55
  56.6 10.0 %collective-permute-start.13 = (f32[4,64,128]{2,1,0:T(8,128)S(1)}, f32[4,64,128]{2,1,0:T(8,128)S(1)}, u32[]{:S(2)}, u32[]{:S(2)}) collective-permute-start(f32[4,64,128]{2,1,0:T(8,128)S(1)} %get-tuple-element.79), channel_id=1, source_target_pairs={{0,1},{1,0},{2,3},{3,2},{4,5},{5,4},{6,7},{7,6},{8,9},{9,8},{10,11... | collective-permute-start | bytes 393224 | tf_op jit(solution)/shard_map/ppermute | solution.py:55
  57.7 8.9 %collective-permute-start.16 = (f32[4,64,128]{2,1,0:T(8,128)S(1)}, f32[4,64,128]{2,1,0:T(8,128)S(1)}, u32[]{:S(2)}, u32[]{:S(2)}) collective-permute-start(f32[4,64,128]{2,1,0:T(8,128)S(1)} %get-tuple-element.80), channel_id=1, source_target_pairs={{0,3},{1,2},{2,1},{3,0},{4,7},{5,6},{6,5},{7,4},{8,11},{9,10},{10,... | collective-permute-start | bytes 393224 | tf_op jit(solution)/shard_map/ppermute | solution.py:55
  61.4 8.0 %collective-permute-start.15 = (f32[4,64,128]{2,1,0:T(8,128)S(1)}, f32[4,64,128]{2,1,0:T(8,128)S(1)}, u32[]{:S(2)}, u32[]{:S(2)}) collective-permute-start(f32[4,64,128]{2,1,0:T(8,128)S(1)} %get-tuple-element.81), channel_id=1, source_target_pairs={{0,3},{1,2},{2,1},{3,0},{4,7},{5,6},{6,5},{7,4},{8,11},{9,10},{10,... | collective-permute-start | bytes 393224 | tf_op jit(solution)/shard_map/ppermute | solution.py:55
  64.0 6.6 %collective-permute-start.18 = (f32[4,64,128]{2,1,0:T(8,128)S(1)}, f32[4,64,128]{2,1,0:T(8,128)S(1)}, u32[]{:S(2)}, u32[]{:S(2)}) collective-permute-start(f32[4,64,128]{2,1,0:T(8,128)S(1)} %get-tuple-element.82), channel_id=1, source_target_pairs={{0,1},{1,0},{2,3},{3,2},{4,5},{5,4},{6,7},{7,6},{8,9},{9,8},{10,11... | collective-permute-start | bytes 393224 | tf_op jit(solution)/shard_map/ppermute | solution.py:55

commit v4 on v3

--- a/solution.py
+++ b/solution.py
@@ -342,20 +342,23 @@
         y0_in, x1_in = swap(y0, "va", 4), swap(x1, "va", 2)
         for m in range(n_vb):
             pieces[m].append(jnp.stack([k0[m] + y0_in[m], k1[m] + x1_in[m]]))
+    far = n_vb // 2
+    early = swap(pieces[far][0], "vb", far)
+    late = swap(pieces[far][1], "vb", far)
     pieces = [jnp.stack(piece) for piece in pieces]
-    seps = [pieces[0]] + [swap(pieces[m], "vb", m) for m in range(1, n_vb)]
-
-    through, direct = [(2, 0), (2, 1)], [(1, 0), (3, 1)]
-    forward, own = [(3, 0), (1, 1)], [(0, 0), (0, 1)]
+    seps = [pieces[0]] + [swap(pieces[m], "vb", m) if m != far else None for m in range(1, n_vb)]
+    seps[far] = jnp.stack([early, late])
+
+    through, middle = [(2, 0), (2, 1)], [(1, 0), (3, 1), (3, 0), (1, 1)]
+    own = [(0, 0), (0, 1)]
     dims = (nr1, nhi, nr2)
-    held_t, held_d = fetch(tie(z, absorbed, y0, x1), b_rows, (through, direct), n_vb)
-    held_f, held_o = fetch(tie(z, held_d, *pieces[1:]), b_rows, (forward, own), n_vb)
+    held_t, held_o = fetch(tie(z, absorbed, y0, x1), b_rows, (through, own), n_vb)
+    (held_m,) = fetch(tie(z, held_o, *pieces[1:]), b_rows, (middle,), n_vb)
     updated, sent, scale = update(z, held_t, b_rows, through, dims, seps=seps, old=old_rows)
     t0, t1 = swap(sent[0], "vb", 1), swap(sent[1], "vb", 3)
-    updated, sent = update(z, held_d, b_rows, direct, dims, scale=scale, before=updated)
+    updated, sent = update(z, held_m, b_rows, middle, dims, scale=scale, before=updated)
     d0, d1 = swap(sent[0], "vb", 1), swap(sent[1], "vb", 3)
-    updated, kept = update(z, held_f, b_rows, forward, dims, scale=scale, before=updated)
-    s0, s1 = swap(kept[0] + t0, "vb", 3), swap(kept[1] + t1, "vb", 1)
+    s0, s1 = swap(sent[2] + t0, "vb", 3), swap(sent[3] + t1, "vb", 1)
     updated, kept = update(z, held_o, b_rows, own, dims, scale=scale, before=updated)
     onward = jnp.concatenate([kept[0] + d0 + s0, kept[1] + d1 + s1], axis=0)
 

time: 71.5 us -> 70.9 us (level)
  starting transfers between devices: 23.6 us -> 27.1 us
  waiting for transfers between devices: 13 us -> 9.92 us
  Pallas kernels: 32.3 us -> 31.3 us
    ppermute x19 -> x20, starting transfers between devices: 23.6 us -> 27.1 us  [swap(): return lax.ppermute(x, axis, [(i, i ^ mask) for i in range(n)])]
    ppermute x19 -> x20, waiting for transfers between devices: 13 us -> 9.92 us  [swap(): return lax.ppermute(x, axis, [(i, i ^ mask) for i in range(n)])]
    pallas_call x4 -> x3, Pallas kernels: 9.56 us -> 8.55 us  [update(): pl.pallas_call(kernel, in_specs=[pl.BlockSpec(memory_space=pltpu.SMEM)] +...]
  transfers between devices with their start and end apart: 19 -> 20, of which waited for: 8 -> 8; matrix products, arithmetic and copies ran while one was open for 1% -> 1% of each run, Pallas kernels for 35% -> 34%
where the time goes in v4:
time: 70.9 us; the launch traced here: 70.7 us
  Pallas kernels  31.3 us (44%)
  starting transfers between devices  27.1 us (38%)
  waiting for transfers between devices  9.92 us (14%)
  other arithmetic  1.41 us (2%)
  between operations  0.93 us (1%)
    ppermute x20, starting transfers between devices, swap(): return lax.ppermute(x, axis, [(i, i ^ mask) for i in range(n)])  27.1 us
    ppermute x20, waiting for transfers between devices, swap(): return lax.ppermute(x, axis, [(i, i ^ mask) for i in range(n)])  9.92 us
    pallas_call x4, Pallas kernels, absorb(): pl.pallas_call(functools.partial(absorb_kernel, chunk, part), in_specs=[p...  9.76 us
    pallas_call x3, Pallas kernels, update(): pl.pallas_call(kernel, in_specs=[pl.BlockSpec(memory_space=pltpu.SMEM)] +...  8.55 us
    pallas_call x2, Pallas kernels, fetch(): pl.pallas_call(functools.partial(fetch_kernel, orders), in_specs=[pl.Bloc...  7.05 us
    pallas_call x1, Pallas kernels, flush(): pl.pallas_call(flush_kernel, in_specs=[pl.BlockSpec(memory_space=pltpu.SM...  5.96 us
  transfers between devices with their start and end apart: 20, of which 8 were waited for; matrix products, arithmetic and copies ran while one was open for 1% of the time, Pallas kernels for 34%

profile of v4, /device:TPU:0, one launch (start us, length us, event | category | flops | bytes accessed | tf_op | source)
XLA Modules:
  0.0 70.7 jit_solution(6116587160579111274)
XLA Ops:
  0.6 2.4 %absorb.4 = (f32[4,2,2,2,8,4096]{5,4,3,2,1,0:T(8,128)S(1)}, f32[4,2,4,2,8,512]{5,4,3,2,1,0:T(8,128)S(1)}) custom-call(s32[1]{0:T(128)} %bitcast.me_ref, s32[1]{0:T(128)} %bitcast.1.z_ref, f32[2,2,2,16,32768]{4,3,2,1,0:T(8,128)} %a_hbm.7, f32[2,2,32768]{2,1,0:T(2,128)} %m_hbm.7), custom_call_target="tpu_custom_call" | custom-call | flops 2097152 | bytes 4194304 | tf_op jit(solution)/shard_map/absorb/pallas_call | solution.py:107
  3.6 2.4 %absorb.5 = (f32[4,2,2,2,8,4096]{5,4,3,2,1,0:T(8,128)S(1)}, f32[4,2,4,2,8,512]{5,4,3,2,1,0:T(8,128)S(1)}) custom-call(s32[1]{0:T(128)} %bitcast.me_ref, s32[1]{0:T(128)} %bitcast.1.z_ref, f32[2,2,2,16,32768]{4,3,2,1,0:T(8,128)} %a_hbm.7, f32[2,2,32768]{2,1,0:T(2,128)} %m_hbm.7), custom_call_target="tpu_custom_call" | custom-call | flops 2097152 | bytes 4194304 | tf_op jit(solution)/shard_map/absorb/pallas_call | solution.py:107
  6.1 2.4 %absorb.6 = (f32[4,2,2,2,8,4096]{5,4,3,2,1,0:T(8,128)S(1)}, f32[4,2,4,2,8,512]{5,4,3,2,1,0:T(8,128)S(1)}) custom-call(s32[1]{0:T(128)} %bitcast.me_ref, s32[1]{0:T(128)} %bitcast.1.z_ref, f32[2,2,2,16,32768]{4,3,2,1,0:T(8,128)} %a_hbm.7, f32[2,2,32768]{2,1,0:T(2,128)} %m_hbm.7), custom_call_target="tpu_custom_call" | custom-call | flops 2097152 | bytes 4194304 | tf_op jit(solution)/shard_map/absorb/pallas_call | solution.py:107
  8.9 2.8 %collective-permute-start.4 = (f32[2,4,2,8,512]{4,3,2,1,0:T(8,128)S(1)}, f32[2,4,2,8,512]{4,3,2,1,0:T(8,128)S(1)}, u32[]{:S(2)}, u32[]{:S(2)}) collective-permute-start(f32[2,4,2,8,512]{4,3,2,1,0:T(8,128)S(1)} %fusion.5), channel_id=1, source_target_pairs={{0,8},{4,12},{8,0},{12,4},{16,24},{20,28},{24,16},{28,20},{1,9},{5... | collective-permute-start | bytes 786440 | tf_op jit(solution)/shard_map/ppermute | solution.py:55
  11.7 1.5 %collective-permute-start.6 = (f32[2,4,2,8,512]{4,3,2,1,0:T(8,128)S(1)}, f32[2,4,2,8,512]{4,3,2,1,0:T(8,128)S(1)}, u32[]{:S(2)}, u32[]{:S(2)}) collective-permute-start(f32[2,4,2,8,512]{4,3,2,1,0:T(8,128)S(1)} %fusion.3), channel_id=1, source_target_pairs={{0,16},{4,20},{8,24},{12,28},{16,0},{20,4},{24,8},{28,12},{1,17},{... | collective-permute-start | bytes 786440 | tf_op jit(solution)/shard_map/ppermute | solution.py:55
  13.2 2.4 %absorb.7 = (f32[4,2,2,2,8,4096]{5,4,3,2,1,0:T(8,128)S(1)}, f32[4,2,4,2,8,512]{5,4,3,2,1,0:T(8,128)S(1)}) custom-call(s32[1]{0:T(128)} %bitcast.me_ref, s32[1]{0:T(128)} %bitcast.1.z_ref, f32[2,2,2,16,32768]{4,3,2,1,0:T(8,128)} %a_hbm.7, f32[2,2,32768]{2,1,0:T(2,128)} %m_hbm.7), custom_call_target="tpu_custom_call" | custom-call | flops 2097152 | bytes 4194304 | tf_op jit(solution)/shard_map/absorb/pallas_call | solution.py:107
  15.7 4.1 %collective-permute-done.6 = f32[2,4,2,8,512]{4,3,2,1,0:T(8,128)S(1)} collective-permute-done((f32[2,4,2,8,512]{4,3,2,1,0:T(8,128)S(1)}, f32[2,4,2,8,512]{4,3,2,1,0:T(8,128)S(1)}, u32[]{:S(2)}, u32[]{:S(2)}) %collective-permute-start.6) | collective-permute-done | bytes 262176 | tf_op jit(solution)/shard_map/ppermute | solution.py:55
  19.9 1.6 %collective-permute-start.5 = (f32[4,2,8,512]{3,2,1,0:T(8,128)S(1)}, f32[4,2,8,512]{3,2,1,0:T(8,128)S(1)}, u32[]{:S(2)}, u32[]{:S(2)}) collective-permute-start(f32[4,2,8,512]{3,2,1,0:T(8,128)S(1)} %get-tuple-element.58), channel_id=1, source_target_pairs={{0,16},{4,20},{8,24},{12,28},{16,0},{20,4},{24,8},{28,12},{1,17},{... | collective-permute-start | bytes 393224 | tf_op jit(solution)/shard_map/ppermute | solution.py:55
  22.4 1.7 %collective-permute-start.7 = (f32[4,2,8,512]{3,2,1,0:T(8,128)S(1)}, f32[4,2,8,512]{3,2,1,0:T(8,128)S(1)}, u32[]{:S(2)}, u32[]{:S(2)}) collective-permute-start(f32[4,2,8,512]{3,2,1,0:T(8,128)S(1)} %get-tuple-element.65), channel_id=1, source_target_pairs={{0,8},{4,12},{8,0},{12,4},{16,24},{20,28},{24,16},{28,20},{1,9},{5... | collective-permute-start | bytes 393224 | tf_op jit(solution)/shard_map/ppermute | solution.py:55
  24.1 6.0 %flush.1 = f32[2,2,2,16,32768]{4,3,2,1,0:T(8,128)} custom-call(s32[1]{0:T(128)} %bitcast.me_ref, f32[4,2,2,2,8,4096]{5,4,3,2,1,0:T(8,128)S(1)} %get-tuple-element.38.rest_0_, f32[4,2,2,2,8,4096]{5,4,3,2,1,0:T(8,128)S(1)} %get-tuple-element.39.rest_1_, f32[4,2,2,2,8,4096]{5,4,3,2,1,0:T(8,128)S(1)} %get-tuple-element.40.rest_2_, ...), custom_call_target="tpu_custom_call" | custom-call | bytes 16777216 | tf_op jit(solution)/shard_map/flush/pallas_call | solution.py:153
  30.1 1.3 %collective-permute-done.7 = f32[4,2,8,512]{3,2,1,0:T(8,128)S(1)} collective-permute-done((f32[4,2,8,512]{3,2,1,0:T(8,128)S(1)}, f32[4,2,8,512]{3,2,1,0:T(8,128)S(1)}, u32[]{:S(2)}, u32[]{:S(2)}) %collective-permute-start.7) | collective-permute-done | bytes 131104 | tf_op jit(solution)/shard_map/ppermute | solution.py:55
  31.4 2.7 %collective-permute-start.11 = (f32[2,2,8,512]{3,2,1,0:T(8,128)S(1)}, f32[2,2,8,512]{3,2,1,0:T(8,128)S(1)}, u32[]{:S(2)}, u32[]{:S(2)}) collective-permute-start(f32[2,2,8,512]{3,2,1,0:T(8,128)S(1)} %pad_maximum_fusion.5), channel_id=1, source_target_pairs={{0,2},{1,3},{2,0},{3,1},{4,6},{5,7},{6,4},{7,5},{8,10},{9,11},{10,... | collective-permute-start | bytes 196616 | tf_op jit(solution)/shard_map/ppermute | solution.py:55
  35.4 3.5 %fetch.2 = (f32[2,4,8,128,128]{4,3,2,1,0:T(8,128)S(1)}, f32[2,4,8,128,128]{4,3,2,1,0:T(8,128)S(1)}) custom-call(s32[1]{0:T(128)} %bitcast.1.z_ref, f32[32,8,128,128]{3,2,1,0:T(8,128)} %bitcast.143), custom_call_target="tpu_custom_call" | custom-call | bytes 16777216 | tf_op jit(solution)/shard_map/fetch/pallas_call | solution.py:182
  40.3 1.6 %collective-permute-start.10 = (f32[2,2,2,8,512]{4,3,2,1,0:T(8,128)S(1)}, f32[2,2,2,8,512]{4,3,2,1,0:T(8,128)S(1)}, u32[]{:S(2)}, u32[]{:S(2)}) collective-permute-start(f32[2,2,2,8,512]{4,3,2,1,0:T(8,128)S(1)} %pad_maximum_fusion.2), channel_id=1, source_target_pairs={{0,1},{1,0},{2,3},{3,2},{4,5},{5,4},{6,7},{7,6},{8,9},{9,8},{10,11... | collective-permute-start | bytes 393224 | tf_op jit(solution)/shard_map/ppermute | solution.py:55
  41.9 2.5 %collective-permute-start.13 = (f32[2,2,2,8,512]{4,3,2,1,0:T(8,128)S(1)}, f32[2,2,2,8,512]{4,3,2,1,0:T(8,128)S(1)}, u32[]{:S(2)}, u32[]{:S(2)}) collective-permute-start(f32[2,2,2,8,512]{4,3,2,1,0:T(8,128)S(1)} %pad_maximum_fusion.4), channel_id=1, source_target_pairs={{0,3},{1,2},{2,1},{3,0},{4,7},{5,6},{6,5},{7,4},{8,11},{9,10},{10,... | collective-permute-start | bytes 393224 | tf_op jit(solution)/shard_map/ppermute | solution.py:55
  44.5 3.6 %fetch.3.held = f32[4,4,8,128,128]{4,3,2,1,0:T(8,128)S(1)} custom-call(s32[1]{0:T(128)} %bitcast.1.z_ref, f32[32,8,128,128]{3,2,1,0:T(8,128)} %bitcast.144), custom_call_target="tpu_custom_call" | custom-call | bytes 16777216 | tf_op jit(solution)/shard_map/fetch/pallas_call | solution.py:182
  48.9 2.5 %update.3 = (f32[32,8,128,128]{3,2,1,0:T(8,128)}, f32[2,4,64,128]{3,2,1,0:T(8,128)S(1)}, f32[8,128,128]{2,1,0:T(8,128)S(1)}) custom-call(s32[1]{0:T(128)} %bitcast.1.z_ref, f32[2,4,8,128,128]{4,3,2,1,0:T(8,128)S(1)} %get-tuple-element.46.held, f32[8,128,128]{2,1,0:T(8,128)S(1)} %bitcast.142, f32[2,2,2,8,512]{4,3,2,1,0:T(8,128)S(1)} %pad_maximum_fusion.1.rest_0_, ...), custom_call_target="tpu_custom_call" | custom-call | flops 2097152 | bytes 4194304 | tf_op jit(solution)/shard_map/update/pallas_call | solution.py:281
  51.7 3.3 %collective-permute-start.18 = (f32[4,64,128]{2,1,0:T(8,128)S(1)}, f32[4,64,128]{2,1,0:T(8,128)S(1)}, u32[]{:S(2)}, u32[]{:S(2)}) collective-permute-start(f32[4,64,128]{2,1,0:T(8,128)S(1)} %get-tuple-element.76), channel_id=1, source_target_pairs={{0,3},{1,2},{2,1},{3,0},{4,7},{5,6},{6,5},{7,4},{8,11},{9,10},{10,... | collective-permute-start | bytes 393224 | tf_op jit(solution)/shard_map/ppermute | solution.py:55
  55.0 3.7 %update.4 = (f32[32,8,128,128]{3,2,1,0:T(8,128)}, f32[4,4,64,128]{3,2,1,0:T(8,128)S(1)}) custom-call(s32[1]{0:T(128)} %bitcast.1.z_ref, f32[4,4,8,128,128]{4,3,2,1,0:T(8,128)S(1)} %fetch.3.held, f32[8,128,128]{2,1,0:T(8,128)S(1)} %get-tuple-element.49.scale, f32[32,8,128,128]{3,2,1,0:T(8,128)} %get-tuple-element.51.before), custom_call_target="tpu_custom_call", output_to_operand_aliasing={{0}: (3, {})} | custom-call | flops 4194304 | bytes 8388608 | tf_op jit(solution)/shard_map/update/pallas_call | solution.py:281
  58.9 1.4 %collective-permute-start.17 = (f32[4,64,128]{2,1,0:T(8,128)S(1)}, f32[4,64,128]{2,1,0:T(8,128)S(1)}, u32[]{:S(2)}, u32[]{:S(2)}) collective-permute-start(f32[4,64,128]{2,1,0:T(8,128)S(1)} %get-tuple-element.70), channel_id=1, source_target_pairs={{0,3},{1,2},{2,1},{3,0},{4,7},{5,6},{6,5},{7,4},{8,11},{9,10},{10,... | collective-permute-start | bytes 393224 | tf_op jit(solution)/shard_map/ppermute | solution.py:55
  61.1 2.4 %collective-permute-start.16 = (f32[4,64,128]{2,1,0:T(8,128)S(1)}, f32[4,64,128]{2,1,0:T(8,128)S(1)}, u32[]{:S(2)}, u32[]{:S(2)}) collective-permute-start(f32[4,64,128]{2,1,0:T(8,128)S(1)} %get-tuple-element.71), channel_id=1, source_target_pairs={{0,3},{1,2},{2,1},{3,0},{4,7},{5,6},{6,5},{7,4},{8,11},{9,10},{10,... | collective-permute-start | bytes 393224 | tf_op jit(solution)/shard_map/ppermute | solution.py:55
  63.5 1.9 %collective-permute-start.19 = (f32[4,64,128]{2,1,0:T(8,128)S(1)}, f32[4,64,128]{2,1,0:T(8,128)S(1)}, u32[]{:S(2)}, u32[]{:S(2)}) collective-permute-start(f32[4,64,128]{2,1,0:T(8,128)S(1)} %get-tuple-element.72), channel_id=1, source_target_pairs={{0,1},{1,0},{2,3},{3,2},{4,5},{5,4},{6,7},{7,6},{8,9},{9,8},{10,11... | collective-permute-start | bytes 393224 | tf_op jit(solution)/shard_map/ppermute | solution.py:55
  65.4 2.4 %update.5 = (f32[32,8,128,128]{3,2,1,0:T(8,128)}, f32[2,4,64,128]{3,2,1,0:T(8,128)S(1)}) custom-call(s32[1]{0:T(128)} %bitcast.1.z_ref, f32[2,4,8,128,128]{4,3,2,1,0:T(8,128)S(1)} %get-tuple-element.45.held, f32[8,128,128]{2,1,0:T(8,128)S(1)} %get-tuple-element.49.scale, f32[32,8,128,128]{3,2,1,0:T(8,128)} %get-tuple-element.52.before), custom_call_target="tpu_custom_call", output_to_operand_aliasing={{0}: (3, {})} | custom-call | flops 2097152 | bytes 4194304 | tf_op jit(solution)/shard_map/update/pallas_call | solution.py:281
  68.6 1.3 %collective-permute-done.19 = f32[4,64,128]{2,1,0:T(8,128)S(1)} collective-permute-done((f32[4,64,128]{2,1,0:T(8,128)S(1)}, f32[4,64,128]{2,1,0:T(8,128)S(1)}, u32[]{:S(2)}, u32[]{:S(2)}) %collective-permute-start.19) | collective-permute-done | bytes 131104 | tf_op jit(solution)/shard_map/ppermute | solution.py:55
  (54 shorter events, 8.2 us)
Async XLA Ops:
  3.1 3.0 %collective-permute-start = (f32[4,2,4,2,8,512]{5,4,3,2,1,0:T(8,128)S(1)}, f32[4,2,4,2,8,512]{5,4,3,2,1,0:T(8,128)S(1)}, u32[]{:S(2)}, u32[]{:S(2)}) collective-permute-start(f32[4,2,4,2,8,512]{5,4,3,2,1,0:T(8,128)S(1)} %get-tuple-element.30), channel_id=1, source_target_pairs={{0,4},{4,0},{8,12},{12,8},{16,20},{20,16},{24,28},{28,24},{1,5},{5... | collective-permute-start | bytes 3145736 | tf_op jit(solution)/shard_map/ppermute | solution.py:55
  8.6 7.0 %collective-permute-start.1 = (f32[4,2,4,2,8,512]{5,4,3,2,1,0:T(8,128)S(1)}, f32[4,2,4,2,8,512]{5,4,3,2,1,0:T(8,128)S(1)}, u32[]{:S(2)}, u32[]{:S(2)}) collective-permute-start(f32[4,2,4,2,8,512]{5,4,3,2,1,0:T(8,128)S(1)} %get-tuple-element.34), channel_id=1, source_target_pairs={{0,4},{4,0},{8,12},{12,8},{16,20},{20,16},{24,28},{28,24},{1,5},{5... | collective-permute-start | bytes 3145736 | tf_op jit(solution)/shard_map/ppermute | solution.py:55
  8.9 10.9 %collective-permute-start.4 = (f32[2,4,2,8,512]{4,3,2,1,0:T(8,128)S(1)}, f32[2,4,2,8,512]{4,3,2,1,0:T(8,128)S(1)}, u32[]{:S(2)}, u32[]{:S(2)}) collective-permute-start(f32[2,4,2,8,512]{4,3,2,1,0:T(8,128)S(1)} %fusion.5), channel_id=1, source_target_pairs={{0,8},{4,12},{8,0},{12,4},{16,24},{20,28},{24,16},{28,20},{1,9},{5... | collective-permute-start | bytes 786440 | tf_op jit(solution)/shard_map/ppermute | solution.py:55
  11.7 8.1 %collective-permute-start.6 = (f32[2,4,2,8,512]{4,3,2,1,0:T(8,128)S(1)}, f32[2,4,2,8,512]{4,3,2,1,0:T(8,128)S(1)}, u32[]{:S(2)}, u32[]{:S(2)}) collective-permute-start(f32[2,4,2,8,512]{4,3,2,1,0:T(8,128)S(1)} %fusion.3), channel_id=1, source_target_pairs={{0,16},{4,20},{8,24},{12,28},{16,0},{20,4},{24,8},{28,12},{1,17},{... | collective-permute-start | bytes 786440 | tf_op jit(solution)/shard_map/ppermute | solution.py:55
  19.9 10.1 %collective-permute-start.5 = (f32[4,2,8,512]{3,2,1,0:T(8,128)S(1)}, f32[4,2,8,512]{3,2,1,0:T(8,128)S(1)}, u32[]{:S(2)}, u32[]{:S(2)}) collective-permute-start(f32[4,2,8,512]{3,2,1,0:T(8,128)S(1)} %get-tuple-element.58), channel_id=1, source_target_pairs={{0,16},{4,20},{8,24},{12,28},{16,0},{20,4},{24,8},{28,12},{1,17},{... | collective-permute-start | bytes 393224 | tf_op jit(solution)/shard_map/ppermute | solution.py:55
  21.5 12.5 %collective-permute-start.2 = (f32[2,4,2,8,512]{4,3,2,1,0:T(8,128)S(1)}, f32[2,4,2,8,512]{4,3,2,1,0:T(8,128)S(1)}, u32[]{:S(2)}, u32[]{:S(2)}) collective-permute-start(f32[2,4,2,8,512]{4,3,2,1,0:T(8,128)S(1)} %fusion.2), channel_id=1, source_target_pairs={{0,8},{4,12},{8,0},{12,4},{16,24},{20,28},{24,16},{28,20},{1,9},{5... | collective-permute-start | bytes 786440 | tf_op jit(solution)/shard_map/ppermute | solution.py:55
  22.1 12.0 %collective-permute-start.3 = (f32[2,4,2,8,512]{4,3,2,1,0:T(8,128)S(1)}, f32[2,4,2,8,512]{4,3,2,1,0:T(8,128)S(1)}, u32[]{:S(2)}, u32[]{:S(2)}) collective-permute-start(f32[2,4,2,8,512]{4,3,2,1,0:T(8,128)S(1)} %fusion.1), channel_id=1, source_target_pairs={{0,16},{4,20},{8,24},{12,28},{16,0},{20,4},{24,8},{28,12},{1,17},{... | collective-permute-start | bytes 786440 | tf_op jit(solution)/shard_map/ppermute | solution.py:55
  22.4 9.0 %collective-permute-start.7 = (f32[4,2,8,512]{3,2,1,0:T(8,128)S(1)}, f32[4,2,8,512]{3,2,1,0:T(8,128)S(1)}, u32[]{:S(2)}, u32[]{:S(2)}) collective-permute-start(f32[4,2,8,512]{3,2,1,0:T(8,128)S(1)} %get-tuple-element.65), channel_id=1, source_target_pairs={{0,8},{4,12},{8,0},{12,4},{16,24},{20,28},{24,16},{28,20},{1,9},{5... | collective-permute-start | bytes 393224 | tf_op jit(solution)/shard_map/ppermute | solution.py:55
  31.4 16.7 %collective-permute-start.11 = (f32[2,2,8,512]{3,2,1,0:T(8,128)S(1)}, f32[2,2,8,512]{3,2,1,0:T(8,128)S(1)}, u32[]{:S(2)}, u32[]{:S(2)}) collective-permute-start(f32[2,2,8,512]{3,2,1,0:T(8,128)S(1)} %pad_maximum_fusion.5), channel_id=1, source_target_pairs={{0,2},{1,3},{2,0},{3,1},{4,6},{5,7},{6,4},{7,5},{8,10},{9,11},{10,... | collective-permute-start | bytes 196616 | tf_op jit(solution)/shard_map/ppermute | solution.py:55
  34.2 5.0 %collective-permute-start.8 = (f32[4,2,8,512]{3,2,1,0:T(8,128)S(1)}, f32[4,2,8,512]{3,2,1,0:T(8,128)S(1)}, u32[]{:S(2)}, u32[]{:S(2)}) collective-permute-start(f32[4,2,8,512]{3,2,1,0:T(8,128)S(1)} %get-tuple-element.62), channel_id=1, source_target_pairs={{0,16},{4,20},{8,24},{12,28},{16,0},{20,4},{24,8},{28,12},{1,17},{... | collective-permute-start | bytes 393224 | tf_op jit(solution)/shard_map/ppermute | solution.py:55
  34.8 5.0 %collective-permute-start.9 = (f32[4,2,8,512]{3,2,1,0:T(8,128)S(1)}, f32[4,2,8,512]{3,2,1,0:T(8,128)S(1)}, u32[]{:S(2)}, u32[]{:S(2)}) collective-permute-start(f32[4,2,8,512]{3,2,1,0:T(8,128)S(1)} %get-tuple-element.67), channel_id=1, source_target_pairs={{0,8},{4,12},{8,0},{12,4},{16,24},{20,28},{24,16},{28,20},{1,9},{5... | collective-permute-start | bytes 393224 | tf_op jit(solution)/shard_map/ppermute | solution.py:55
  39.9 8.2 %collective-permute-start.12 = (f32[2,2,8,512]{3,2,1,0:T(8,128)S(1)}, f32[2,2,8,512]{3,2,1,0:T(8,128)S(1)}, u32[]{:S(2)}, u32[]{:S(2)}) collective-permute-start(f32[2,2,8,512]{3,2,1,0:T(8,128)S(1)} %pad_maximum_fusion.6), channel_id=1, source_target_pairs={{0,2},{1,3},{2,0},{3,1},{4,6},{5,7},{6,4},{7,5},{8,10},{9,11},{10,... | collective-permute-start | bytes 196616 | tf_op jit(solution)/shard_map/ppermute | solution.py:55
  40.3 7.9 %collective-permute-start.10 = (f32[2,2,2,8,512]{4,3,2,1,0:T(8,128)S(1)}, f32[2,2,2,8,512]{4,3,2,1,0:T(8,128)S(1)}, u32[]{:S(2)}, u32[]{:S(2)}) collective-permute-start(f32[2,2,2,8,512]{4,3,2,1,0:T(8,128)S(1)} %pad_maximum_fusion.2), channel_id=1, source_target_pairs={{0,1},{1,0},{2,3},{3,2},{4,5},{5,4},{6,7},{7,6},{8,9},{9,8},{10,11... | collective-permute-start | bytes 393224 | tf_op jit(solution)/shard_map/ppermute | solution.py:55
  41.9 7.0 %collective-permute-start.13 = (f32[2,2,2,8,512]{4,3,2,1,0:T(8,128)S(1)}, f32[2,2,2,8,512]{4,3,2,1,0:T(8,128)S(1)}, u32[]{:S(2)}, u32[]{:S(2)}) collective-permute-start(f32[2,2,2,8,512]{4,3,2,1,0:T(8,128)S(1)} %pad_maximum_fusion.4), channel_id=1, source_target_pairs={{0,3},{1,2},{2,1},{3,0},{4,7},{5,6},{6,5},{7,4},{8,11},{9,10},{10,... | collective-permute-start | bytes 393224 | tf_op jit(solution)/shard_map/ppermute | solution.py:55
  44.5 4.4 %copy-start = (f32[8,16,2,2,256]{4,3,2,1,0:T(2,128)S(1)}, f32[8,16,2,2,256]{4,3,2,1,0:T(2,128)}, u32[]{:S(2)}) copy-start(f32[8,16,2,2,256]{4,3,2,1,0:T(2,128)} %param.7) | copy-start | bytes 1572868
  51.5 8.8 %collective-permute-start.15 = (f32[4,64,128]{2,1,0:T(8,128)S(1)}, f32[4,64,128]{2,1,0:T(8,128)S(1)}, u32[]{:S(2)}, u32[]{:S(2)}) collective-permute-start(f32[4,64,128]{2,1,0:T(8,128)S(1)} %get-tuple-element.75), channel_id=1, source_target_pairs={{0,1},{1,0},{2,3},{3,2},{4,5},{5,4},{6,7},{7,6},{8,9},{9,8},{10,11... | collective-permute-start | bytes 393224 | tf_op jit(solution)/shard_map/ppermute | solution.py:55
  51.7 9.4 %collective-permute-start.18 = (f32[4,64,128]{2,1,0:T(8,128)S(1)}, f32[4,64,128]{2,1,0:T(8,128)S(1)}, u32[]{:S(2)}, u32[]{:S(2)}) collective-permute-start(f32[4,64,128]{2,1,0:T(8,128)S(1)} %get-tuple-element.76), channel_id=1, source_target_pairs={{0,3},{1,2},{2,1},{3,0},{4,7},{5,6},{6,5},{7,4},{8,11},{9,10},{10,... | collective-permute-start | bytes 393224 | tf_op jit(solution)/shard_map/ppermute | solution.py:55
  58.8 9.0 %collective-permute-start.14 = (f32[4,64,128]{2,1,0:T(8,128)S(1)}, f32[4,64,128]{2,1,0:T(8,128)S(1)}, u32[]{:S(2)}, u32[]{:S(2)}) collective-permute-start(f32[4,64,128]{2,1,0:T(8,128)S(1)} %get-tuple-element.69), channel_id=1, source_target_pairs={{0,1},{1,0},{2,3},{3,2},{4,5},{5,4},{6,7},{7,6},{8,9},{9,8},{10,11... | collective-permute-start | bytes 393224 | tf_op jit(solution)/shard_map/ppermute | solution.py:55
  58.9 8.9 %collective-permute-start.17 = (f32[4,64,128]{2,1,0:T(8,128)S(1)}, f32[4,64,128]{2,1,0:T(8,128)S(1)}, u32[]{:S(2)}, u32[]{:S(2)}) collective-permute-start(f32[4,64,128]{2,1,0:T(8,128)S(1)} %get-tuple-element.70), channel_id=1, source_target_pairs={{0,3},{1,2},{2,1},{3,0},{4,7},{5,6},{6,5},{7,4},{8,11},{9,10},{10,... | collective-permute-start | bytes 393224 | tf_op jit(solution)/shard_map/ppermute | solution.py:55
  61.1 7.5 %collective-permute-start.16 = (f32[4,64,128]{2,1,0:T(8,128)S(1)}, f32[4,64,128]{2,1,0:T(8,128)S(1)}, u32[]{:S(2)}, u32[]{:S(2)}) collective-permute-start(f32[4,64,128]{2,1,0:T(8,128)S(1)} %get-tuple-element.71), channel_id=1, source_target_pairs={{0,3},{1,2},{2,1},{3,0},{4,7},{5,6},{6,5},{7,4},{8,11},{9,10},{10,... | collective-permute-start | bytes 393224 | tf_op jit(solution)/shard_map/ppermute | solution.py:55
  63.5 6.4 %collective-permute-start.19 = (f32[4,64,128]{2,1,0:T(8,128)S(1)}, f32[4,64,128]{2,1,0:T(8,128)S(1)}, u32[]{:S(2)}, u32[]{:S(2)}) collective-permute-start(f32[4,64,128]{2,1,0:T(8,128)S(1)} %get-tuple-element.72), channel_id=1, source_target_pairs={{0,1},{1,0},{2,3},{3,2},{4,5},{5,4},{6,7},{7,6},{8,9},{9,8},{10,11... | collective-permute-start | bytes 393224 | tf_op jit(solution)/shard_map/ppermute | solution.py:55

commit v5 on v4

--- a/solution.py
+++ b/solution.py
@@ -343,7 +343,7 @@
         for m in range(n_vb):
             pieces[m].append(jnp.stack([k0[m] + y0_in[m], k1[m] + x1_in[m]]))
     far = n_vb // 2
-    early = swap(pieces[far][0], "vb", far)
+    early = swap(tie(pieces[far][0], y0, x1), "vb", far)
     late = swap(pieces[far][1], "vb", far)
     pieces = [jnp.stack(piece) for piece in pieces]
     seps = [pieces[0]] + [swap(pieces[m], "vb", m) if m != far else None for m in range(1, n_vb)]

time: 70.9 us -> 70.6 us (level)
  starting transfers between devices: 27.1 us -> 24.3 us
  waiting for transfers between devices: 9.92 us -> 12.4 us
    ppermute x20, starting transfers between devices: 27.1 us -> 24.3 us  [swap(): return lax.ppermute(x, axis, [(i, i ^ mask) for i in range(n)])]
    ppermute x20, waiting for transfers between devices: 9.92 us -> 12.4 us  [swap(): return lax.ppermute(x, axis, [(i, i ^ mask) for i in range(n)])]
  transfers between devices with their start and end apart: 20 -> 20, of which waited for: 8 -> 7; matrix products, arithmetic and copies ran while one was open for 1% -> 0% of each run, Pallas kernels for 34% -> 34%
where the time goes in v5:
time: 70.6 us; the launch traced here: 70.4 us
  Pallas kernels  31.3 us (44%)
  starting transfers between devices  24.3 us (34%)
  waiting for transfers between devices  12.4 us (18%)
  other arithmetic  1.41 us (2%)
  between operations  0.96 us (1%)
    ppermute x20, starting transfers between devices, swap(): return lax.ppermute(x, axis, [(i, i ^ mask) for i in range(n)])  24.3 us
    ppermute x20, waiting for transfers between devices, swap(): return lax.ppermute(x, axis, [(i, i ^ mask) for i in range(n)])  12.4 us
    pallas_call x4, Pallas kernels, absorb(): pl.pallas_call(functools.partial(absorb_kernel, chunk, part), in_specs=[p...  9.76 us
    pallas_call x3, Pallas kernels, update(): pl.pallas_call(kernel, in_specs=[pl.BlockSpec(memory_space=pltpu.SMEM)] +...  8.55 us
    pallas_call x2, Pallas kernels, fetch(): pl.pallas_call(functools.partial(fetch_kernel, orders), in_specs=[pl.Bloc...  7.05 us
    pallas_call x1, Pallas kernels, flush(): pl.pallas_call(flush_kernel, in_specs=[pl.BlockSpec(memory_space=pltpu.SM...  5.96 us
  transfers between devices with their start and end apart: 20, of which 7 were waited for; matrix products, arithmetic and copies ran while one was open for 0% of the time, Pallas kernels for 34%

profile of v5, /device:TPU:0, one launch (start us, length us, event | category | flops | bytes accessed | tf_op | source)
XLA Modules:
  0.0 70.4 jit_solution(11907207468587782142)
XLA Ops:
  0.6 2.4 %absorb.4 = (f32[4,2,2,2,8,4096]{5,4,3,2,1,0:T(8,128)S(1)}, f32[4,2,4,2,8,512]{5,4,3,2,1,0:T(8,128)S(1)}) custom-call(s32[1]{0:T(128)} %bitcast.me_ref, s32[1]{0:T(128)} %bitcast.1.z_ref, f32[2,2,2,16,32768]{4,3,2,1,0:T(8,128)} %a_hbm.7, f32[2,2,32768]{2,1,0:T(2,128)} %m_hbm.7), custom_call_target="tpu_custom_call" | custom-call | flops 2097152 | bytes 4194304 | tf_op jit(solution)/shard_map/absorb/pallas_call | solution.py:107
  3.6 2.4 %absorb.5 = (f32[4,2,2,2,8,4096]{5,4,3,2,1,0:T(8,128)S(1)}, f32[4,2,4,2,8,512]{5,4,3,2,1,0:T(8,128)S(1)}) custom-call(s32[1]{0:T(128)} %bitcast.me_ref, s32[1]{0:T(128)} %bitcast.1.z_ref, f32[2,2,2,16,32768]{4,3,2,1,0:T(8,128)} %a_hbm.7, f32[2,2,32768]{2,1,0:T(2,128)} %m_hbm.7), custom_call_target="tpu_custom_call" | custom-call | flops 2097152 | bytes 4194304 | tf_op jit(solution)/shard_map/absorb/pallas_call | solution.py:107
  6.1 2.4 %absorb.6 = (f32[4,2,2,2,8,4096]{5,4,3,2,1,0:T(8,128)S(1)}, f32[4,2,4,2,8,512]{5,4,3,2,1,0:T(8,128)S(1)}) custom-call(s32[1]{0:T(128)} %bitcast.me_ref, s32[1]{0:T(128)} %bitcast.1.z_ref, f32[2,2,2,16,32768]{4,3,2,1,0:T(8,128)} %a_hbm.7, f32[2,2,32768]{2,1,0:T(2,128)} %m_hbm.7), custom_call_target="tpu_custom_call" | custom-call | flops 2097152 | bytes 4194304 | tf_op jit(solution)/shard_map/absorb/pallas_call | solution.py:107
  8.9 2.8 %collective-permute-start.4 = (f32[2,4,2,8,512]{4,3,2,1,0:T(8,128)S(1)}, f32[2,4,2,8,512]{4,3,2,1,0:T(8,128)S(1)}, u32[]{:S(2)}, u32[]{:S(2)}) collective-permute-start(f32[2,4,2,8,512]{4,3,2,1,0:T(8,128)S(1)} %fusion.5), channel_id=1, source_target_pairs={{0,8},{4,12},{8,0},{12,4},{16,24},{20,28},{24,16},{28,20},{1,9},{5... | collective-permute-start | bytes 786440 | tf_op jit(solution)/shard_map/ppermute | solution.py:55
  11.7 1.5 %collective-permute-start.6 = (f32[2,4,2,8,512]{4,3,2,1,0:T(8,128)S(1)}, f32[2,4,2,8,512]{4,3,2,1,0:T(8,128)S(1)}, u32[]{:S(2)}, u32[]{:S(2)}) collective-permute-start(f32[2,4,2,8,512]{4,3,2,1,0:T(8,128)S(1)} %fusion.3), channel_id=1, source_target_pairs={{0,16},{4,20},{8,24},{12,28},{16,0},{20,4},{24,8},{28,12},{1,17},{... | collective-permute-start | bytes 786440 | tf_op jit(solution)/shard_map/ppermute | solution.py:55
  13.2 2.4 %absorb.7 = (f32[4,2,2,2,8,4096]{5,4,3,2,1,0:T(8,128)S(1)}, f32[4,2,4,2,8,512]{5,4,3,2,1,0:T(8,128)S(1)}) custom-call(s32[1]{0:T(128)} %bitcast.me_ref, s32[1]{0:T(128)} %bitcast.1.z_ref, f32[2,2,2,16,32768]{4,3,2,1,0:T(8,128)} %a_hbm.7, f32[2,2,32768]{2,1,0:T(2,128)} %m_hbm.7), custom_call_target="tpu_custom_call" | custom-call | flops 2097152 | bytes 4194304 | tf_op jit(solution)/shard_map/absorb/pallas_call | solution.py:107
  15.7 4.1 %collective-permute-done.6 = f32[2,4,2,8,512]{4,3,2,1,0:T(8,128)S(1)} collective-permute-done((f32[2,4,2,8,512]{4,3,2,1,0:T(8,128)S(1)}, f32[2,4,2,8,512]{4,3,2,1,0:T(8,128)S(1)}, u32[]{:S(2)}, u32[]{:S(2)}) %collective-permute-start.6) | collective-permute-done | bytes 262176 | tf_op jit(solution)/shard_map/ppermute | solution.py:55
  19.9 1.6 %collective-permute-start.5 = (f32[4,2,8,512]{3,2,1,0:T(8,128)S(1)}, f32[4,2,8,512]{3,2,1,0:T(8,128)S(1)}, u32[]{:S(2)}, u32[]{:S(2)}) collective-permute-start(f32[4,2,8,512]{3,2,1,0:T(8,128)S(1)} %get-tuple-element.60), channel_id=1, source_target_pairs={{0,16},{4,20},{8,24},{12,28},{16,0},{20,4},{24,8},{28,12},{1,17},{... | collective-permute-start | bytes 393224 | tf_op jit(solution)/shard_map/ppermute | solution.py:55
  22.4 1.7 %collective-permute-start.7 = (f32[4,2,8,512]{3,2,1,0:T(8,128)S(1)}, f32[4,2,8,512]{3,2,1,0:T(8,128)S(1)}, u32[]{:S(2)}, u32[]{:S(2)}) collective-permute-start(f32[4,2,8,512]{3,2,1,0:T(8,128)S(1)} %get-tuple-element.67), channel_id=1, source_target_pairs={{0,8},{4,12},{8,0},{12,4},{16,24},{20,28},{24,16},{28,20},{1,9},{5... | collective-permute-start | bytes 393224 | tf_op jit(solution)/shard_map/ppermute | solution.py:55
  24.1 6.0 %flush.1 = f32[2,2,2,16,32768]{4,3,2,1,0:T(8,128)} custom-call(s32[1]{0:T(128)} %bitcast.me_ref, f32[4,2,2,2,8,4096]{5,4,3,2,1,0:T(8,128)S(1)} %get-tuple-element.39.rest_0_, f32[4,2,2,2,8,4096]{5,4,3,2,1,0:T(8,128)S(1)} %get-tuple-element.40.rest_1_, f32[4,2,2,2,8,4096]{5,4,3,2,1,0:T(8,128)S(1)} %get-tuple-element.41.rest_2_, ...), custom_call_target="tpu_custom_call" | custom-call | bytes 16777216 | tf_op jit(solution)/shard_map/flush/pallas_call | solution.py:153
  30.1 1.3 %collective-permute-done.7 = f32[4,2,8,512]{3,2,1,0:T(8,128)S(1)} collective-permute-done((f32[4,2,8,512]{3,2,1,0:T(8,128)S(1)}, f32[4,2,8,512]{3,2,1,0:T(8,128)S(1)}, u32[]{:S(2)}, u32[]{:S(2)}) %collective-permute-start.7) | collective-permute-done | bytes 131104 | tf_op jit(solution)/shard_map/ppermute | solution.py:55
  32.8 2.6 %collective-permute-start.11 = (f32[2,2,8,512]{3,2,1,0:T(8,128)S(1)}, f32[2,2,8,512]{3,2,1,0:T(8,128)S(1)}, u32[]{:S(2)}, u32[]{:S(2)}) collective-permute-start(f32[2,2,8,512]{3,2,1,0:T(8,128)S(1)} %pad_maximum_fusion.5), channel_id=1, source_target_pairs={{0,2},{1,3},{2,0},{3,1},{4,6},{5,7},{6,4},{7,5},{8,10},{9,11},{10,... | collective-permute-start | bytes 196616 | tf_op jit(solution)/shard_map/ppermute | solution.py:55
  35.4 3.5 %fetch.2 = (f32[2,4,8,128,128]{4,3,2,1,0:T(8,128)S(1)}, f32[2,4,8,128,128]{4,3,2,1,0:T(8,128)S(1)}) custom-call(s32[1]{0:T(128)} %bitcast.1.z_ref, f32[32,8,128,128]{3,2,1,0:T(8,128)} %bitcast.143), custom_call_target="tpu_custom_call" | custom-call | bytes 16777216 | tf_op jit(solution)/shard_map/fetch/pallas_call | solution.py:182
  39.9 1.6 %collective-permute-start.10 = (f32[2,2,2,8,512]{4,3,2,1,0:T(8,128)S(1)}, f32[2,2,2,8,512]{4,3,2,1,0:T(8,128)S(1)}, u32[]{:S(2)}, u32[]{:S(2)}) collective-permute-start(f32[2,2,2,8,512]{4,3,2,1,0:T(8,128)S(1)} %pad_maximum_fusion.2), channel_id=1, source_target_pairs={{0,1},{1,0},{2,3},{3,2},{4,5},{5,4},{6,7},{7,6},{8,9},{9,8},{10,11... | collective-permute-start | bytes 393224 | tf_op jit(solution)/shard_map/ppermute | solution.py:55
  41.5 2.1 %collective-permute-start.13 = (f32[2,2,2,8,512]{4,3,2,1,0:T(8,128)S(1)}, f32[2,2,2,8,512]{4,3,2,1,0:T(8,128)S(1)}, u32[]{:S(2)}, u32[]{:S(2)}) collective-permute-start(f32[2,2,2,8,512]{4,3,2,1,0:T(8,128)S(1)} %pad_maximum_fusion.4), channel_id=1, source_target_pairs={{0,3},{1,2},{2,1},{3,0},{4,7},{5,6},{6,5},{7,4},{8,11},{9,10},{10,... | collective-permute-start | bytes 393224 | tf_op jit(solution)/shard_map/ppermute | solution.py:55
  43.7 3.6 %fetch.3.held = f32[4,4,8,128,128]{4,3,2,1,0:T(8,128)S(1)} custom-call(s32[1]{0:T(128)} %bitcast.1.z_ref, f32[32,8,128,128]{3,2,1,0:T(8,128)} %bitcast.144), custom_call_target="tpu_custom_call" | custom-call | bytes 16777216 | tf_op jit(solution)/shard_map/fetch/pallas_call | solution.py:182
  48.4 2.5 %update.3 = (f32[32,8,128,128]{3,2,1,0:T(8,128)}, f32[2,4,64,128]{3,2,1,0:T(8,128)S(1)}, f32[8,128,128]{2,1,0:T(8,128)S(1)}) custom-call(s32[1]{0:T(128)} %bitcast.1.z_ref, f32[2,4,8,128,128]{4,3,2,1,0:T(8,128)S(1)} %get-tuple-element.47.held, f32[8,128,128]{2,1,0:T(8,128)S(1)} %bitcast.142, f32[2,2,2,8,512]{4,3,2,1,0:T(8,128)S(1)} %pad_maximum_fusion.1.rest_0_, ...), custom_call_target="tpu_custom_call" | custom-call | flops 2097152 | bytes 4194304 | tf_op jit(solution)/shard_map/update/pallas_call | solution.py:281
  51.0 3.2 %collective-permute-start.18 = (f32[4,64,128]{2,1,0:T(8,128)S(1)}, f32[4,64,128]{2,1,0:T(8,128)S(1)}, u32[]{:S(2)}, u32[]{:S(2)}) collective-permute-start(f32[4,64,128]{2,1,0:T(8,128)S(1)} %get-tuple-element.78), channel_id=1, source_target_pairs={{0,3},{1,2},{2,1},{3,0},{4,7},{5,6},{6,5},{7,4},{8,11},{9,10},{10,... | collective-permute-start | bytes 393224 | tf_op jit(solution)/shard_map/ppermute | solution.py:55
  54.2 3.7 %update.4 = (f32[32,8,128,128]{3,2,1,0:T(8,128)}, f32[4,4,64,128]{3,2,1,0:T(8,128)S(1)}) custom-call(s32[1]{0:T(128)} %bitcast.1.z_ref, f32[4,4,8,128,128]{4,3,2,1,0:T(8,128)S(1)} %fetch.3.held, f32[8,128,128]{2,1,0:T(8,128)S(1)} %get-tuple-element.51.scale, f32[32,8,128,128]{3,2,1,0:T(8,128)} %get-tuple-element.53.before), custom_call_target="tpu_custom_call", output_to_operand_aliasing={{0}: (3, {})} | custom-call | flops 4194304 | bytes 8388608 | tf_op jit(solution)/shard_map/update/pallas_call | solution.py:281
  58.0 1.7 %collective-permute-start.17 = (f32[4,64,128]{2,1,0:T(8,128)S(1)}, f32[4,64,128]{2,1,0:T(8,128)S(1)}, u32[]{:S(2)}, u32[]{:S(2)}) collective-permute-start(f32[4,64,128]{2,1,0:T(8,128)S(1)} %get-tuple-element.72), channel_id=1, source_target_pairs={{0,3},{1,2},{2,1},{3,0},{4,7},{5,6},{6,5},{7,4},{8,11},{9,10},{10,... | collective-permute-start | bytes 393224 | tf_op jit(solution)/shard_map/ppermute | solution.py:55
  60.9 1.6 %collective-permute-start.16 = (f32[4,64,128]{2,1,0:T(8,128)S(1)}, f32[4,64,128]{2,1,0:T(8,128)S(1)}, u32[]{:S(2)}, u32[]{:S(2)}) collective-permute-start(f32[4,64,128]{2,1,0:T(8,128)S(1)} %get-tuple-element.73), channel_id=1, source_target_pairs={{0,3},{1,2},{2,1},{3,0},{4,7},{5,6},{6,5},{7,4},{8,11},{9,10},{10,... | collective-permute-start | bytes 393224 | tf_op jit(solution)/shard_map/ppermute | solution.py:55
  62.5 2.4 %update.5 = (f32[32,8,128,128]{3,2,1,0:T(8,128)}, f32[2,4,64,128]{3,2,1,0:T(8,128)S(1)}) custom-call(s32[1]{0:T(128)} %bitcast.1.z_ref, f32[2,4,8,128,128]{4,3,2,1,0:T(8,128)S(1)} %get-tuple-element.46.held, f32[8,128,128]{2,1,0:T(8,128)S(1)} %get-tuple-element.51.scale, f32[32,8,128,128]{3,2,1,0:T(8,128)} %get-tuple-element.54.before), custom_call_target="tpu_custom_call", output_to_operand_aliasing={{0}: (3, {})} | custom-call | flops 2097152 | bytes 4194304 | tf_op jit(solution)/shard_map/update/pallas_call | solution.py:281
  64.9 2.3 %collective-permute-done.14 = f32[4,64,128]{2,1,0:T(8,128)S(1)} collective-permute-done((f32[4,64,128]{2,1,0:T(8,128)S(1)}, f32[4,64,128]{2,1,0:T(8,128)S(1)}, u32[]{:S(2)}, u32[]{:S(2)}) %collective-permute-start.14) | collective-permute-done | bytes 131104 | tf_op jit(solution)/shard_map/ppermute | solution.py:55
  68.3 1.3 %collective-permute-done.19 = f32[4,64,128]{2,1,0:T(8,128)S(1)} collective-permute-done((f32[4,64,128]{2,1,0:T(8,128)S(1)}, f32[4,64,128]{2,1,0:T(8,128)S(1)}, u32[]{:S(2)}, u32[]{:S(2)}) %collective-permute-start.19) | collective-permute-done | bytes 131104 | tf_op jit(solution)/shard_map/ppermute | solution.py:55
  (54 shorter events, 8.8 us)
Async XLA Ops:
  3.1 3.0 %collective-permute-start = (f32[4,2,4,2,8,512]{5,4,3,2,1,0:T(8,128)S(1)}, f32[4,2,4,2,8,512]{5,4,3,2,1,0:T(8,128)S(1)}, u32[]{:S(2)}, u32[]{:S(2)}) collective-permute-start(f32[4,2,4,2,8,512]{5,4,3,2,1,0:T(8,128)S(1)} %get-tuple-element.31), channel_id=1, source_target_pairs={{0,4},{4,0},{8,12},{12,8},{16,20},{20,16},{24,28},{28,24},{1,5},{5... | collective-permute-start | bytes 3145736 | tf_op jit(solution)/shard_map/ppermute | solution.py:55
  8.6 7.0 %collective-permute-start.1 = (f32[4,2,4,2,8,512]{5,4,3,2,1,0:T(8,128)S(1)}, f32[4,2,4,2,8,512]{5,4,3,2,1,0:T(8,128)S(1)}, u32[]{:S(2)}, u32[]{:S(2)}) collective-permute-start(f32[4,2,4,2,8,512]{5,4,3,2,1,0:T(8,128)S(1)} %get-tuple-element.35), channel_id=1, source_target_pairs={{0,4},{4,0},{8,12},{12,8},{16,20},{20,16},{24,28},{28,24},{1,5},{5... | collective-permute-start | bytes 3145736 | tf_op jit(solution)/shard_map/ppermute | solution.py:55
  8.9 10.9 %collective-permute-start.4 = (f32[2,4,2,8,512]{4,3,2,1,0:T(8,128)S(1)}, f32[2,4,2,8,512]{4,3,2,1,0:T(8,128)S(1)}, u32[]{:S(2)}, u32[]{:S(2)}) collective-permute-start(f32[2,4,2,8,512]{4,3,2,1,0:T(8,128)S(1)} %fusion.5), channel_id=1, source_target_pairs={{0,8},{4,12},{8,0},{12,4},{16,24},{20,28},{24,16},{28,20},{1,9},{5... | collective-permute-start | bytes 786440 | tf_op jit(solution)/shard_map/ppermute | solution.py:55
  11.7 8.1 %collective-permute-start.6 = (f32[2,4,2,8,512]{4,3,2,1,0:T(8,128)S(1)}, f32[2,4,2,8,512]{4,3,2,1,0:T(8,128)S(1)}, u32[]{:S(2)}, u32[]{:S(2)}) collective-permute-start(f32[2,4,2,8,512]{4,3,2,1,0:T(8,128)S(1)} %fusion.3), channel_id=1, source_target_pairs={{0,16},{4,20},{8,24},{12,28},{16,0},{20,4},{24,8},{28,12},{1,17},{... | collective-permute-start | bytes 786440 | tf_op jit(solution)/shard_map/ppermute | solution.py:55
  19.9 10.1 %collective-permute-start.5 = (f32[4,2,8,512]{3,2,1,0:T(8,128)S(1)}, f32[4,2,8,512]{3,2,1,0:T(8,128)S(1)}, u32[]{:S(2)}, u32[]{:S(2)}) collective-permute-start(f32[4,2,8,512]{3,2,1,0:T(8,128)S(1)} %get-tuple-element.60), channel_id=1, source_target_pairs={{0,16},{4,20},{8,24},{12,28},{16,0},{20,4},{24,8},{28,12},{1,17},{... | collective-permute-start | bytes 393224 | tf_op jit(solution)/shard_map/ppermute | solution.py:55
  21.5 9.8 %collective-permute-start.2 = (f32[2,4,2,8,512]{4,3,2,1,0:T(8,128)S(1)}, f32[2,4,2,8,512]{4,3,2,1,0:T(8,128)S(1)}, u32[]{:S(2)}, u32[]{:S(2)}) collective-permute-start(f32[2,4,2,8,512]{4,3,2,1,0:T(8,128)S(1)} %fusion.2), channel_id=1, source_target_pairs={{0,8},{4,12},{8,0},{12,4},{16,24},{20,28},{24,16},{28,20},{1,9},{5... | collective-permute-start | bytes 786440 | tf_op jit(solution)/shard_map/ppermute | solution.py:55
  22.1 9.3 %collective-permute-start.3 = (f32[2,4,2,8,512]{4,3,2,1,0:T(8,128)S(1)}, f32[2,4,2,8,512]{4,3,2,1,0:T(8,128)S(1)}, u32[]{:S(2)}, u32[]{:S(2)}) collective-permute-start(f32[2,4,2,8,512]{4,3,2,1,0:T(8,128)S(1)} %fusion.1), channel_id=1, source_target_pairs={{0,16},{4,20},{8,24},{12,28},{16,0},{20,4},{24,8},{28,12},{1,17},{... | collective-permute-start | bytes 786440 | tf_op jit(solution)/shard_map/ppermute | solution.py:55
  22.4 9.0 %collective-permute-start.7 = (f32[4,2,8,512]{3,2,1,0:T(8,128)S(1)}, f32[4,2,8,512]{3,2,1,0:T(8,128)S(1)}, u32[]{:S(2)}, u32[]{:S(2)}) collective-permute-start(f32[4,2,8,512]{3,2,1,0:T(8,128)S(1)} %get-tuple-element.67), channel_id=1, source_target_pairs={{0,8},{4,12},{8,0},{12,4},{16,24},{20,28},{24,16},{28,20},{1,9},{5... | collective-permute-start | bytes 393224 | tf_op jit(solution)/shard_map/ppermute | solution.py:55
  31.6 7.3 %collective-permute-start.8 = (f32[4,2,8,512]{3,2,1,0:T(8,128)S(1)}, f32[4,2,8,512]{3,2,1,0:T(8,128)S(1)}, u32[]{:S(2)}, u32[]{:S(2)}) collective-permute-start(f32[4,2,8,512]{3,2,1,0:T(8,128)S(1)} %get-tuple-element.64), channel_id=1, source_target_pairs={{0,16},{4,20},{8,24},{12,28},{16,0},{20,4},{24,8},{28,12},{1,17},{... | collective-permute-start | bytes 393224 | tf_op jit(solution)/shard_map/ppermute | solution.py:55
  32.1 6.8 %collective-permute-start.9 = (f32[4,2,8,512]{3,2,1,0:T(8,128)S(1)}, f32[4,2,8,512]{3,2,1,0:T(8,128)S(1)}, u32[]{:S(2)}, u32[]{:S(2)}) collective-permute-start(f32[4,2,8,512]{3,2,1,0:T(8,128)S(1)} %get-tuple-element.69), channel_id=1, source_target_pairs={{0,8},{4,12},{8,0},{12,4},{16,24},{20,28},{24,16},{28,20},{1,9},{5... | collective-permute-start | bytes 393224 | tf_op jit(solution)/shard_map/ppermute | solution.py:55
  32.8 14.4 %collective-permute-start.11 = (f32[2,2,8,512]{3,2,1,0:T(8,128)S(1)}, f32[2,2,8,512]{3,2,1,0:T(8,128)S(1)}, u32[]{:S(2)}, u32[]{:S(2)}) collective-permute-start(f32[2,2,8,512]{3,2,1,0:T(8,128)S(1)} %pad_maximum_fusion.5), channel_id=1, source_target_pairs={{0,2},{1,3},{2,0},{3,1},{4,6},{5,7},{6,4},{7,5},{8,10},{9,11},{10,... | collective-permute-start | bytes 196616 | tf_op jit(solution)/shard_map/ppermute | solution.py:55
  39.0 8.2 %collective-permute-start.12 = (f32[2,2,8,512]{3,2,1,0:T(8,128)S(1)}, f32[2,2,8,512]{3,2,1,0:T(8,128)S(1)}, u32[]{:S(2)}, u32[]{:S(2)}) collective-permute-start(f32[2,2,8,512]{3,2,1,0:T(8,128)S(1)} %pad_maximum_fusion.6), channel_id=1, source_target_pairs={{0,2},{1,3},{2,0},{3,1},{4,6},{5,7},{6,4},{7,5},{8,10},{9,11},{10,... | collective-permute-start | bytes 196616 | tf_op jit(solution)/shard_map/ppermute | solution.py:55
  39.9 7.4 %collective-permute-start.10 = (f32[2,2,2,8,512]{4,3,2,1,0:T(8,128)S(1)}, f32[2,2,2,8,512]{4,3,2,1,0:T(8,128)S(1)}, u32[]{:S(2)}, u32[]{:S(2)}) collective-permute-start(f32[2,2,2,8,512]{4,3,2,1,0:T(8,128)S(1)} %pad_maximum_fusion.2), channel_id=1, source_target_pairs={{0,1},{1,0},{2,3},{3,2},{4,5},{5,4},{6,7},{7,6},{8,9},{9,8},{10,11... | collective-permute-start | bytes 393224 | tf_op jit(solution)/shard_map/ppermute | solution.py:55
  41.5 6.8 %collective-permute-start.13 = (f32[2,2,2,8,512]{4,3,2,1,0:T(8,128)S(1)}, f32[2,2,2,8,512]{4,3,2,1,0:T(8,128)S(1)}, u32[]{:S(2)}, u32[]{:S(2)}) collective-permute-start(f32[2,2,2,8,512]{4,3,2,1,0:T(8,128)S(1)} %pad_maximum_fusion.4), channel_id=1, source_target_pairs={{0,3},{1,2},{2,1},{3,0},{4,7},{5,6},{6,5},{7,4},{8,11},{9,10},{10,... | collective-permute-start | bytes 393224 | tf_op jit(solution)/shard_map/ppermute | solution.py:55
  43.6 4.7 %copy-start = (f32[8,16,2,2,256]{4,3,2,1,0:T(2,128)S(1)}, f32[8,16,2,2,256]{4,3,2,1,0:T(2,128)}, u32[]{:S(2)}) copy-start(f32[8,16,2,2,256]{4,3,2,1,0:T(2,128)} %param.7) | copy-start | bytes 1572868
  50.9 8.8 %collective-permute-start.15 = (f32[4,64,128]{2,1,0:T(8,128)S(1)}, f32[4,64,128]{2,1,0:T(8,128)S(1)}, u32[]{:S(2)}, u32[]{:S(2)}) collective-permute-start(f32[4,64,128]{2,1,0:T(8,128)S(1)} %get-tuple-element.77), channel_id=1, source_target_pairs={{0,1},{1,0},{2,3},{3,2},{4,5},{5,4},{6,7},{7,6},{8,9},{9,8},{10,11... | collective-permute-start | bytes 393224 | tf_op jit(solution)/shard_map/ppermute | solution.py:55
  51.0 9.9 %collective-permute-start.18 = (f32[4,64,128]{2,1,0:T(8,128)S(1)}, f32[4,64,128]{2,1,0:T(8,128)S(1)}, u32[]{:S(2)}, u32[]{:S(2)}) collective-permute-start(f32[4,64,128]{2,1,0:T(8,128)S(1)} %get-tuple-element.78), channel_id=1, source_target_pairs={{0,3},{1,2},{2,1},{3,0},{4,7},{5,6},{6,5},{7,4},{8,11},{9,10},{10,... | collective-permute-start | bytes 393224 | tf_op jit(solution)/shard_map/ppermute | solution.py:55
  57.9 9.3 %collective-permute-start.14 = (f32[4,64,128]{2,1,0:T(8,128)S(1)}, f32[4,64,128]{2,1,0:T(8,128)S(1)}, u32[]{:S(2)}, u32[]{:S(2)}) collective-permute-start(f32[4,64,128]{2,1,0:T(8,128)S(1)} %get-tuple-element.71), channel_id=1, source_target_pairs={{0,1},{1,0},{2,3},{3,2},{4,5},{5,4},{6,7},{7,6},{8,9},{9,8},{10,11... | collective-permute-start | bytes 393224 | tf_op jit(solution)/shard_map/ppermute | solution.py:55
  58.0 9.2 %collective-permute-start.17 = (f32[4,64,128]{2,1,0:T(8,128)S(1)}, f32[4,64,128]{2,1,0:T(8,128)S(1)}, u32[]{:S(2)}, u32[]{:S(2)}) collective-permute-start(f32[4,64,128]{2,1,0:T(8,128)S(1)} %get-tuple-element.72), channel_id=1, source_target_pairs={{0,3},{1,2},{2,1},{3,0},{4,7},{5,6},{6,5},{7,4},{8,11},{9,10},{10,... | collective-permute-start | bytes 393224 | tf_op jit(solution)/shard_map/ppermute | solution.py:55
  60.9 7.4 %collective-permute-start.16 = (f32[4,64,128]{2,1,0:T(8,128)S(1)}, f32[4,64,128]{2,1,0:T(8,128)S(1)}, u32[]{:S(2)}, u32[]{:S(2)}) collective-permute-start(f32[4,64,128]{2,1,0:T(8,128)S(1)} %get-tuple-element.73), channel_id=1, source_target_pairs={{0,3},{1,2},{2,1},{3,0},{4,7},{5,6},{6,5},{7,4},{8,11},{9,10},{10,... | collective-permute-start | bytes 393224 | tf_op jit(solution)/shard_map/ppermute | solution.py:55
  62.5 7.2 %collective-permute-start.19 = (f32[4,64,128]{2,1,0:T(8,128)S(1)}, f32[4,64,128]{2,1,0:T(8,128)S(1)}, u32[]{:S(2)}, u32[]{:S(2)}) collective-permute-start(f32[4,64,128]{2,1,0:T(8,128)S(1)} %get-tuple-element.74), channel_id=1, source_target_pairs={{0,1},{1,0},{2,3},{3,2},{4,5},{5,4},{6,7},{7,6},{8,9},{9,8},{10,11... | collective-permute-start | bytes 393224 | tf_op jit(solution)/shard_map/ppermute | solution.py:55
